TPU v7x, 32 devices: a whole 2x2x4 slice. The times are simulated.
32 devices in a mesh: replica: 8 (over z, x), shard: 4 (over y, core).
Axes of the slice: x: 2, y: 2, z: 4, core: 2. Of those that a mesh axis runs over, the one named last changes fastest.
Arguments:
- tokens: bfloat16 [32768, 768], P(('replica', 'shard')), may hold values from -6 to 6
- segment_ids: int32 [32, 1024], P(('replica', 'shard')), may hold values from 0 to 4, as said below
- positions: int32 [32, 1024], P(('replica', 'shard')), may hold values from 0 to 799, as said below
- first_gain: bfloat16 [768], P('shard'), may hold values from 0.5 to 1.5
- first_shift: bfloat16 [768], P('shard'), may hold values from -1.25 to 1.25
- query_weight: bfloat16 [768, 768], P('shard'), may hold values from -0.21875 to 0.21875
- query_bias: bfloat16 [768], P('shard'), may hold values from -1.25 to 1.25
- shared_weight: bfloat16 [768, 128], P('shard'), may hold values from -0.21875 to 0.21875
- shared_bias: bfloat16 [128], P('shard'), may hold values from -1.25 to 1.25
- output_weight: bfloat16 [768, 768], P('shard'), may hold values from -1.5 to 1.5
- output_bias: bfloat16 [768], P('shard'), may hold values from -1.25 to 1.25
- second_gain: bfloat16 [768], P('shard'), may hold values from 0.5 to 1.5
- second_shift: bfloat16 [768], P('shard'), may hold values from -1.25 to 1.25
- up_weight: bfloat16 [768, 3072], P('shard'), may hold values from -0.21875 to 0.21875
- up_bias: bfloat16 [3072], P('shard'), may hold values from -1.25 to 1.25
- down_weight: bfloat16 [3072, 768], P('shard'), may hold values from -0.109375 to 0.109375
- down_bias: bfloat16 [768], P('shard'), may hold values from -1.25 to 1.25
- result_grad: bfloat16 [32768, 768], P(('replica', 'shard')), may hold values from -6 to 6
- shared_grad: bfloat16 [32768, 128], P(('replica', 'shard')), may hold values from -6 to 6
Outputs:
- block_output: bfloat16 [32768, 768], P(('replica', 'shard'))
- shared_cache: bfloat16 [32768, 128], P(('replica', 'shard'))
- tokens_grad: bfloat16 [32768, 768], P(('replica', 'shard'))
- grad_first_gain: float32 [768], P('shard')
- grad_first_shift: float32 [768], P('shard')
- grad_query_weight: float32 [768, 768], P('shard')
- grad_query_bias: float32 [768], P('shard')
- grad_shared_weight: float32 [768, 128], P('shard')
- grad_shared_bias: float32 [128], P('shard')
- grad_output_weight: float32 [768, 768], P('shard')
- grad_output_bias: float32 [768], P('shard')
- grad_second_gain: float32 [768], P('shard')
- grad_second_shift: float32 [768], P('shard')
- grad_up_weight: float32 [768, 3072], P('shard')
- grad_up_bias: float32 [3072], P('shard')
- grad_down_weight: float32 [3072, 768], P('shard')
- grad_down_bias: float32 [768], P('shard')
Inputs may be any that keep to these rules, and one draw needn't show every extreme that they name: `segment_ids`: ids start at 0 and rise by one at each new document of a sequence; the first document of every sequence has 800 tokens and every other document except the last has 60 to 800; in the first sequence every document after the first except the last has exactly 60. `positions`: the place of a token counted from its document's first token.
All inputs are finite; a program needn't handle non-finite values.
Results may differ from a plain program's by a relative error of at most 0.011.
Values may be sent and summed in bfloat16 or wider, within the bound.
No kernel may reach another device: no remote copies, remote signals or barrier semaphores. Data moves between devices by JAX's collectives and lax.ppermute only.
A program may use at most 256 MiB of HBM per device.

v0:
```python
import jax
import jax.numpy as jnp
from jax import lax
from jax.experimental import pallas as pl
from jax.experimental.pallas import tpu as pltpu
from jax.sharding import PartitionSpec as P


HEAD_DIM = 64
ROT = 16
FIRST_DOC = 800
EPS = 1e-05
F32 = jnp.float32
BF16 = jnp.bfloat16
WAVES = 3


def dnn(a, b):
    return lax.dot_general(a, b, (((1,), (0,)), ((), ())), preferred_element_type=F32)


def dnt(a, b):
    return lax.dot_general(a, b, (((1,), (1,)), ((), ())), preferred_element_type=F32)


def dtn(a, b):
    return lax.dot_general(a, b, (((0,), (0,)), ((), ())), preferred_element_type=F32)


def sum8(v):
    return jnp.sum(v.reshape(-1, 8, v.shape[1]), axis=0)


def normalize(x):
    centre = x - jnp.mean(x, axis=-1, keepdims=True)
    var = jnp.mean(centre * centre, axis=-1, keepdims=True)
    rstd = lax.rsqrt(var + EPS)
    return centre * rstd, rstd


ANY = pl.BlockSpec(memory_space=pl.ANY)
SMEM = pl.BlockSpec(memory_space=pltpu.SMEM)
VM = pl.BlockSpec(memory_space=pltpu.VMEM)


def shape(dims, kind):
    return jax.ShapeDtypeStruct(dims, kind)


def head_columns(w, c):
    width = w.shape[1]
    part = width // 4
    lane = lax.broadcasted_iota(jnp.int32, (1, width), 1)
    r = pltpu.roll(w, (width - c * part) % width, 1)
    return jnp.where(lane < part, r, pltpu.roll(r, width - part, 1))[:, : 2 * part]


def head_spread(x, c, width):
    part = width // 4
    lane = lax.broadcasted_iota(jnp.int32, (1, width), 1)
    v = jnp.concatenate([x, jnp.zeros_like(x)], axis=1)
    zero = jnp.zeros_like(v)
    u = jnp.where(lane < part, v, zero)
    u = u + pltpu.roll(jnp.where((lane >= part) & (lane < 2 * part), v, zero), part, 1)
    return pltpu.roll(u, c * part, 1)


def up_piece(w_ref, s, k, w, chunk):
    wid = chunk // WAVES
    t = jnp.bitwise_xor(s, k)
    a = pl.multiple_of(t * chunk + w * wid, 256)
    b = pl.multiple_of(jnp.bitwise_xor(t, 2) * chunk + w * wid, 256)
    return jnp.concatenate([w_ref[:, pl.ds(a, wid)], w_ref[:, pl.ds(b, wid)]], axis=1)


def fold(out, at, rows, v, lanes):
    h = rows // 2
    out[at : at + rows, :] = v[:, :lanes]
    out[at + rows : at + rows + h, : lanes // 2] = v[:h, lanes:]
    out[at + rows : at + rows + h, lanes // 2 :] = v[h:, lanes:]


def unfold(ref, at, rows, lanes):
    h = rows // 2
    top = ref[at : at + rows, :]
    low = ref[at + rows : at + rows + h, :]
    return jnp.concatenate(
        [top, jnp.concatenate([low[:, : lanes // 2], low[:, lanes // 2 :]], axis=0)], axis=1
    )


def pack_small(sc, seven, shared_bias, up_bias):
    part = seven[0].shape[0]
    width = up_bias.shape[0]
    few = shared_bias.shape[0]

    def kern(sc_ref, *refs):
        out, tmp = refs[-2:]
        s = sc_ref[0]
        tmp[...] = jnp.zeros_like(tmp)
        for i in range(7):
            tmp[i : i + 1, :part] = refs[i][...].astype(F32).reshape(1, part)
        tmp[:7, :] = pltpu.roll(tmp[0:8, :], s * part, 1)[:7]
        tmp[7:8, :few] = refs[7][...].astype(F32).reshape(1, few)
        tmp[7:8, :] = pltpu.roll(tmp[0:8, :], s * few, 1)[7:8]
        tmp[pl.ds(8 + s, 1), :] = refs[8][...].astype(F32).reshape(1, width)
        out[...] = tmp[...].astype(BF16)

    return pl.pallas_call(
        kern,
        in_specs=[SMEM] + [VM] * 9,
        out_specs=VM,
        out_shape=shape((16, width), BF16),
        scratch_shapes=[pltpu.VMEM((16, width), F32)],
        name="pack_small",
    )(sc, *seven, shared_bias, up_bias)


def pack_first(sc, up_weight, down_weight):
    rows, ff = up_weight.shape
    chunk, width = down_weight.shape
    wid = chunk // WAVES

    def kern(sc_ref, w_ref, d_ref, own, k1, k3, m2):
        s = sc_ref[0]
        own[...] = up_piece(w_ref, s, 0, 0, chunk)
        k1[...] = up_piece(w_ref, s, 1, 0, chunk)
        k3[...] = up_piece(w_ref, s, 3, 0, chunk)
        m2[:rows, :] = up_piece(w_ref, s, 2, 0, chunk)
        fold(m2, rows, wid, d_ref[...], 2 * wid)

    return pl.pallas_call(
        kern,
        grid=(1,),
        in_specs=[SMEM, pl.BlockSpec((rows, ff), lambda i: (0, 0)), pl.BlockSpec((wid, width), lambda i: (0, 0))],
        out_specs=[pl.BlockSpec((rows, 2 * wid), lambda i: (0, 0))] * 3
        + [pl.BlockSpec((rows + wid * 3 // 2, 2 * wid), lambda i: (0, 0))],
        out_shape=[shape((rows, 2 * wid), BF16)] * 3 + [shape((rows + wid * 3 // 2, 2 * wid), BF16)],
        name="pack_first",
    )(sc, up_weight, down_weight)


def pack_core(sc, up_weight, query_weight, shared_weight):
    rows, ff = up_weight.shape
    width = query_weight.shape[1]
    chunk = ff // 4
    wid = chunk // WAVES
    n = 2 * (WAVES - 1)
    half = width // 2

    def kern(sc_ref, w_ref, q_ref, s_ref, out):
        s = sc_ref[0]
        c = jnp.bitwise_and(s, 1)
        for w in range(1, WAVES):
            for i, k in enumerate((1, 3)):
                at = (2 * (w - 1) + i) * rows
                out[at : at + rows, :] = up_piece(w_ref, s, k, w, chunk)
        out[n * rows :, :half] = head_columns(q_ref[...].astype(F32), 1 - c).astype(BF16)
        out[n * rows :, half:] = s_ref[...]

    return pl.pallas_call(
        kern,
        in_specs=[SMEM, VM, VM, VM],
        out_specs=VM,
        out_shape=shape(((n + 1) * rows, 2 * wid), BF16),
        name="pack_core",
    )(sc, up_weight, query_weight, shared_weight)


def pack_rest(sc, up_weight, down_weight, query_weight, shared_weight, output_weight, got):
    rows, _ = up_weight.shape
    chunk, width = down_weight.shape
    wid = chunk // WAVES
    lanes = 2 * wid
    n = 2 * (WAVES - 1)
    half = width // 2

    def kern(sc_ref, w_ref, d_ref, q_ref, s_ref, o_ref, g_ref, own1, own2, ownq, y1, y2, ya):
        s = sc_ref[0]
        c = jnp.bitwise_and(s, 1)
        for w, own, out in ((1, own1, y1), (2, own2, y2)):
            own[...] = up_piece(w_ref, s, 0, w, chunk)
            out[:rows, :] = up_piece(w_ref, s, 2, w, chunk)
            at = (2 * (w - 1) + 1) * rows
            out[rows : 2 * rows, :] = g_ref[at : at + rows, :]
            fold(out, 2 * rows, wid, d_ref[w * wid : (w + 1) * wid, :], lanes)
        mine = head_columns(q_ref[...].astype(F32), c).astype(BF16)
        for out in (ownq, ya):
            out[:rows, :half] = mine
            out[:rows, half:] = s_ref[...]
        ya[rows : 2 * rows, :] = g_ref[n * rows :, :]
        fold(ya, 2 * rows, rows, o_ref[...], lanes)

    msg = 2 * rows + wid * 3 // 2
    msg_a = 2 * rows + rows * 3 // 2
    return pl.pallas_call(
        kern,
        in_specs=[SMEM] + [VM] * 6,
        out_specs=[VM] * 6,
        out_shape=[shape((rows, lanes), BF16)] * 3
        + [shape((msg, lanes), BF16)] * 2
        + [shape((msg_a, lanes), BF16)],
        name="pack_rest",
    )(sc, up_weight, down_weight, query_weight, shared_weight, output_weight, got)


def norm_pair(which, tok, dy, near, prev):
    n_tok, width = tok.shape
    n_near = len(near)
    blk = n_tok // 2
    base = 2 * which

    def kern(tok_ref, dy_ref, *refs):
        nm, nmt, na, nat, dyc, dyt, ob, vec_ref = refs[n_near + len(prev) :]
        vec_ref[...] = sum([r[...].astype(F32) for r in refs[1:n_near]], refs[0][...].astype(F32))
        xhat, _ = normalize(tok_ref[...].astype(F32))
        a = (xhat * vec_ref[0:1, :] + vec_ref[1:2, :]).astype(BF16)
        m = (xhat * vec_ref[2:3, :] + vec_ref[3:4, :]).astype(BF16)
        g = dy_ref[...]
        na[...] = a
        nm[...] = m
        dyc[...] = g
        nat[...] = a.T
        nmt[...] = m.T
        dyt[...] = g.T

        @pl.when(pl.program_id(0) == 0)
        def _():
            ob[...] = jnp.zeros_like(ob)

        ob[...] += sum8(g.astype(F32))

    row = pl.BlockSpec((blk, width), lambda i: (i + base, 0))
    col = pl.BlockSpec((width, blk), lambda i: (0, i + base))
    src = pl.BlockSpec((blk, width), lambda i: (i, 0))
    whole = pl.BlockSpec((8, width), lambda i: (0, 0))
    small = pl.BlockSpec((16, width), lambda i: (0, 0))
    res = pl.pallas_call(
        kern,
        grid=(2,),
        in_specs=[src, src] + [small] * n_near + [ANY] * len(prev),
        out_specs=[row, col, row, col, row, col, whole, small],
        out_shape=[shape((2 * n_tok, width), BF16), shape((width, 2 * n_tok), BF16)] * 3
        + [shape((8, width), F32), shape((16, width), F32)],
        input_output_aliases={2 + n_near + i: i for i in range(len(prev))},
        cost_estimate=pl.CostEstimate(
            flops=20 * n_tok * width, bytes_accessed=16 * n_tok * width, transcendentals=0
        ),
        name="norm_pair",
    )(tok, dy, *near, *prev)
    return res[:6], res[6], res[7]


def col_sums(v):
    part = v[:, :128]
    for i in range(128, v.shape[1], 128):
        part = part + v[:, i : i + 128]
    return sum8(part.T)


def mlp_wave(wave, sc, nm, nmt, dy, dyt, pieces, down_at, down_own, vec, split):
    n_tok, width = nm.shape
    blk = n_tok // 4
    rows = width // 4
    chunk = down_own.shape[0]
    wid = chunk // WAVES
    wid2 = 2 * wid
    half = width // 2
    srcs = []
    for arr, _ in list(pieces) + [down_at]:
        if not any(arr is t for t in srcs):
            srcs.append(arr)
    where = [next(i for i, t in enumerate(srcs) if t is arr) for arr, _ in list(pieces) + [down_at]]
    n_src = len(srcs)

    def kern(sc_ref, nm_r, nmt_r, dy_r, dyt_r, d0, vec_r, *refs):
        got, refs = refs[:n_src], refs[n_src:]
        hid_o, gl_o, w_s, wd_s, ub, rs = refs[:6]
        b_s, acc_u, acc_d = refs[-3:]
        grads = refs[6:-3]
        i = pl.program_id(0)
        s = sc_ref[0]
        y = jnp.right_shift(s, 1)

        @pl.when(i == 0)
        def _():
            acc_u[...] = jnp.zeros_like(acc_u)
            acc_d[...] = jnp.zeros_like(acc_d)
            ub[...] = jnp.zeros_like(ub)
            for k in range(4):
                at = pl.multiple_of(jnp.bitwise_xor(s, k) * rows, 16)
                r0 = pieces[k][1]
                w_s[pl.ds(at, rows), :] = got[where[k]][r0 : r0 + rows, :]
            wd_s[:wid, :] = d0[...]
            wd_s[wid:, :] = unfold(got[where[4]], down_at[1], wid, wid2)
            for h, t in enumerate((s, jnp.bitwise_xor(s, 2))):
                line = vec_r[pl.ds(8 + t, 1), :]
                b_s[:, h * wid : (h + 1) * wid] = jnp.broadcast_to(line[:, wave * wid : (wave + 1) * wid], (8, wid))

        up = dnn(nm_r[...], w_s[...]) + b_s[0:1, :]
        cdf = 0.5 * (1.0 + lax.erf(up * 0.7071067811865476))
        hid = (up * cdf).astype(BF16)
        slope = cdf + up * (jnp.exp(-0.5 * up * up) * 0.3989422804014327)
        gu = dnt(dy_r[...], wd_s[...]) * slope
        gl = gu.astype(BF16)
        hid_o[...] = hid
        gl_o[...] = gl
        acc_u[...] += dnn(nmt_r[...], gl)
        acc_d[...] += dnn(dyt_r[...], hid)
        ub[...] += sum8(gu)

        @pl.when(i == pl.num_programs(0) - 1)
        def _():
            mine = pl.multiple_of(y * half, 16)
            other = pl.multiple_of((1 - y) * half, 16)
            if split:
                keep_u, send_u, keep_d, send_d = grads
                d = 0
            else:
                keep_u = keep_d = grads[0]
                send_u = send_d = grads[1]
                d = half
            keep_u[:half, :] = acc_u[pl.ds(mine, half), :].astype(BF16)
            send_u[:half, :wid] = acc_u[pl.ds(other, half), wid:].astype(BF16)
            send_u[:half, wid:] = acc_u[pl.ds(other, half), :wid].astype(BF16)
            keep_d[d:, :wid] = acc_d[:half, :wid].astype(BF16)
            keep_d[d:, wid:] = acc_d[half:, :wid].astype(BF16)
            send_d[d:, :wid] = acc_d[:half, wid:].astype(BF16)
            send_d[d:, wid:] = acc_d[half:, wid:].astype(BF16)
            w = w_s[...].astype(F32)
            rs[0:8, :] = col_sums(w * acc_u[...])
            rs[8:16, :] = col_sums(w * jnp.sum(ub[...], axis=0, keepdims=True))

    row = pl.BlockSpec((blk, width), lambda i: (i, 0))
    col = pl.BlockSpec((width, blk), lambda i: (0, i))
    mid = pl.BlockSpec((blk, wid2), lambda i: (i, 0))

    def fixed(dims, at=(0, 0)):
        return pl.BlockSpec(dims, lambda i: at)

    grads = [(half, wid2)] * 4 if split else [(width, wid2)] * 2
    return pl.pallas_call(
        kern,
        grid=(4,),
        in_specs=[SMEM, row, col, row, col]
        + [fixed((wid, width), (wave, 0)), fixed((16, width))]
        + [fixed(t.shape) for t in srcs],
        out_specs=[mid, mid, fixed((width, wid2)), fixed((wid2, width)), fixed((8, wid2)), fixed((16, width))]
        + [fixed(g) for g in grads],
        out_shape=[shape((n_tok, wid2), BF16)] * 2
        + [shape((width, wid2), BF16), shape((wid2, width), BF16), shape((8, wid2), F32), shape((16, width), F32)]
        + [shape(g, BF16) for g in grads],
        scratch_shapes=[
            pltpu.VMEM((8, wid2), F32),
            pltpu.VMEM((width, wid2), F32),
            pltpu.VMEM((width, wid2), F32),
        ],
        cost_estimate=pl.CostEstimate(
            flops=8 * n_tok * width * wid2,
            bytes_accessed=10 * n_tok * width,
            transcendentals=2 * n_tok * wid2,
        ),
        name="mlp_wave",
    )(sc, nm, nmt, dy, dyt, down_own, vec, *srcs)


def attention(sc, na, dy, weights, vec, waves_of, seg_rows, cgrad):
    width = na.shape[1]
    length = cgrad.shape[0]
    rows, wq = weights[0].shape
    o_rows = weights[3].shape[0]
    core_rows = weights[1].shape[0]
    wh = wq - 2 * HEAD_DIM
    pairs = wh // 128
    chunk = 256
    n_chunk = length // chunk
    tail = length - FIRST_DOC
    blocks = []
    at = 0
    while at + chunk <= FIRST_DOC - FIRST_DOC % chunk - chunk:
        blocks.append((at, chunk, 0, at + chunk, False))
        at += chunk
    blocks.append((at, FIRST_DOC - at, 0, FIRST_DOC, False))
    blocks.append((FIRST_DOC, tail, FIRST_DOC, tail, True))

    def kern(sc_ref, na_r, dy_r, vec_r, cs_r, sr_r, cg_r, *refs):
        q0, cg_in, mg_in, o0 = refs[:4]
        o_s, gqs_s, cache, sums, wqs, wo = refs[4:10]
        q_s, do_s, dq_s, kz, zk, vz, zv, ek, ok, ev, ov, tc_r, ta_r, tb_r, sg_s = refs[10:]
        s = sc_ref[0]
        c = jnp.bitwise_and(s, 1)
        y = jnp.right_shift(s, 1)
        step = pl.program_id(0)

        @pl.when(step == 0)
        def _():
            for k in range(4):
                at = pl.multiple_of(jnp.bitwise_xor(s, k) * rows, 16)
                piece = (q0, cg_in, mg_in, mg_in)[k]
                r0 = (0, 0, 0, rows)[k]
                wqs[pl.ds(at, rows), :] = piece[r0 : r0 + rows, :]
            wo[pl.ds(pl.multiple_of(y * o_rows, 16), o_rows), :] = o0[...]
            wo[pl.ds(pl.multiple_of((1 - y) * o_rows, 16), o_rows), :] = unfold(mg_in, 2 * rows, o_rows, wq)
            sums[...] = jnp.zeros_like(sums)

        ek[...] = jnp.zeros_like(ek)
        ok[...] = jnp.zeros_like(ok)
        ev[...] = jnp.zeros_like(ev)
        ov[...] = jnp.zeros_like(ov)
        lane = lax.broadcasted_iota(jnp.int32, (1, 128), 1)
        low = lane < HEAD_DIM
        qb_line = jnp.broadcast_to(head_columns(vec_r[0:8, :], c)[6:7, :], (8, wh))
        sb_line = jnp.broadcast_to(vec_r[7:8, : 2 * HEAD_DIM], (8, 2 * HEAD_DIM))
        qb_all = jnp.concatenate([qb_line, sb_line], axis=1)[0:1, :]

        def spread(v, lo, hi):
            i = lax.broadcasted_iota(jnp.int32, (8, 128), 0)
            ln = lax.broadcasted_iota(jnp.int32, (8, 128), 1)
            ln = jnp.bitwise_and(ln, HEAD_DIM - 1)
            hit = (jnp.bitwise_and(ln, ROT // 2 - 1) == i) & (ln >= lo) & (ln < hi)
            return lax.dot_general(v, hit.astype(F32), (((0,), (0,)), ((), ())),
                                   precision=lax.Precision.HIGHEST, preferred_element_type=F32)

        still = jnp.bitwise_and(lax.broadcasted_iota(jnp.int32, (1, 128), 1), HEAD_DIM - 1) >= ROT
        cs = cs_r[0]
        tc_r[...] = spread(cs[0:8, :], 0, ROT) + jnp.where(still, 1.0, 0.0)
        ta_r[...] = spread(-cs[8:16, :], 0, ROT // 2)
        tb_r[...] = spread(cs[8:16, :], ROT // 2, ROT)
        last = jnp.broadcast_to(sr_r[0].astype(F32), (8, length))
        sg_s[...] = pltpu.roll(last, length - FIRST_DOC, 1)[:, : sg_s.shape[1]]
        seg_cols = sg_s[...].T[:tail, 0:1]

        def turn(v, c, a, b, sign):
            return v * c + sign * (pltpu.roll(v, 120, 1) * a + pltpu.roll(v, 8, 1) * b)

        def tabs(at, keys):
            c = tc_r[pl.ds(at, chunk), :]
            a = ta_r[pl.ds(at, chunk), :]
            b = tb_r[pl.ds(at, chunk), :]
            if keys:
                c = jnp.where(low, c, 1.0)
                a = jnp.where(low, a, 0.0)
                b = jnp.where(low, b, 0.0)
            return c, a, b

        @pl.loop(0, n_chunk)
        def _(n):
            at = pl.multiple_of(n * chunk, chunk)
            sl = pl.ds(at, chunk)
            lin = dnn(na_r[sl, :], wqs[...]) + qb_all
            tq = tabs(at, False)
            for p in range(pairs):
                v = turn(lin[:, p * 128 : (p + 1) * 128], *tq, 1.0)
                q_s[sl, p * 128 : (p + 1) * 128] = v.astype(BF16) * BF16(0.125)
            v = turn(lin[:, wh:], *tabs(at, True), 1.0)
            kv = v.astype(BF16)
            cache[sl, :] = kv
            vr = pltpu.roll(v, 64, 1)
            zero = jnp.zeros_like(v)
            kz[sl, :] = jnp.where(low, v, zero).astype(BF16)
            zv[sl, :] = jnp.where(low, zero, v).astype(BF16)
            zk[sl, :] = jnp.where(low, zero, vr).astype(BF16)
            vz[sl, :] = jnp.where(low, vr, zero).astype(BF16)
            do_s[sl, :] = dnt(dy_r[sl, :], wo[...]).astype(BF16)

        @pl.loop(0, pairs)
        def _(p):
            cols = pl.ds(pl.multiple_of(p * 128, 128), 128)
            for r0, rn, k0, kn, segs in blocks:
                q2 = q_s[r0 : r0 + rn, cols]
                do2 = do_s[r0 : r0 + rn, cols]
                dof = do2.astype(F32)
                keys = [ks[k0 : k0 + kn, :] for ks in (kz, zk)]
                vals = [vs[k0 : k0 + kn, :] for vs in (vz, zv)]
                free = 0 if segs else r0 // 128 * 128
                qi = lax.broadcasted_iota(jnp.int32, (rn, kn - free), 0) + r0
                ki = lax.broadcasted_iota(jnp.int32, (rn, kn - free), 1) + k0 + free
                allowed = ki <= qi
                if segs:
                    allowed = allowed & (seg_cols == sg_s[0:1, :tail])
                exps, invs = [], []
                for kk in keys:
                    logit = dnt(q2, kk)
                    edge = jnp.where(allowed, logit[:, free:], -1e30)
                    logit = jnp.concatenate([logit[:, :free], edge], axis=1) if free else edge
                    ex = jnp.exp(logit - jnp.max(logit, axis=-1, keepdims=True))
                    exps.append(ex)
                    invs.append(1.0 / jnp.sum(ex, axis=-1, keepdims=True))
                scale = jnp.where(low, invs[0], invs[1])
                dos = (dof * scale).astype(BF16)
                exb = [ex.astype(BF16) for ex in exps]
                o2 = (dnn(exb[0], vals[0]) + dnn(exb[1], vals[1])) * scale
                o_s[r0 : r0 + rn, cols] = o2.astype(BF16)
                dsb = []
                for e in range(2):
                    dp = dnt(dos, vals[e])
                    mean = jnp.sum(exps[e] * dp, axis=-1, keepdims=True) * invs[e]
                    dsb.append((exps[e] * (dp - mean)).astype(BF16))
                dq_s[r0 : r0 + rn, cols] = dnn(dsb[0], keys[0]) + dnn(dsb[1], keys[1])
                for e, (ak, av) in enumerate(((ek, ev), (ok, ov))):
                    ak[k0 : k0 + kn, :] += dtn(dsb[e], q2)
                    av[k0 : k0 + kn, :] += dtn(exb[e], dos)

        @pl.loop(0, n_chunk)
        def _(n):
            at = pl.multiple_of(n * chunk, chunk)
            sl = pl.ds(at, chunk)
            tq = tabs(at, False)
            for p in range(pairs):
                cc = slice(p * 128, (p + 1) * 128)
                v = turn(dq_s[sl, cc] * 0.125, *tq, -1.0)
                sums[:, cc] += sum8(v)
                gqs_s[sl, cc] = v.astype(BF16)
            gk = ek[sl, :] + pltpu.roll(ok[sl, :], 64, 1)
            gv = pltpu.roll(ev[sl, :], 64, 1) + ov[sl, :]
            v = jnp.where(low, gk, gv)
            v = v + jnp.where(step == 1, cg_r[sl, :].astype(F32), 0.0)
            v = turn(v, *tabs(at, True), -1.0)
            sums[:, wh:] += sum8(v)
            gqs_s[sl, wh:] = v.astype(BF16)

    def fixed(dims, at=(0, 0)):
        return pl.BlockSpec(dims, lambda i: at, pipeline_mode=pl.Buffered(1))

    def seq(lanes):
        return pl.BlockSpec((length, lanes), lambda i: (1 - i, 0))

    seg_w = (tail + 127) // 128 * 128
    total = na.shape[0]
    return pl.pallas_call(
        kern,
        grid=(2,),
        in_specs=[SMEM, seq(width), seq(width), fixed((16, width))]
        + [pl.BlockSpec((1, 16, length), lambda i: (1 - i, 0, 0)), pl.BlockSpec((1, 1, length), lambda i: (1 - i, 0, 0))]
        + [fixed((length, 128))]
        + [fixed((rows, wq)), fixed((rows, wq), (core_rows // rows - 1, 0)), fixed(weights[2].shape), fixed((o_rows, width))],
        out_specs=[seq(wh), seq(wq), fixed((length, 128)), fixed((8, wq)), fixed((width, wq)), fixed((wh, width))],
        out_shape=[
            shape((total, wh), BF16), shape((total, wq), BF16), shape((length, 128), BF16), shape((8, wq), F32),
            shape((width, wq), BF16), shape((wh, width), BF16),
        ],
        scratch_shapes=[
            pltpu.VMEM((length, wh), BF16),
            pltpu.VMEM((length, wh), BF16),
            pltpu.VMEM((length, wh), F32),
        ]
        + [pltpu.VMEM((length, 128), BF16)] * 4
        + [pltpu.VMEM((length, 128), F32)] * 7
        + [pltpu.VMEM((8, seg_w), F32)],
        cost_estimate=pl.CostEstimate(
            flops=4 * length * width * (wq + wh) + 24 * length * length * wh,
            bytes_accessed=12 * length * width,
            transcendentals=length * length * wh // 64,
        ),
        name="attention",
    )(sc, na, dy, vec, waves_of, seg_rows, cgrad, *weights)


def attn_terms(sc, nat, dyt, o_all, gqs_all, wqs, vec, sums, ob, ubs, rss):
    width, total = nat.shape
    wq = gqs_all.shape[1]
    wh = o_all.shape[1]
    blk = total // 4
    half = width // 2
    o_rows = width // 4
    n_w = len(ubs)

    def kern(sc_ref, nat_r, dyt_r, o_r, g_r, w_r, vec_r, s0, ob_r, *refs):
        ub_r, rs_r = refs[:n_w], refs[n_w : 2 * n_w]
        keep, send, acc_q, acc_o, tbl = refs[2 * n_w :]
        s = sc_ref[0]
        c = jnp.bitwise_and(s, 1)
        y = jnp.right_shift(s, 1)
        i = pl.program_id(0)
        pq = dnn(nat_r[...], g_r[...])
        po = dnn(dyt_r[...], o_r[...])

        @pl.when(i == 0)
        def _():
            acc_q[...] = pq
            acc_o[...] = po

        @pl.when(i > 0)
        def _():
            acc_q[...] += pq
            acc_o[...] += po

        @pl.when(i == pl.num_programs(0) - 1)
        def _():
            mine = pl.multiple_of(y * half, 16)
            other = pl.multiple_of((1 - y) * half, 16)
            keep[:half, :] = acc_q[pl.ds(mine, half), :].astype(BF16)
            send[:half, :] = acc_q[pl.ds(other, half), :].astype(BF16)
            got = acc_o[...].T
            lower = got[:o_rows, :].astype(BF16)
            upper = got[o_rows:, :].astype(BF16)
            fold(keep, half, o_rows, jnp.where(y == 0, lower, upper), wq)
            fold(send, half, o_rows, jnp.where(y == 0, upper, lower), wq)
            line = lambda v: jnp.sum(v, axis=0, keepdims=True)
            w = w_r[...].astype(F32)
            both = s0[...]
            fs = line(col_sums(w * line(both)))
            fg = line(col_sums(w * acc_q[...]))
            ss = sum([line(r[8:16, :]) for r in rs_r])
            sg = sum([line(r[0:8, :]) for r in rs_r])
            tbl[...] = jnp.zeros_like(tbl)
            tbl[0:1, :] = (fg - vec_r[1:2, :] * fs) / vec_r[0:1, :]
            tbl[1:2, :] = fs
            tbl[2:3, :] = (sg - vec_r[3:4, :] * ss) / vec_r[2:3, :]
            tbl[3:4, :] = ss
            tbl[4:5, :] = line(ob_r[...])
            qb8 = jnp.broadcast_to(line(both[:, :wh]), (8, wh))
            tbl[5:6, :] = head_spread(qb8, c, width)[0:1, :]
            tbl[6:7, : wq - wh] = line(both[:, wh:])
            for w_i, ref in enumerate(ub_r):
                u = line(ref[...])
                wd = wq // 2
                tbl[pl.ds(8 + s, 1), w_i * wd : (w_i + 1) * wd] = u[:, :wd]
                tbl[pl.ds(8 + jnp.bitwise_xor(s, 2), 1), w_i * wd : (w_i + 1) * wd] = u[:, wd:]
            at = half + o_rows * 3 // 2
            for out in (keep, send):
                out[at : at + 16, :] = tbl[:, :wq].astype(BF16)
                out[at + 16 : at + 32, : width - wq] = tbl[:, wq:].astype(BF16)
                out[at + 16 : at + 32, width - wq :] = jnp.zeros((16, 2 * wq - width), BF16)
                out[at + 32 :, :] = jnp.zeros((width - at - 32, wq), BF16)

    def fixed(dims):
        return pl.BlockSpec(dims, lambda i: (0, 0))

    col = pl.BlockSpec((width, blk), lambda i: (0, i))
    return pl.pallas_call(
        kern,
        grid=(4,),
        in_specs=[SMEM, col, col, pl.BlockSpec((blk, wh), lambda i: (i, 0)), pl.BlockSpec((blk, wq), lambda i: (i, 0))]
        + [fixed((width, wq)), fixed((16, width)), fixed((8, wq)), fixed((8, width))]
        + [fixed((8, wq))] * n_w
        + [fixed((16, width))] * n_w,
        out_specs=[fixed((width, wq))] * 2,
        out_shape=[shape((width, wq), BF16)] * 2,
        scratch_shapes=[pltpu.VMEM((width, wq), F32), pltpu.VMEM((width, wh), F32), pltpu.VMEM((16, width), F32)],
        cost_estimate=pl.CostEstimate(
            flops=2 * total * width * (wq + wh), bytes_accessed=4 * total * width, transcendentals=0
        ),
        name="attn_terms",
    )(sc, nat, dyt, o_all, gqs_all, wqs, vec, sums, ob, *ubs, *rss)


def outputs(which, hids, gls, ups, downs, o_all, gqs_all, wo, wqs, vec):
    total, wid2 = hids[0].shape
    width = wqs.shape[0]
    n_w = len(hids)
    blk = total // 8
    base = 4 * which

    def kern(*refs):
        h_r, g_r, u_r, d_r = (refs[k * n_w : (k + 1) * n_w] for k in range(4))
        o_r, q_r, wo_r, wq_r, vec_r, out, hp = refs[4 * n_w :]
        br = dnn(o_r[...], wo_r[...])
        ea = dnt(q_r[...], wq_r[...])
        em = None
        for w in range(n_w):
            br = br + dnn(h_r[w][...], d_r[w][...])
            t = dnt(g_r[w][...], u_r[w][...])
            em = t if em is None else em + t
        out[...] = br.astype(BF16)
        hp[...] = (ea * vec_r[0:1, :] + em * vec_r[2:3, :]).astype(BF16)

    def rows(lanes):
        return pl.BlockSpec((blk, lanes), lambda i: (i + base, 0))

    def fixed(dims):
        return pl.BlockSpec(dims, lambda i: (0, 0))

    res = pl.BlockSpec((blk, width), lambda i: (i, 0))
    return pl.pallas_call(
        kern,
        grid=(4,),
        in_specs=[rows(wid2)] * (2 * n_w)
        + [fixed((width, wid2))] * n_w
        + [fixed((wid2, width))] * n_w
        + [rows(o_all.shape[1]), rows(gqs_all.shape[1]), fixed(wo.shape), fixed(wqs.shape), fixed((16, width))],
        out_specs=[res, res],
        out_shape=[shape((total // 2, width), BF16)] * 2,
        cost_estimate=pl.CostEstimate(
            flops=total * width * (2 * n_w * wid2 + 900), bytes_accessed=12 * total * width, transcendentals=0
        ),
        name="outputs",
    )(*hids, *gls, *ups, *downs, o_all, gqs_all, wo, wqs, vec)


def finish(tok, dy, out_own, out_in, h_own, h_in, vec):
    n_tok, width = tok.shape
    blk = n_tok // 4

    def kern(tok_r, dy_r, oo, oi, ho, hi, vec_r, out, tg):
        x = tok_r[...].astype(F32)
        xhat, rstd = normalize(x)
        out[...] = (x + oo[...].astype(F32) + oi[...].astype(F32) + vec_r[4:5, :] + vec_r[5:6, :]).astype(BF16)
        h = ho[...].astype(F32) + hi[...].astype(F32)
        mean = jnp.mean(h, axis=-1, keepdims=True)
        cov = jnp.mean(h * xhat, axis=-1, keepdims=True)
        tg[...] = (dy_r[...].astype(F32) + rstd * (h - mean - xhat * cov)).astype(BF16)

    row = pl.BlockSpec((blk, width), lambda i: (i, 0))
    return pl.pallas_call(
        kern,
        grid=(4,),
        in_specs=[row] * 6 + [pl.BlockSpec((16, width), lambda i: (0, 0))],
        out_specs=[row, row],
        out_shape=[shape((n_tok, width), BF16)] * 2,
        cost_estimate=pl.CostEstimate(
            flops=20 * n_tok * width, bytes_accessed=16 * n_tok * width, transcendentals=0
        ),
        name="finish",
    )(tok, dy, out_own, out_in, h_own, h_in, vec)


def piece_row(sc_ref, n, h):
    b0, b1 = jnp.bitwise_xor(sc_ref[1], n & 1), jnp.bitwise_xor(sc_ref[2], n >> 1)
    return pl.multiple_of(b0 * (h // 2) + b1 * (h // 4), 8)


def mlp_grads(sc, pieces, width, ff):
    prow, wid2 = pieces[0][0].shape[1:]
    wid = wid2 // 2
    chunk = ff // 4
    shard_rows = width // 4
    flat = [p for ps in pieces for p in ps]
    n_p = len(pieces[0])

    def kern(sc_ref, *refs):
        up, down, tmp = refs[-3:]
        s = sc_ref[0]
        for w in range(WAVES):
            for n in range(n_p):
                ref = refs[w * n_p + n]
                at = piece_row(sc_ref, n, shard_rows)
                for p in range(4):
                    for h in range(2):
                        v = ref[p, :, h * wid : (h + 1) * wid].astype(F32)
                        if p < 2:
                            t = jnp.bitwise_xor(s, p + 2 * h)
                            lanes = pl.multiple_of(t * chunk + w * wid, 256)
                            up[pl.ds(at, prow), pl.ds(lanes, wid)] = v
                        else:
                            tmp[pl.ds((2 * h + p - 2) * shard_rows + at, prow), :] = v
            down[w * wid : (w + 1) * wid, :] = tmp[...].T

    return pl.pallas_call(
        kern,
        in_specs=[SMEM] + [VM] * len(flat),
        out_specs=[VM, VM],
        out_shape=[shape((shard_rows, ff), F32), shape((chunk, width), F32)],
        scratch_shapes=[pltpu.VMEM((width, wid), F32)],
        cost_estimate=pl.CostEstimate(flops=0, bytes_accessed=12 * shard_rows * ff, transcendentals=0),
        name="mlp_grads",
    )(sc, *flat)


def attn_grads(sc, pieces, width, shared_w):
    n_p = len(pieces)
    _, prow, wq = pieces[0].shape
    part = width // 4
    wh = wq - shared_w

    def kern(sc_ref, *refs):
        full = refs[-1]
        ins = refs[:n_p]
        gq, gs, go = refs[n_p : n_p + 3]
        lines = refs[n_p + 3 : -1]
        s = sc_ref[0]
        c = jnp.bitwise_and(s, 1)
        for n in range(n_p):
            at = piece_row(sc_ref, n, part // 2)
            for p in range(8):
                full[pl.ds(p * (part // 2) + at, prow), :] = ins[n][p].astype(F32)
        gq[...] = head_spread(full[:part, :wh], c, width) + head_spread(full[part : 2 * part, :wh], 1 - c, width)
        gs[...] = full[:part, wh:]
        go[...] = unfold(full, 2 * part, part, wq)
        at = 2 * part + part * 3 // 2
        tab = jnp.concatenate([full[at : at + 16, :], full[at + 16 : at + 32, : width - wq]], axis=1)
        left = pltpu.roll(tab, (width - s * part) % width, 1)
        for out, i in zip(lines, (0, 1, 2, 3, 4, 5)):
            out[...] = left[i : i + 1, :part]
        few = shared_w // 4
        lines[6][...] = pltpu.roll(tab, (width - s * few) % width, 1)[6:7, :few]
        full[0:16, :] = tab[:, :wq]
        full[16:32, : width - wq] = tab[:, wq:]
        lines[7][:, :wq] = full[pl.ds(8 + s, 1), :]
        lines[7][:, wq:] = full[pl.ds(24 + s, 1), : width - wq]

    return pl.pallas_call(
        kern,
        in_specs=[SMEM] + [VM] * n_p,
        out_specs=[VM] * 11,
        out_shape=[shape((part, width), F32), shape((part, shared_w), F32), shape((part, width), F32)]
        + [shape((1, part), F32)] * 6
        + [shape((1, shared_w // 4), F32), shape((1, width), F32)],
        scratch_shapes=[pltpu.VMEM((width, wq), F32)],
        name="attn_grads",
    )(sc, *pieces)


def to_shard(value, k):
    return lax.ppermute(value, "shard", [(s, s ^ k) for s in range(4)])


def to_replica(value, k, count):
    return lax.ppermute(value, "replica", [(r, r ^ k) for r in range(count)])


def both_add(a, b):
    return (a.astype(F32) + b.astype(F32)).astype(BF16)


def after(value, *others):
    return lax.optimization_barrier((value,) + others)[0]


def send_y(value):
    return to_shard(value, 2)


def reduce_chain(keep, got, count, rank, mix, join):
    def halve(mine, other, k):
        h = mine.shape[1] // 2
        b = (rank // k) & 1

        def cut(which):
            f = lambda v: lax.dynamic_slice_in_dim(v, which * h, h, axis=1)
            return both_add(f(mine), f(other))

        half, away = cut(b), cut(1 - b)
        return half, to_replica(away, k, count)

    half, got = halve(keep, got, 1)
    half, got = halve(half, got, 2)
    half = both_add(half, got)
    k = 4
    while k < count:
        half = both_add(half, to_replica(half, k, count))
        k *= 2
    sent, kept = mix(half)
    half = join(kept, to_shard(sent, 1))
    return [half] + [to_replica(half, k, count) for k in (1, 2, 3)]


def shards(
    tokens, segment_ids, positions, first_gain, first_shift, query_weight, query_bias, shared_weight,
    shared_bias, output_weight, output_bias, second_gain, second_shift, up_weight, up_bias, down_weight,
    down_bias, result_grad, shared_grad, *, replicas,
):
    width = tokens.shape[1]
    ff = up_weight.shape[1]
    part = width // 4
    sw = shared_weight.shape[1]
    s = lax.axis_index("shard")
    r = lax.axis_index("replica")
    c = s & 1
    sc = jnp.stack([s, r & 1, (r >> 1) & 1]).astype(jnp.int32)

    small = pack_small(
        sc,
        [first_gain, first_shift, second_gain, second_shift, output_bias, down_bias, query_bias],
        shared_bias, up_bias,
    )
    near = [small] + [to_shard(small, k) for k in (1, 2, 3)]
    own0, k1, k3, m2 = pack_first(sc, after(up_weight, small), down_weight)
    k1 = to_shard(k1, 1)
    m2 = to_shard(m2, 2)
    k3 = to_shard(k3, 3)
    core_out = pack_core(sc, after(up_weight, own0), query_weight, shared_weight)
    core_got = to_shard(core_out, 1)
    tok_in = to_shard(tokens, 1)
    dy_in = to_shard(result_grad, 1)
    ints_in = to_shard(jnp.concatenate([segment_ids, positions], axis=0), 1)

    prev, ob, vec = norm_pair(0, tokens, result_grad, near, [])
    prev, _, _ = norm_pair(1, tok_in, dy_in, near, prev)
    nm, nmt, na, nat, dy, dyt = prev
    own1, own2, ownq, y1, y2, ya = pack_rest(
        sc, up_weight, down_weight, query_weight, shared_weight, output_weight, after(core_got, vec)
    )

    pos = jnp.concatenate([positions, ints_in[1:]], axis=0)
    inv = 10000.0 ** (-2.0 * jnp.arange(ROT // 2, dtype=F32) / ROT)
    ang = pos.astype(F32)[:, None, :] * inv[None, :, None]
    angles = jnp.concatenate([jnp.cos(ang), jnp.sin(ang)], axis=1)
    segs = jnp.stack([segment_ids, ints_in[:1]])

    rows = part

    def mix_mlp(v):
        mine = jnp.where(c == 0, v[0], v[1])
        theirs = jnp.where(c == 0, v[1], v[0])
        return theirs, (mine, v[2:])

    def join_mlp(kept, got):
        return jnp.concatenate([kept[0][None], got[None], kept[1]], axis=0)

    wh = width // 2

    def mix_attn(v):
        mine = jnp.where(c == 0, v[:2], v[2:4])
        theirs = jnp.where(c == 0, v[2:4], v[:2])
        return jnp.concatenate([theirs, v[7:]], axis=0), (mine, v[4:7], v[7:])

    def join_attn(kept, got):
        mine, outs_rows, table = kept
        front = jnp.concatenate([mine[:, :, :wh], both_add(mine[:, :, wh:], got[:2, :, wh:])], axis=2)
        return jnp.concatenate([front, got[:2], outs_rows, both_add(table, got[2:])], axis=0)

    def wave(w, pieces, down_at, split):
        return mlp_wave(w, sc, nm, nmt, dy, dyt, pieces, down_at, down_weight, vec, split)

    m1 = to_shard(y1, 2)
    hid0, gl0, wu0, wd0, ub0, rs0, keep0, send0 = wave(0, [(own0, 0), (k1, 0), (m2, 0), (k3, 0)], (m2, rows), False)
    ma = to_shard(after(ya, m1), 2)
    hid1, gl1, wu1, wd1, ub1, rs1, keep1, send1 = wave(
        1, [(own1, 0), (core_got, 0), (m1, 0), (m1, rows)], (m1, 2 * rows), False
    )
    m2b = to_shard(after(y2, ma), 2)
    got0 = send_y(after(send0, ma))
    got1 = send_y(after(send1, ma))
    o_all, gqs_all, cache, sums, wqs, wo = attention(
        sc, na, dy, (ownq, core_got, ma, output_weight), vec, angles, segs, shared_grad
    )
    hid2, gl2, wu2, wd2, ub2, rs2, keep2, send2 = wave(
        2, [(own2, 0), (core_got, 2 * rows), (m2b, 0), (m2b, rows)], (m2b, 2 * rows), False
    )
    keepa, senda = attn_terms(
        sc, nat, dyt, o_all, gqs_all, wqs, vec, sums, ob, (ub0, ub1, ub2), (rs0, rs1, rs2)
    )

    def chain(keep, got, planes, mix, join):
        lanes = keep.shape[1]
        return reduce_chain(keep.reshape(planes, -1, lanes), got.reshape(planes, -1, lanes), replicas, r, mix, join)

    p0 = chain(keep0, got0, 4, mix_mlp, join_mlp)
    p1 = chain(keep1, got1, 4, mix_mlp, join_mlp)
    p2 = chain(keep2, send_y(send2), 4, mix_mlp, join_mlp)
    pa = chain(keepa, send_y(senda), 8, mix_attn, join_attn)

    hids, gls, wus, wds = (hid0, hid1, hid2), (gl0, gl1, gl2), (wu0, wu1, wu2), (wd0, wd1, wd2)

    def outs(which):
        return outputs(which, hids, gls, wus, wds, o_all, gqs_all, wo, wqs, vec)

    out_p, h_p = outs(1)
    out_in = to_shard(out_p, 1)
    h_in = to_shard(h_p, 1)
    out_o, h_o = outs(0)
    block_output, tokens_grad = finish(tokens, result_grad, out_o, out_in, h_o, h_in, vec)

    grad_up, grad_down = mlp_grads(sc, [p0, p1, p2], width, ff)
    out = attn_grads(sc, pa, width, sw)
    grad_q, grad_s, grad_o = out[:3]
    fg, fs, sg, ss, ob_g, qb_g, sb_g, ub_g = [v.reshape(-1) for v in out[3:]]
    return (
        block_output, cache, tokens_grad,
        fg, fs, grad_q, qb_g, grad_s, sb_g, grad_o, ob_g,
        sg, ss, grad_up, ub_g, grad_down, ob_g,
    )


def solution(mesh):
    both = P(("replica", "shard"), None)
    one, two = P("shard"), P("shard", None)

    def body(*args):
        return shards(*args, replicas=mesh.shape["replica"])

    return jax.shard_map(
        body,
        mesh=mesh,
        in_specs=(both, both, both, one, one, two, one, two, one, two, one, one, one, two, one, two, one, both, both),
        out_specs=(both, both, both, one, one, two, one, two, one, two, one, one, one, two, one, two, one),
        check_vma=False,
    )
```

profile of v0, /device:TPU:0, one launch (start us, length us, event | category | flops | bytes accessed | tf_op | source)
XLA Modules:
  0.0 309.9 jit_solution(6547505775693132061)
XLA Ops:
  1.8 1.6 pack_small.1.refs_0_
  3.4 2.6 pack_first.1
  6.0 2.6 pack_core.1
  9.2 2.9 collective-permute-start.3
  12.2 1.6 collective-permute-done.2.refs_1_
  13.8 2.6 collective-permute-start.4
  16.6 1.4 collective-permute-done.4.refs_3_
  18.5 6.3 %norm_pair.2 = (bf16[2048,768]{1,0:T(8,128)(2,1)}, bf16[768,2048]{1,0:T(8,128)(2,1)}, bf16[2048,768]{1,0:T(8,128)(2,1)}, bf16[768,2048]{1,0:T(8,128)(2,1)}, bf16...) custom-call(bf16[1024,768]{1,0:T(8,128)(2,1)} %tok_r.1, ...), custom_call_target="tpu_custom_call" | custom-call | flops 15728640 | bytes 12582912 | tf_op jit(solution)/shard_map/norm_pair/pallas_call | solution.py:238
  24.8 1.8 collective-permute-start.6
  26.6 3.9 %pack_rest.1 = (bf16[192,512]{1,0:T(8,128)(2,1)}, bf16[192,512]{1,0:T(8,128)(2,1)}, bf16[192,512]{1,0:T(8,128)(2,1)}, bf16[768,512]{1,0:T(8,128)(2,1)}, bf16[768...) custom-call(s32[3]{0:T(128)} %pad_add_fusion.2.sc_ref, bf16[192,3072]{1,0:T(8,128)(2,1)} %w_ref.3, bf16[768,768]{1,0:T(8,128)(2,1)} %d0.5, ...), custom_call_target="tpu_custom_call" | custom-call | tf_op jit(solution)/shard_map/pack_rest/pallas_call | solution.py:196
  31.2 1.2 collective-permute-start.7
  33.7 6.3 %norm_pair.3 = (bf16[2048,768]{1,0:T(8,128)(2,1)}, bf16[768,2048]{1,0:T(8,128)(2,1)}, bf16[2048,768]{1,0:T(8,128)(2,1)}, bf16[768,2048]{1,0:T(8,128)(2,1)}, bf16...) custom-call(bf16[1024,768]{1,0:T(8,128)(2,1)} %copy-done.3, ...), custom_call_target="tpu_custom_call", output_to_operand_aliasing={{0}: (6, {}), {1}: (7, {}), {2}: (8, {}), {3}: (9, {}), {4}... | custom-call | flops 15728640 | bytes 12582912 | tf_op jit(solution)/shard_map/norm_pair/pallas_call | solution.py:238
  40.0 18.3 %collective-permute-done.9.refs_2_ = bf16[768,512]{1,0:T(8,128)(2,1)} collective-permute-done((bf16[768,512]{1,0:T(8,128)(2,1)}, bf16[768,512]{1,0:T(8,128)(2,1)}, u32[]{:S(2)}, u32[]{:S(2)}) %collective-permute-start.9) | collective-permute-done | bytes 786464 | tf_op jit(solution)/shard_map/ppermute | solution.py:805
  58.3 1.8 collective-permute-start.10
  60.0 1.6 collective-permute-done.7.refs_3_
  61.6 13.7 %mlp_wave.3 = (bf16[2048,512]{1,0:T(8,128)(2,1)}, bf16[2048,512]{1,0:T(8,128)(2,1)}, bf16[768,512]{1,0:T(8,128)(2,1)}, bf16[512,768]{1,0:T(8,128)(2,1)}, f32[8,5...) custom-call(s32[3]{0:T(128)} %pad_add_fusion.2.sc_ref, ...), custom_call_target="tpu_custom_call" | custom-call | flops 6442450944 | bytes 15728640 | tf_op jit(solution)/shard_map/mlp_wave/pallas_call | solution.py:342
  75.3 14.0 %mlp_wave.4 = (bf16[2048,512]{1,0:T(8,128)(2,1)}, bf16[2048,512]{1,0:T(8,128)(2,1)}, bf16[768,512]{1,0:T(8,128)(2,1)}, bf16[512,768]{1,0:T(8,128)(2,1)}, f32[8,5...) custom-call(s32[3]{0:T(128)} %pad_add_fusion.2.sc_ref, ...), custom_call_target="tpu_custom_call" | custom-call | flops 6442450944 | bytes 15728640 | tf_op jit(solution)/shard_map/mlp_wave/pallas_call | solution.py:342
  89.3 1.5 collective-permute-start.11
  91.4 1.4 collective-permute-start.31
  92.8 49.8 %attention.1 = (bf16[2048,384]{1,0:T(8,128)(2,1)}, bf16[2048,512]{1,0:T(8,128)(2,1)}, bf16[1024,128]{1,0:T(8,128)(2,1)}, f32[8,512]{1,0:T(8,128)}, bf16[768,512]{1,0:T(8,128)(2,1)}, /*index=5*/bf16[384,768]{1,0:T(8,128)(2,1)}) custom-call(s32[3]{0:T(128)} %pad_add_fusion.2.sc_ref, bf16[2048,768]{1,0:T(8,128)(2,1)} %get-tuple-element.136.na_r, ...), custom_call_target="tpu_custom_call" | custom-call | flops 12482248704 | bytes 9437184 | tf_op jit(solution)/shard_map/attention/pallas_call | solution.py:530
  142.9 1.6 collective-permute-start.24
  144.5 14.0 %mlp_wave.5 = (bf16[2048,512]{1,0:T(8,128)(2,1)}, bf16[2048,512]{1,0:T(8,128)(2,1)}, bf16[768,512]{1,0:T(8,128)(2,1)}, bf16[512,768]{1,0:T(8,128)(2,1)}, f32[8,5...) custom-call(s32[3]{0:T(128)} %pad_add_fusion.2.sc_ref, ...), custom_call_target="tpu_custom_call" | custom-call | flops 6442450944 | bytes 15728640 | tf_op jit(solution)/shard_map/mlp_wave/pallas_call | solution.py:342
  158.4 9.7 %attn_terms.1 = (bf16[768,512]{1,0:T(8,128)(2,1)}, bf16[768,512]{1,0:T(8,128)(2,1)}) custom-call(s32[3]{0:T(128)} %pad_add_fusion.2.sc_ref, bf16[768,2048]{1,0:T(8,128)(2,1)} %get-tuple-element.149.nat_r, bf16[768,2048]{1,0:T(8,128)(2,1)} %get-tuple-element.108.dyt_r, bf16[2048,384]{1,0:T(8,128)(2,1)} %get-tuple-element.138.refs_12_.o_r, ...), custom_call_target="tpu_custom_call" | custom-call | flops 2818572288 | bytes 6291456 | tf_op jit(solution)/shard_map/attn_terms/pallas_call | solution.py:631
  168.9 1.0 add_convert_fusion.3
  170.4 1.4 collective-permute-start.39
  171.8 0.8 add_convert_fusion.18
  172.6 1.6 collective-permute-start.25
  174.2 11.9 %outputs.3 = (bf16[1024,768]{1,0:T(8,128)(2,1)}, bf16[1024,768]{1,0:T(8,128)(2,1)}) custom-call(bf16[2048,512]{1,0:T(8,128)(2,1)} %get-tuple-element.115.refs_0_, bf16[2048,512]{1,0:T(8,128)(2,1)} %get-tuple-element.120.refs_1_, bf16[2048,512]{1,0:T(8,128)(2,1)} %get-tuple-element.126.refs_2_, bf16[2048,512]{1,0:T(8,128)(2,1)} %get-tuple-element.127.refs_3_, ...), custom_call_target="tpu_custom_call" | custom-call | flops 6247415808 | bytes 18874368 | tf_op jit(solution)/shard_map/outputs/pallas_call | solution.py:675
  186.2 0.7 copy-done.12
  187.5 1.1 add_convert_fusion.14
  189.1 1.1 add_convert_fusion.17
  190.2 5.3 %collective-permute-done.33 = bf16[4,48,512]{2,1,0:T(8,128)(2,1)S(1)} collective-permute-done((bf16[4,48,512]{2,1,0:T(8,128)(2,1)S(1)}, bf16[4,48,512]{2,1,0:T(8,128)(2,1)S(1)}, u32[]{:S(2)}, u32[]{:S(2)}) %collective-permute-start.33) | collective-permute-done | bytes 196640 | tf_op jit(solution)/shard_map/ppermute | solution.py:809
  195.5 2.6 collective-permute-start.26
  198.1 1.1 add_convert_fusion.13
  199.6 1.3 add_convert_fusion.7
  200.9 3.8 %collective-permute-done.39 = bf16[768,512]{1,0:T(8,128)(2,1)} collective-permute-done((bf16[768,512]{1,0:T(8,128)(2,1)}, bf16[768,512]{1,0:T(8,128)(2,1)}, u32[]{:S(2)}, u32[]{:S(2)}) %collective-permute-start.39) | collective-permute-done | bytes 786464 | tf_op jit(solution)/shard_map/ppermute | solution.py:805
  205.3 1.3 add_convert_fusion.1
  206.6 4.2 %collective-permute-done.26 = bf16[4,48,512]{2,1,0:T(8,128)(2,1)S(1)} collective-permute-done((bf16[4,48,512]{2,1,0:T(8,128)(2,1)S(1)}, bf16[4,48,512]{2,1,0:T(8,128)(2,1)S(1)}, u32[]{:S(2)}, u32[]{:S(2)}) %collective-permute-start.26) | collective-permute-done | bytes 196640 | tf_op jit(solution)/shard_map/ppermute | solution.py:809
  210.8 1.5 collective-permute-start.40
  212.4 2.5 collective-permute-done.34
  215.1 1.1 collective-permute-done.27
  216.4 1.6 collective-permute-start.28
  218.0 0.9 collective-permute-start.17
  219.0 5.6 %collective-permute-done.40 = bf16[4,96,512]{2,1,0:T(8,128)(2,1)S(1)} collective-permute-done((bf16[4,96,512]{2,1,0:T(8,128)(2,1)S(1)}, bf16[4,96,512]{2,1,0:T(8,128)(2,1)S(1)}, u32[]{:S(2)}, u32[]{:S(2)}) %collective-permute-start.40) | collective-permute-done | bytes 393248 | tf_op jit(solution)/shard_map/ppermute | solution.py:809
  224.6 2.1 collective-permute-start.29
  226.9 6.4 %collective-permute-done.41 = bf16[4,48,512]{2,1,0:T(8,128)(2,1)S(1)} collective-permute-done((bf16[4,48,512]{2,1,0:T(8,128)(2,1)S(1)}, bf16[4,48,512]{2,1,0:T(8,128)(2,1)S(1)}, u32[]{:S(2)}, u32[]{:S(2)}) %collective-permute-start.41) | collective-permute-done | bytes 196640 | tf_op jit(solution)/shard_map/ppermute | solution.py:809
  233.4 4.2 %collective-permute-start.18 = (bf16[8,24,512]{2,1,0:T(8,128)(2,1)S(1)}, bf16[8,24,512]{2,1,0:T(8,128)(2,1)S(1)}, u32[]{:S(2)}, u32[]{:S(2)}) collective-permute-start(bf16[8,24,512]{2,1,0:T(8,128)(2,1)S(1)} %add_convert_fusion.21), channel_id=1, source_target_pairs={{0,16},{4,20},{8,24},{12,28},{16,0},{20,4},{24,8},{28,12},{1,17},{... | collective-permute-start | bytes 589832 | tf_op jit(solution)/shard_map/ppermute | solution.py:809
  237.7 9.3 %collective-permute-done.18 = bf16[8,24,512]{2,1,0:T(8,128)(2,1)S(1)} collective-permute-done((bf16[8,24,512]{2,1,0:T(8,128)(2,1)S(1)}, bf16[8,24,512]{2,1,0:T(8,128)(2,1)S(1)}, u32[]{:S(2)}, u32[]{:S(2)}) %collective-permute-start.18) | collective-permute-done | bytes 196640 | tf_op jit(solution)/shard_map/ppermute | solution.py:809
  247.0 8.6 %collective-permute-done.42 = bf16[4,48,512]{2,1,0:T(8,128)(2,1)S(1)} collective-permute-done((bf16[4,48,512]{2,1,0:T(8,128)(2,1)S(1)}, bf16[4,48,512]{2,1,0:T(8,128)(2,1)S(1)}, u32[]{:S(2)}, u32[]{:S(2)}) %collective-permute-start.42) | collective-permute-done | bytes 196640 | tf_op jit(solution)/shard_map/ppermute | solution.py:809
  255.9 1.1 collective-permute-done.43
  257.2 0.7 pad_maximum_fusion.3.refs_8_
  258.5 3.1 collective-permute-start.37
  261.5 5.1 %collective-permute-done.30.refs_3_ = bf16[4,48,512]{2,1,0:T(8,128)(2,1)S(1)} collective-permute-done((bf16[4,48,512]{2,1,0:T(8,128)(2,1)S(1)}, bf16[4,48,512]{2,1,0:T(8,128)(2,1)S(1)}, u32[]{:S(2)}, u32[]{:S(2)}) %collective-permute-start.30) | collective-permute-done | bytes 196640 | tf_op jit(solution)/shard_map/ppermute | solution.py:809
  266.7 2.8 collective-permute-done.36.refs_5_
  269.9 1.6 collective-permute-start.45
  271.5 3.9 %collective-permute-done.38.refs_7_ = bf16[4,48,512]{2,1,0:T(8,128)(2,1)S(1)} collective-permute-done((bf16[4,48,512]{2,1,0:T(8,128)(2,1)S(1)}, bf16[4,48,512]{2,1,0:T(8,128)(2,1)S(1)}, u32[]{:S(2)}, u32[]{:S(2)}) %collective-permute-start.38) | collective-permute-done | bytes 196640 | tf_op jit(solution)/shard_map/ppermute | solution.py:809
  275.5 3.4 %collective-permute-start.21 = (bf16[8,24,512]{2,1,0:T(8,128)(2,1)S(1)}, bf16[8,24,512]{2,1,0:T(8,128)(2,1)}, u32[]{:S(2)}, u32[]{:S(2)}) collective-permute-start(bf16[8,24,512]{2,1,0:T(8,128)(2,1)S(1)} %pad_maximum_fusion.refs_0_), channel_id=1, source_target_pairs={{0,8},{4,12},{8,0},{12,4},{16,24},{20,28},{24,16},{28,20},{1,9},{5... | collective-permute-start | bytes 589832 | tf_op jit(solution)/shard_map/ppermute | solution.py:809
  278.9 0.8 collective-permute-done.44.refs_9_
  280.8 11.9 %outputs.2 = (bf16[1024,768]{1,0:T(8,128)(2,1)}, bf16[1024,768]{1,0:T(8,128)(2,1)}) custom-call(bf16[2048,512]{1,0:T(8,128)(2,1)} %get-tuple-element.115.refs_0_, bf16[2048,512]{1,0:T(8,128)(2,1)} %get-tuple-element.120.refs_1_, bf16[2048,512]{1,0:T(8,128)(2,1)} %get-tuple-element.126.refs_2_, bf16[2048,512]{1,0:T(8,128)(2,1)} %get-tuple-element.127.refs_3_, ...), custom_call_target="tpu_custom_call" | custom-call | flops 6247415808 | bytes 18874368 | tf_op jit(solution)/shard_map/outputs/pallas_call | solution.py:675
  292.8 6.7 %finish.1 = (bf16[1024,768]{1,0:T(8,128)(2,1)}, bf16[1024,768]{1,0:T(8,128)(2,1)}) custom-call(bf16[1024,768]{1,0:T(8,128)(2,1)} %tok_r.1, bf16[1024,768]{1,0:T(8,128)(2,1)} %dy_r.1, bf16[1024,768]{1,0:T(8,128)(2,1)} %get-tuple-element.142.oo, bf16[1024,768]{1,0:T(8,128)(2,1)} %copy-done.1, bf16[1024,768]{1,0:T(8,128)(2,1)} %get-tuple-element.144.ho, ...), custom_call_target="tpu_custom_call" | custom-call | flops 15728640 | bytes 12582912 | tf_op jit(solution)/shard_map/finish/pallas_call | solution.py:705
  299.6 4.7 %mlp_grads.1 = (f32[192,3072]{1,0:T(8,128)}, f32[768,768]{1,0:T(8,128)}) custom-call(s32[3]{0:T(128)} %pad_add_fusion.2.sc_ref, bf16[4,48,512]{2,1,0:T(8,128)(2,1)} %copy-done.4, bf16[4,48,512]{2,1,0:T(8,128)(2,1)} %copy-done.14, bf16[4,48,512]{2,1,0:T(8,128)(2,1)} %copy-done.15, bf16[4,48,512]{2,1,0:T(8,128)(2,1)} %copy-done.16, ...), custom_call_target="tpu_custom_call" | custom-call | bytes 7077888 | tf_op jit(solution)/shard_map/mlp_grads/pallas_call | solution.py:749
  304.3 3.0 attn_grads.1
  307.3 1.3 reduce
  308.6 1.2 copy.49
  (150 shorter events, 11.9 us)
Async XLA Ops:
  0.7 30.6 %collective-permute-start = (bf16[1024,768]{1,0:T(8,128)(2,1)}, bf16[1024,768]{1,0:T(8,128)(2,1)S(1)}, u32[]{:S(2)}, u32[]{:S(2)}) collective-permute-start(bf16[1024,768]{1,0:T(8,128)(2,1)} %tok_r.1), channel_id=1, source_target_pairs={{0,1},{1,0},{2,3},{3,2},{4,5},{5,4},{6,7},{7,6},{8,9},{9,8},{10,11... | collective-permute-start | bytes 4718600 | tf_op jit(solution)/shard_map/ppermute | solution.py:805
  8.6 16.2 %collective-permute-start.8 = (bf16[960,512]{1,0:T(8,128)(2,1)}, bf16[960,512]{1,0:T(8,128)(2,1)}, u32[]{:S(2)}, u32[]{:S(2)}) collective-permute-start(bf16[960,512]{1,0:T(8,128)(2,1)} %pack_core.1), channel_id=1, source_target_pairs={{0,1},{1,0},{2,3},{3,2},{4,5},{5,4},{6,7},{7,6},{8,9},{9,8},{10,11... | collective-permute-start | bytes 2949128 | tf_op jit(solution)/shard_map/ppermute | solution.py:805
  8.7 25.1 %collective-permute-start.1 = (bf16[1024,768]{1,0:T(8,128)(2,1)S(1)}, bf16[1024,768]{1,0:T(8,128)(2,1)}, u32[]{:S(2)}, u32[]{:S(2)}) collective-permute-start(bf16[1024,768]{1,0:T(8,128)(2,1)S(1)} %copy-done), channel_id=1, source_target_pairs={{0,1},{1,0},{2,3},{3,2},{4,5},{5,4},{6,7},{7,6},{8,9},{9,8},{10,11... | collective-permute-start | bytes 4718600 | tf_op jit(solution)/shard_map/ppermute | solution.py:805
  9.1 4.6 %collective-permute-start.2 = (bf16[16,768]{1,0:T(8,128)(2,1)S(1)}, bf16[16,768]{1,0:T(8,128)(2,1)S(1)}, u32[]{:S(2)}, u32[]{:S(2)}) collective-permute-start(bf16[16,768]{1,0:T(8,128)(2,1)S(1)} %copy-done.13), channel_id=1, source_target_pairs={{0,1},{1,0},{2,3},{3,2},{4,5},{5,4},{6,7},{7,6},{8,9},{9,8},{10,11... | collective-permute-start | bytes 73736 | tf_op jit(solution)/shard_map/ppermute | solution.py:805
  9.2 7.2 %collective-permute-start.3 = (bf16[16,768]{1,0:T(8,128)(2,1)S(1)}, bf16[16,768]{1,0:T(8,128)(2,1)S(1)}, u32[]{:S(2)}, u32[]{:S(2)}) collective-permute-start(bf16[16,768]{1,0:T(8,128)(2,1)S(1)} %copy-done.13), channel_id=1, source_target_pairs={{0,2},{1,3},{2,0},{3,1},{4,6},{5,7},{6,4},{7,5},{8,10},{9,11},{10,... | collective-permute-start | bytes 73736 | tf_op jit(solution)/shard_map/ppermute | solution.py:805
  13.8 4.1 %collective-permute-start.4 = (bf16[16,768]{1,0:T(8,128)(2,1)S(1)}, bf16[16,768]{1,0:T(8,128)(2,1)S(1)}, u32[]{:S(2)}, u32[]{:S(2)}) collective-permute-start(bf16[16,768]{1,0:T(8,128)(2,1)S(1)} %copy-done.13), channel_id=1, source_target_pairs={{0,3},{1,2},{2,1},{3,0},{4,7},{5,6},{6,5},{7,4},{8,11},{9,10},{10,... | collective-permute-start | bytes 73736 | tf_op jit(solution)/shard_map/ppermute | solution.py:805
  16.4 14.2 %collective-permute-start.12 = (s32[2,1024]{1,0:T(2,128)S(1)}, s32[2,1024]{1,0:T(2,128)S(1)}, u32[]{:S(2)}, u32[]{:S(2)}) collective-permute-start(s32[2,1024]{1,0:T(2,128)S(1)} %pad_add_fusion), channel_id=1, source_target_pairs={{0,1},{1,0},{2,3},{3,2},{4,5},{5,4},{6,7},{7,6},{8,9},{9,8},{10,11... | collective-permute-start | bytes 24584 | tf_op jit(solution)/shard_map/ppermute | solution.py:805
  17.9 42.1 %collective-permute-start.5 = (bf16[192,512]{1,0:T(8,128)(2,1)}, bf16[192,512]{1,0:T(8,128)(2,1)}, u32[]{:S(2)}, u32[]{:S(2)}) collective-permute-start(bf16[192,512]{1,0:T(8,128)(2,1)} %get-tuple-element.112), channel_id=1, source_target_pairs={{0,1},{1,0},{2,3},{3,2},{4,5},{5,4},{6,7},{7,6},{8,9},{9,8},{10,11... | collective-permute-start | bytes 589832 | tf_op jit(solution)/shard_map/ppermute | solution.py:805
  24.8 36.8 %collective-permute-start.6 = (bf16[576,512]{1,0:T(8,128)(2,1)}, bf16[576,512]{1,0:T(8,128)(2,1)}, u32[]{:S(2)}, u32[]{:S(2)}) collective-permute-start(bf16[576,512]{1,0:T(8,128)(2,1)} %get-tuple-element.113), channel_id=1, source_target_pairs={{0,2},{1,3},{2,0},{3,1},{4,6},{5,7},{6,4},{7,5},{8,10},{9,11},{10,... | collective-permute-start | bytes 1769480 | tf_op jit(solution)/shard_map/ppermute | solution.py:805
  30.6 27.7 %collective-permute-start.9 = (bf16[768,512]{1,0:T(8,128)(2,1)}, bf16[768,512]{1,0:T(8,128)(2,1)}, u32[]{:S(2)}, u32[]{:S(2)}) collective-permute-start(bf16[768,512]{1,0:T(8,128)(2,1)} %get-tuple-element.119), channel_id=1, source_target_pairs={{0,2},{1,3},{2,0},{3,1},{4,6},{5,7},{6,4},{7,5},{8,10},{9,11},{10,... | collective-permute-start | bytes 2359304 | tf_op jit(solution)/shard_map/ppermute | solution.py:805
  31.2 30.4 %collective-permute-start.7 = (bf16[192,512]{1,0:T(8,128)(2,1)S(1)}, bf16[192,512]{1,0:T(8,128)(2,1)}, u32[]{:S(2)}, u32[]{:S(2)}) collective-permute-start(bf16[192,512]{1,0:T(8,128)(2,1)S(1)} %copy-done.29), channel_id=1, source_target_pairs={{0,3},{1,2},{2,1},{3,0},{4,7},{5,6},{6,5},{7,4},{8,11},{9,10},{10,... | collective-permute-start | bytes 589832 | tf_op jit(solution)/shard_map/ppermute | solution.py:805
  33.7 24.5 %copy-start.27 = (bf16[672,512]{1,0:T(8,128)(2,1)S(1)}, bf16[672,512]{1,0:T(8,128)(2,1)}, u32[]{:S(2)}) copy-start(bf16[672,512]{1,0:T(8,128)(2,1)} %get-tuple-element.124) | copy-start | bytes 2064388
  58.3 31.1 %collective-permute-start.10 = (bf16[672,512]{1,0:T(8,128)(2,1)S(1)}, bf16[672,512]{1,0:T(8,128)(2,1)S(1)}, u32[]{:S(2)}, u32[]{:S(2)}) collective-permute-start(bf16[672,512]{1,0:T(8,128)(2,1)S(1)} %copy-done.27), channel_id=1, source_target_pairs={{0,2},{1,3},{2,0},{3,1},{4,6},{5,7},{6,4},{7,5},{8,10},{9,11},{10,... | collective-permute-start | bytes 2064392 | tf_op jit(solution)/shard_map/ppermute | solution.py:805
  75.3 15.5 %copy-start.26 = (bf16[768,512]{1,0:T(8,128)(2,1)S(1)}, bf16[768,512]{1,0:T(8,128)(2,1)}, u32[]{:S(2)}) copy-start(bf16[768,512]{1,0:T(8,128)(2,1)} %get-tuple-element.172) | copy-start | bytes 2359300
  89.3 55.1 %collective-permute-start.11 = (bf16[768,512]{1,0:T(8,128)(2,1)}, bf16[768,512]{1,0:T(8,128)(2,1)}, u32[]{:S(2)}, u32[]{:S(2)}) collective-permute-start(bf16[768,512]{1,0:T(8,128)(2,1)} %get-tuple-element.125), channel_id=1, source_target_pairs={{0,2},{1,3},{2,0},{3,1},{4,6},{5,7},{6,4},{7,5},{8,10},{9,11},{10,... | collective-permute-start | bytes 2359304 | tf_op jit(solution)/shard_map/ppermute | solution.py:805
  90.8 51.8 %collective-permute-start.23 = (bf16[768,512]{1,0:T(8,128)(2,1)S(1)}, bf16[768,512]{1,0:T(8,128)(2,1)S(1)}, u32[]{:S(2)}, u32[]{:S(2)}) collective-permute-start(bf16[768,512]{1,0:T(8,128)(2,1)S(1)} %copy-done.26), channel_id=1, source_target_pairs={{0,2},{1,3},{2,0},{3,1},{4,6},{5,7},{6,4},{7,5},{8,10},{9,11},{10,... | collective-permute-start | bytes 2359304 | tf_op jit(solution)/shard_map/ppermute | solution.py:805
  91.4 77.4 %collective-permute-start.31 = (bf16[768,512]{1,0:T(8,128)(2,1)}, bf16[768,512]{1,0:T(8,128)(2,1)S(1)}, u32[]{:S(2)}, u32[]{:S(2)}) collective-permute-start(bf16[768,512]{1,0:T(8,128)(2,1)} %get-tuple-element.175), channel_id=1, source_target_pairs={{0,2},{1,3},{2,0},{3,1},{4,6},{5,7},{6,4},{7,5},{8,10},{9,11},{10,... | collective-permute-start | bytes 2359304 | tf_op jit(solution)/shard_map/ppermute | solution.py:805
  92.8 49.8 %copy-start.10 = (bf16[768,512]{1,0:T(8,128)(2,1)S(1)}, bf16[768,512]{1,0:T(8,128)(2,1)}, u32[]{:S(2)}) copy-start(bf16[768,512]{1,0:T(8,128)(2,1)} %get-tuple-element.170) | copy-start | bytes 2359300
  142.9 28.9 %collective-permute-start.24 = (bf16[4,96,512]{2,1,0:T(8,128)(2,1)S(1)}, bf16[4,96,512]{2,1,0:T(8,128)(2,1)S(1)}, u32[]{:S(2)}, u32[]{:S(2)}) collective-permute-start(bf16[4,96,512]{2,1,0:T(8,128)(2,1)S(1)} %get-tuple-element.186), channel_id=1, source_target_pairs={{0,4},{4,0},{8,12},{12,8},{16,20},{20,16},{24,28},{28,24},{1,5},{5... | collective-permute-start | bytes 1179656 | tf_op jit(solution)/shard_map/ppermute | solution.py:809
  158.4 10.4 %copy-start.9 = (bf16[768,512]{1,0:T(8,128)(2,1)S(1)}, bf16[768,512]{1,0:T(8,128)(2,1)}, u32[]{:S(2)}) copy-start(bf16[768,512]{1,0:T(8,128)(2,1)} %get-tuple-element.173) | copy-start | bytes 2359300
  168.2 31.0 %collective-permute-start.15 = (bf16[768,512]{1,0:T(8,128)(2,1)}, bf16[768,512]{1,0:T(8,128)(2,1)}, u32[]{:S(2)}, u32[]{:S(2)}) collective-permute-start(bf16[768,512]{1,0:T(8,128)(2,1)} %get-tuple-element.159), channel_id=1, source_target_pairs={{0,2},{1,3},{2,0},{3,1},{4,6},{5,7},{6,4},{7,5},{8,10},{9,11},{10,... | collective-permute-start | bytes 2359304 | tf_op jit(solution)/shard_map/ppermute | solution.py:805
  169.9 16.4 %collective-permute-start.32 = (bf16[4,96,512]{2,1,0:T(8,128)(2,1)S(1)}, bf16[4,96,512]{2,1,0:T(8,128)(2,1)S(1)}, u32[]{:S(2)}, u32[]{:S(2)}) collective-permute-start(bf16[4,96,512]{2,1,0:T(8,128)(2,1)S(1)} %get-tuple-element.184), channel_id=1, source_target_pairs={{0,4},{4,0},{8,12},{12,8},{16,20},{20,16},{24,28},{28,24},{1,5},{5... | collective-permute-start | bytes 1179656 | tf_op jit(solution)/shard_map/ppermute | solution.py:809
  170.4 34.3 %collective-permute-start.39 = (bf16[768,512]{1,0:T(8,128)(2,1)}, bf16[768,512]{1,0:T(8,128)(2,1)}, u32[]{:S(2)}, u32[]{:S(2)}) collective-permute-start(bf16[768,512]{1,0:T(8,128)(2,1)} %get-tuple-element.177), channel_id=1, source_target_pairs={{0,2},{1,3},{2,0},{3,1},{4,6},{5,7},{6,4},{7,5},{8,10},{9,11},{10,... | collective-permute-start | bytes 2359304 | tf_op jit(solution)/shard_map/ppermute | solution.py:805
  171.8 14.4 %copy-start.11 = (bf16[4,96,512]{2,1,0:T(8,128)(2,1)}, bf16[4,96,512]{2,1,0:T(8,128)(2,1)S(1)}, u32[]{:S(2)}) copy-start(bf16[4,96,512]{2,1,0:T(8,128)(2,1)S(1)} %collective-permute-done.24) | copy-start | bytes 1179652
  172.6 16.0 %collective-permute-start.25 = (bf16[4,48,512]{2,1,0:T(8,128)(2,1)}, bf16[4,48,512]{2,1,0:T(8,128)(2,1)}, u32[]{:S(2)}, u32[]{:S(2)}) collective-permute-start(bf16[4,48,512]{2,1,0:T(8,128)(2,1)} %add_convert_fusion.18), channel_id=1, source_target_pairs={{0,8},{4,12},{8,0},{12,4},{16,24},{20,28},{24,16},{28,20},{1,9},{5... | collective-permute-start | bytes 589832 | tf_op jit(solution)/shard_map/ppermute | solution.py:809
  186.1 13.4 %copy-start.8 = (bf16[768,512]{1,0:T(8,128)(2,1)S(1)}, bf16[768,512]{1,0:T(8,128)(2,1)}, u32[]{:S(2)}) copy-start(bf16[768,512]{1,0:T(8,128)(2,1)} %get-tuple-element.158) | copy-start | bytes 2359300
  186.1 89.3 %collective-permute-start.13 = (bf16[1024,768]{1,0:T(8,128)(2,1)}, bf16[1024,768]{1,0:T(8,128)(2,1)S(1)}, u32[]{:S(2)}, u32[]{:S(2)}) collective-permute-start(bf16[1024,768]{1,0:T(8,128)(2,1)} %get-tuple-element.143), channel_id=1, source_target_pairs={{0,1},{1,0},{2,3},{3,2},{4,5},{5,4},{6,7},{7,6},{8,9},{9,8},{10,11... | collective-permute-start | bytes 4718600 | tf_op jit(solution)/shard_map/ppermute | solution.py:805
  187.0 88.5 %collective-permute-start.14 = (bf16[1024,768]{1,0:T(8,128)(2,1)}, bf16[1024,768]{1,0:T(8,128)(2,1)S(1)}, u32[]{:S(2)}, u32[]{:S(2)}) collective-permute-start(bf16[1024,768]{1,0:T(8,128)(2,1)} %get-tuple-element.145), channel_id=1, source_target_pairs={{0,1},{1,0},{2,3},{3,2},{4,5},{5,4},{6,7},{7,6},{8,9},{9,8},{10,11... | collective-permute-start | bytes 4718600 | tf_op jit(solution)/shard_map/ppermute | solution.py:805
  188.6 16.7 %copy-start.7 = (bf16[768,512]{1,0:T(8,128)(2,1)S(1)}, bf16[768,512]{1,0:T(8,128)(2,1)}, u32[]{:S(2)}) copy-start(bf16[768,512]{1,0:T(8,128)(2,1)} %get-tuple-element.176) | copy-start | bytes 2359300
  188.6 6.9 %collective-permute-start.33 = (bf16[4,48,512]{2,1,0:T(8,128)(2,1)S(1)}, bf16[4,48,512]{2,1,0:T(8,128)(2,1)S(1)}, u32[]{:S(2)}, u32[]{:S(2)}) collective-permute-start(bf16[4,48,512]{2,1,0:T(8,128)(2,1)S(1)} %add_convert_fusion.14), channel_id=1, source_target_pairs={{0,8},{4,12},{8,0},{12,4},{16,24},{20,28},{24,16},{28,20},{1,9},{5... | collective-permute-start | bytes 589832 | tf_op jit(solution)/shard_map/ppermute | solution.py:809
  195.5 15.4 %collective-permute-start.26 = (bf16[4,48,512]{2,1,0:T(8,128)(2,1)S(1)}, bf16[4,48,512]{2,1,0:T(8,128)(2,1)S(1)}, u32[]{:S(2)}, u32[]{:S(2)}) collective-permute-start(bf16[4,48,512]{2,1,0:T(8,128)(2,1)S(1)} %add_convert_fusion.17), channel_id=1, source_target_pairs={{0,16},{4,20},{8,24},{12,28},{16,0},{20,4},{24,8},{28,12},{1,17},{... | collective-permute-start | bytes 589832 | tf_op jit(solution)/shard_map/ppermute | solution.py:809
  199.2 15.8 %collective-permute-start.34 = (bf16[4,48,512]{2,1,0:T(8,128)(2,1)S(1)}, bf16[4,48,512]{2,1,0:T(8,128)(2,1)S(1)}, u32[]{:S(2)}, u32[]{:S(2)}) collective-permute-start(bf16[4,48,512]{2,1,0:T(8,128)(2,1)S(1)} %add_convert_fusion.13), channel_id=1, source_target_pairs={{0,16},{4,20},{8,24},{12,28},{16,0},{20,4},{24,8},{28,12},{1,17},{... | collective-permute-start | bytes 589832 | tf_op jit(solution)/shard_map/ppermute | solution.py:809
  204.7 11.7 %collective-permute-start.16 = (bf16[8,48,512]{2,1,0:T(8,128)(2,1)S(1)}, bf16[8,48,512]{2,1,0:T(8,128)(2,1)S(1)}, u32[]{:S(2)}, u32[]{:S(2)}) collective-permute-start(bf16[8,48,512]{2,1,0:T(8,128)(2,1)S(1)} %get-tuple-element.188), channel_id=1, source_target_pairs={{0,4},{4,0},{8,12},{12,8},{16,20},{20,16},{24,28},{28,24},{1,5},{5... | collective-permute-start | bytes 1179656 | tf_op jit(solution)/shard_map/ppermute | solution.py:809
  210.8 13.8 %collective-permute-start.40 = (bf16[4,96,512]{2,1,0:T(8,128)(2,1)S(1)}, bf16[4,96,512]{2,1,0:T(8,128)(2,1)S(1)}, u32[]{:S(2)}, u32[]{:S(2)}) collective-permute-start(bf16[4,96,512]{2,1,0:T(8,128)(2,1)S(1)} %get-tuple-element.182), channel_id=1, source_target_pairs={{0,4},{4,0},{8,12},{12,8},{16,20},{20,16},{24,28},{28,24},{1,5},{5... | collective-permute-start | bytes 1179656 | tf_op jit(solution)/shard_map/ppermute | solution.py:809
  215.0 1.2 collective-permute-start.27
  216.2 1.8 collective-permute-start.35
  216.4 41.5 %copy-start.4 = (bf16[4,48,512]{2,1,0:T(8,128)(2,1)}, bf16[4,48,512]{2,1,0:T(8,128)(2,1)S(1)}, u32[]{:S(2)}) copy-start(bf16[4,48,512]{2,1,0:T(8,128)(2,1)S(1)} %pad_maximum_fusion.1.refs_0_) | copy-start | bytes 589828
  216.4 41.5 %collective-permute-start.28 = (bf16[4,48,512]{2,1,0:T(8,128)(2,1)S(1)}, bf16[4,48,512]{2,1,0:T(8,128)(2,1)S(1)}, u32[]{:S(2)}, u32[]{:S(2)}) collective-permute-start(bf16[4,48,512]{2,1,0:T(8,128)(2,1)S(1)} %pad_maximum_fusion.1.refs_0_), channel_id=1, source_target_pairs={{0,4},{4,0},{8,12},{12,8},{16,20},{20,16},{24,28},{28,24},{1,5},{5... | collective-permute-start | bytes 589832 | tf_op jit(solution)/shard_map/ppermute | solution.py:809
  218.0 8.7 %collective-permute-start.17 = (bf16[8,24,512]{2,1,0:T(8,128)(2,1)S(1)}, bf16[8,24,512]{2,1,0:T(8,128)(2,1)S(1)}, u32[]{:S(2)}, u32[]{:S(2)}) collective-permute-start(bf16[8,24,512]{2,1,0:T(8,128)(2,1)S(1)} %add_convert_fusion.22), channel_id=1, source_target_pairs={{0,8},{4,12},{8,0},{12,4},{16,24},{20,28},{24,16},{28,20},{1,9},{5... | collective-permute-start | bytes 589832 | tf_op jit(solution)/shard_map/ppermute | solution.py:809
  219.0 47.7 %copy-start.5 = (bf16[4,48,512]{2,1,0:T(8,128)(2,1)}, bf16[4,48,512]{2,1,0:T(8,128)(2,1)S(1)}, u32[]{:S(2)}) copy-start(bf16[4,48,512]{2,1,0:T(8,128)(2,1)S(1)} %pad_maximum_fusion.2.refs_4_) | copy-start | bytes 589828
  224.6 33.8 %collective-permute-start.29 = (bf16[4,48,512]{2,1,0:T(8,128)(2,1)S(1)}, bf16[4,48,512]{2,1,0:T(8,128)(2,1)S(1)}, u32[]{:S(2)}, u32[]{:S(2)}) collective-permute-start(bf16[4,48,512]{2,1,0:T(8,128)(2,1)S(1)} %pad_maximum_fusion.1.refs_0_), channel_id=1, source_target_pairs={{0,8},{4,12},{8,0},{12,4},{16,24},{20,28},{24,16},{28,20},{1,9},{5... | collective-permute-start | bytes 589832 | tf_op jit(solution)/shard_map/ppermute | solution.py:809
  226.8 6.6 %collective-permute-start.41 = (bf16[4,48,512]{2,1,0:T(8,128)(2,1)S(1)}, bf16[4,48,512]{2,1,0:T(8,128)(2,1)S(1)}, u32[]{:S(2)}, u32[]{:S(2)}) collective-permute-start(bf16[4,48,512]{2,1,0:T(8,128)(2,1)S(1)} %add_convert_fusion.10), channel_id=1, source_target_pairs={{0,8},{4,12},{8,0},{12,4},{16,24},{20,28},{24,16},{28,20},{1,9},{5... | collective-permute-start | bytes 589832 | tf_op jit(solution)/shard_map/ppermute | solution.py:809
  233.4 13.6 %collective-permute-start.18 = (bf16[8,24,512]{2,1,0:T(8,128)(2,1)S(1)}, bf16[8,24,512]{2,1,0:T(8,128)(2,1)S(1)}, u32[]{:S(2)}, u32[]{:S(2)}) collective-permute-start(bf16[8,24,512]{2,1,0:T(8,128)(2,1)S(1)} %add_convert_fusion.21), channel_id=1, source_target_pairs={{0,16},{4,20},{8,24},{12,28},{16,0},{20,4},{24,8},{28,12},{1,17},{... | collective-permute-start | bytes 589832 | tf_op jit(solution)/shard_map/ppermute | solution.py:809
  247.0 8.7 %collective-permute-start.42 = (bf16[4,48,512]{2,1,0:T(8,128)(2,1)S(1)}, bf16[4,48,512]{2,1,0:T(8,128)(2,1)S(1)}, u32[]{:S(2)}, u32[]{:S(2)}) collective-permute-start(bf16[4,48,512]{2,1,0:T(8,128)(2,1)S(1)} %add_convert_fusion.9), channel_id=1, source_target_pairs={{0,16},{4,20},{8,24},{12,28},{16,0},{20,4},{24,8},{28,12},{1,17},{... | collective-permute-start | bytes 589832 | tf_op jit(solution)/shard_map/ppermute | solution.py:809
  255.7 1.3 collective-permute-start.43
  257.0 1.3 collective-permute-start.19
  257.9 34.9 %copy-start.14 = (bf16[4,48,512]{2,1,0:T(8,128)(2,1)}, bf16[4,48,512]{2,1,0:T(8,128)(2,1)S(1)}, u32[]{:S(2)}) copy-start(bf16[4,48,512]{2,1,0:T(8,128)(2,1)S(1)} %collective-permute-done.28.refs_1_) | copy-start | bytes 589828
  257.9 8.8 %collective-permute-start.30 = (bf16[4,48,512]{2,1,0:T(8,128)(2,1)S(1)}, bf16[4,48,512]{2,1,0:T(8,128)(2,1)S(1)}, u32[]{:S(2)}, u32[]{:S(2)}) collective-permute-start(bf16[4,48,512]{2,1,0:T(8,128)(2,1)S(1)} %pad_maximum_fusion.1.refs_0_), channel_id=1, source_target_pairs={{0,12},{4,8},{8,4},{12,0},{16,28},{20,24},{24,20},{28,16},{1,13},{... | collective-permute-start | bytes 589832 | tf_op jit(solution)/shard_map/ppermute | solution.py:809
  258.3 11.2 %collective-permute-start.36 = (bf16[4,48,512]{2,1,0:T(8,128)(2,1)S(1)}, bf16[4,48,512]{2,1,0:T(8,128)(2,1)S(1)}, u32[]{:S(2)}, u32[]{:S(2)}) collective-permute-start(bf16[4,48,512]{2,1,0:T(8,128)(2,1)S(1)} %pad_maximum_fusion.2.refs_4_), channel_id=1, source_target_pairs={{0,4},{4,0},{8,12},{12,8},{16,20},{20,16},{24,28},{28,24},{1,5},{5... | collective-permute-start | bytes 589832 | tf_op jit(solution)/shard_map/ppermute | solution.py:809
  258.4 11.4 %copy-start.15 = (bf16[4,48,512]{2,1,0:T(8,128)(2,1)}, bf16[4,48,512]{2,1,0:T(8,128)(2,1)S(1)}, u32[]{:S(2)}) copy-start(bf16[4,48,512]{2,1,0:T(8,128)(2,1)S(1)} %collective-permute-done.29.refs_2_) | copy-start | bytes 589828
  258.5 11.5 %collective-permute-start.37 = (bf16[4,48,512]{2,1,0:T(8,128)(2,1)S(1)}, bf16[4,48,512]{2,1,0:T(8,128)(2,1)S(1)}, u32[]{:S(2)}, u32[]{:S(2)}) collective-permute-start(bf16[4,48,512]{2,1,0:T(8,128)(2,1)S(1)} %pad_maximum_fusion.2.refs_4_), channel_id=1, source_target_pairs={{0,8},{4,12},{8,0},{12,4},{16,24},{20,28},{24,16},{28,20},{1,9},{5... | collective-permute-start | bytes 589832 | tf_op jit(solution)/shard_map/ppermute | solution.py:809
  266.7 12.2 %copy-start.16 = (bf16[4,48,512]{2,1,0:T(8,128)(2,1)}, bf16[4,48,512]{2,1,0:T(8,128)(2,1)S(1)}, u32[]{:S(2)}) copy-start(bf16[4,48,512]{2,1,0:T(8,128)(2,1)S(1)} %collective-permute-done.30.refs_3_) | copy-start | bytes 589828
  266.7 8.7 %collective-permute-start.38 = (bf16[4,48,512]{2,1,0:T(8,128)(2,1)S(1)}, bf16[4,48,512]{2,1,0:T(8,128)(2,1)S(1)}, u32[]{:S(2)}, u32[]{:S(2)}) collective-permute-start(bf16[4,48,512]{2,1,0:T(8,128)(2,1)S(1)} %pad_maximum_fusion.2.refs_4_), channel_id=1, source_target_pairs={{0,12},{4,8},{8,4},{12,0},{16,28},{20,24},{24,20},{28,16},{1,13},{... | collective-permute-start | bytes 589832 | tf_op jit(solution)/shard_map/ppermute | solution.py:809
  269.4 10.2 %copy-start.17 = (bf16[4,48,512]{2,1,0:T(8,128)(2,1)}, bf16[4,48,512]{2,1,0:T(8,128)(2,1)S(1)}, u32[]{:S(2)}) copy-start(bf16[4,48,512]{2,1,0:T(8,128)(2,1)S(1)} %collective-permute-done.36.refs_5_) | copy-start | bytes 589828
  269.5 10.2 %collective-permute-start.44 = (bf16[4,48,512]{2,1,0:T(8,128)(2,1)}, bf16[4,48,512]{2,1,0:T(8,128)(2,1)S(1)}, u32[]{:S(2)}, u32[]{:S(2)}) collective-permute-start(bf16[4,48,512]{2,1,0:T(8,128)(2,1)} %pad_maximum_fusion.3.refs_8_), channel_id=1, source_target_pairs={{0,4},{4,0},{8,12},{12,8},{16,20},{20,16},{24,28},{28,24},{1,5},{5... | collective-permute-start | bytes 589832 | tf_op jit(solution)/shard_map/ppermute | solution.py:809
  269.9 22.9 %copy-start.6 = (bf16[8,24,512]{2,1,0:T(8,128)(2,1)}, bf16[8,24,512]{2,1,0:T(8,128)(2,1)S(1)}, u32[]{:S(2)}) copy-start(bf16[8,24,512]{2,1,0:T(8,128)(2,1)S(1)} %pad_maximum_fusion.refs_0_) | copy-start | bytes 589828
  269.9 9.8 %copy-start.18 = (bf16[4,48,512]{2,1,0:T(8,128)(2,1)}, bf16[4,48,512]{2,1,0:T(8,128)(2,1)S(1)}, u32[]{:S(2)}) copy-start(bf16[4,48,512]{2,1,0:T(8,128)(2,1)S(1)} %collective-permute-done.37.refs_6_) | copy-start | bytes 589828
  269.9 29.6 %collective-permute-start.45 = (bf16[4,48,512]{2,1,0:T(8,128)(2,1)}, bf16[4,48,512]{2,1,0:T(8,128)(2,1)}, u32[]{:S(2)}, u32[]{:S(2)}) collective-permute-start(bf16[4,48,512]{2,1,0:T(8,128)(2,1)} %pad_maximum_fusion.3.refs_8_), channel_id=1, source_target_pairs={{0,8},{4,12},{8,0},{12,4},{16,24},{20,28},{24,16},{28,20},{1,9},{5... | collective-permute-start | bytes 589832 | tf_op jit(solution)/shard_map/ppermute | solution.py:809
  275.4 24.2 %collective-permute-start.46 = (bf16[4,48,512]{2,1,0:T(8,128)(2,1)}, bf16[4,48,512]{2,1,0:T(8,128)(2,1)}, u32[]{:S(2)}, u32[]{:S(2)}) collective-permute-start(bf16[4,48,512]{2,1,0:T(8,128)(2,1)} %pad_maximum_fusion.3.refs_8_), channel_id=1, source_target_pairs={{0,12},{4,8},{8,4},{12,0},{16,28},{20,24},{24,20},{28,16},{1,13},{... | collective-permute-start | bytes 589832 | tf_op jit(solution)/shard_map/ppermute | solution.py:809
  275.4 17.4 %copy-start.1 = (bf16[1024,768]{1,0:T(8,128)(2,1)}, bf16[1024,768]{1,0:T(8,128)(2,1)S(1)}, u32[]{:S(2)}) copy-start(bf16[1024,768]{1,0:T(8,128)(2,1)S(1)} %collective-permute-done.13.oi) | copy-start | bytes 4718596
  275.4 28.9 %collective-permute-start.20 = (bf16[8,24,512]{2,1,0:T(8,128)(2,1)S(1)}, bf16[8,24,512]{2,1,0:T(8,128)(2,1)}, u32[]{:S(2)}, u32[]{:S(2)}) collective-permute-start(bf16[8,24,512]{2,1,0:T(8,128)(2,1)S(1)} %pad_maximum_fusion.refs_0_), channel_id=1, source_target_pairs={{0,4},{4,0},{8,12},{12,8},{16,20},{20,16},{24,28},{28,24},{1,5},{5... | collective-permute-start | bytes 589832 | tf_op jit(solution)/shard_map/ppermute | solution.py:809
  275.5 17.3 %copy-start.2 = (bf16[1024,768]{1,0:T(8,128)(2,1)}, bf16[1024,768]{1,0:T(8,128)(2,1)S(1)}, u32[]{:S(2)}) copy-start(bf16[1024,768]{1,0:T(8,128)(2,1)S(1)} %collective-permute-done.14.hi) | copy-start | bytes 4718596
  275.5 28.8 %collective-permute-start.21 = (bf16[8,24,512]{2,1,0:T(8,128)(2,1)S(1)}, bf16[8,24,512]{2,1,0:T(8,128)(2,1)}, u32[]{:S(2)}, u32[]{:S(2)}) collective-permute-start(bf16[8,24,512]{2,1,0:T(8,128)(2,1)S(1)} %pad_maximum_fusion.refs_0_), channel_id=1, source_target_pairs={{0,8},{4,12},{8,0},{12,4},{16,24},{20,28},{24,16},{28,20},{1,9},{5... | collective-permute-start | bytes 589832 | tf_op jit(solution)/shard_map/ppermute | solution.py:809
  280.3 24.0 %collective-permute-start.22 = (bf16[8,24,512]{2,1,0:T(8,128)(2,1)S(1)}, bf16[8,24,512]{2,1,0:T(8,128)(2,1)}, u32[]{:S(2)}, u32[]{:S(2)}) collective-permute-start(bf16[8,24,512]{2,1,0:T(8,128)(2,1)S(1)} %pad_maximum_fusion.refs_0_), channel_id=1, source_target_pairs={{0,12},{4,8},{8,4},{12,0},{16,28},{20,24},{24,20},{28,16},{1,13},{... | collective-permute-start | bytes 589832 | tf_op jit(solution)/shard_map/ppermute | solution.py:809
  (13 other events, 51.7 us)
where the time goes:
time: 310 us
  Pallas kernels  163 us (53%)
  waiting for transfers between devices  83.8 us (27%)
  starting transfers between devices  45.9 us (15%)
  other arithmetic  12.8 us (4%)
  local copies, waits for them, and re-layouts  3.28 us (1%)
    ppermute x24, waiting for transfers between devices, to_replica(): return lax.ppermute(value, 'replica', [(r, r ^ k) for r in range(count)])  54.6 us
    pallas_call x1, Pallas kernels, attention(): pl.pallas_call(kern, grid=(2,), in_specs=[SMEM, seq(width), seq(width), f...  49.8 us
    pallas_call x3, Pallas kernels, mlp_wave(): pl.pallas_call(kern, grid=(4,), in_specs=[SMEM, row, col, row, col] + [fi...  41.6 us
    ppermute x23, waiting for transfers between devices, to_shard(): return lax.ppermute(value, 'shard', [(s, s ^ k) for s in range(4)])  29.2 us
    ppermute x24, starting transfers between devices, to_replica(): return lax.ppermute(value, 'replica', [(r, r ^ k) for r in range(count)])  27.3 us
    pallas_call x2, Pallas kernels, outputs(): pl.pallas_call(kern, grid=(4,), in_specs=[rows(wid2)] * (2 * n_w) + [fixe...  23.9 us
    ppermute x23, starting transfers between devices, to_shard(): return lax.ppermute(value, 'shard', [(s, s ^ k) for s in range(4)])  18.6 us
    pallas_call x2, Pallas kernels, norm_pair(): pl.pallas_call(kern, grid=(2,), in_specs=[src, src] + [small] * n_near +...  12.5 us
  transfers between devices with their start and end apart: 47, of which 19 were waited for; matrix products, arithmetic and copies ran while one was open for 4% of the time, Pallas kernels for 52%

commit v1 on v0

--- a/solution.py
+++ b/solution.py
@@ -211,7 +211,7 @@
     base = 2 * which
 
     def kern(tok_ref, dy_ref, *refs):
-        nm, nmt, na, nat, dyc, dyt, ob, vec_ref = refs[n_near + len(prev) :]
+        nm, na, dyc, ob, vec_ref = refs[n_near + len(prev) :]
         vec_ref[...] = sum([r[...].astype(F32) for r in refs[1:n_near]], refs[0][...].astype(F32))
         xhat, _ = normalize(tok_ref[...].astype(F32))
         a = (xhat * vec_ref[0:1, :] + vec_ref[1:2, :]).astype(BF16)
@@ -220,9 +220,6 @@
         na[...] = a
         nm[...] = m
         dyc[...] = g
-        nat[...] = a.T
-        nmt[...] = m.T
-        dyt[...] = g.T
 
         @pl.when(pl.program_id(0) == 0)
         def _():
@@ -231,7 +228,6 @@
         ob[...] += sum8(g.astype(F32))
 
     row = pl.BlockSpec((blk, width), lambda i: (i + base, 0))
-    col = pl.BlockSpec((width, blk), lambda i: (0, i + base))
     src = pl.BlockSpec((blk, width), lambda i: (i, 0))
     whole = pl.BlockSpec((8, width), lambda i: (0, 0))
     small = pl.BlockSpec((16, width), lambda i: (0, 0))
@@ -239,8 +235,8 @@
         kern,
         grid=(2,),
         in_specs=[src, src] + [small] * n_near + [ANY] * len(prev),
-        out_specs=[row, col, row, col, row, col, whole, small],
-        out_shape=[shape((2 * n_tok, width), BF16), shape((width, 2 * n_tok), BF16)] * 3
+        out_specs=[row, row, row, whole, small],
+        out_shape=[shape((2 * n_tok, width), BF16)] * 3
         + [shape((8, width), F32), shape((16, width), F32)],
         input_output_aliases={2 + n_near + i: i for i in range(len(prev))},
         cost_estimate=pl.CostEstimate(
@@ -248,7 +244,22 @@
         ),
         name="norm_pair",
     )(tok, dy, *near, *prev)
-    return res[:6], res[6], res[7]
+    return res[:3], res[3], res[4]
+
+
+def write_table(outs, tbl, lanes):
+    width = tbl.shape[1]
+    for out in outs:
+        at = out.shape[0] - 32
+        out[at : at + 16, :] = tbl[:, :lanes].astype(BF16)
+        out[at + 16 :, : width - lanes] = tbl[:, lanes:].astype(BF16)
+        out[at + 16 :, width - lanes :] = jnp.zeros((16, 2 * lanes - width), BF16)
+
+
+def put_hidden_bias(tbl, s, w, u):
+    wd = u.shape[1] // 2
+    tbl[pl.ds(8 + s, 1), w * wd : (w + 1) * wd] = u[:, :wd]
+    tbl[pl.ds(8 + jnp.bitwise_xor(s, 2), 1), w * wd : (w + 1) * wd] = u[:, wd:]
 
 
 def col_sums(v):
@@ -258,7 +269,7 @@
     return sum8(part.T)
 
 
-def mlp_wave(wave, sc, nm, nmt, dy, dyt, pieces, down_at, down_own, vec, split):
+def mlp_wave(wave, sc, nm, dy, pieces, down_at, down_own, vec, table=None):
     n_tok, width = nm.shape
     blk = n_tok // 4
     rows = width // 4
@@ -273,14 +284,15 @@
     where = [next(i for i, t in enumerate(srcs) if t is arr) for arr, _ in list(pieces) + [down_at]]
     n_src = len(srcs)
 
-    def kern(sc_ref, nm_r, nmt_r, dy_r, dyt_r, d0, vec_r, *refs):
+    def kern(sc_ref, nm_r, dy_r, d0, vec_r, *refs):
         got, refs = refs[:n_src], refs[n_src:]
+        if table is not None:
+            t_r, refs = refs[0], refs[1:]
         hid_o, gl_o, w_s, wd_s, ub, rs = refs[:6]
-        b_s, acc_u, acc_d = refs[-3:]
-        grads = refs[6:-3]
+        b_s, acc_u, acc_d, tbl = refs[-4:]
+        keep, to1, to2, to3 = refs[6:-4]
         i = pl.program_id(0)
         s = sc_ref[0]
-        y = jnp.right_shift(s, 1)
 
         @pl.when(i == 0)
         def _():
@@ -305,46 +317,50 @@
         gl = gu.astype(BF16)
         hid_o[...] = hid
         gl_o[...] = gl
-        acc_u[...] += dnn(nmt_r[...], gl)
-        acc_d[...] += dnn(dyt_r[...], hid)
+        acc_u[...] += dtn(nm_r[...], gl)
+        acc_d[...] += dtn(dy_r[...], hid)
         ub[...] += sum8(gu)
 
         @pl.when(i == pl.num_programs(0) - 1)
         def _():
-            mine = pl.multiple_of(y * half, 16)
-            other = pl.multiple_of((1 - y) * half, 16)
-            if split:
-                keep_u, send_u, keep_d, send_d = grads
-                d = 0
-            else:
-                keep_u = keep_d = grads[0]
-                send_u = send_d = grads[1]
-                d = half
-            keep_u[:half, :] = acc_u[pl.ds(mine, half), :].astype(BF16)
-            send_u[:half, :wid] = acc_u[pl.ds(other, half), wid:].astype(BF16)
-            send_u[:half, wid:] = acc_u[pl.ds(other, half), :wid].astype(BF16)
-            keep_d[d:, :wid] = acc_d[:half, :wid].astype(BF16)
-            keep_d[d:, wid:] = acc_d[half:, :wid].astype(BF16)
-            send_d[d:, :wid] = acc_d[:half, wid:].astype(BF16)
-            send_d[d:, wid:] = acc_d[half:, wid:].astype(BF16)
+            for k, out in enumerate((keep, to1, to2, to3)):
+                v = acc_u[pl.ds(pl.multiple_of(jnp.bitwise_xor(s, k) * rows, 16), rows), :].astype(BF16)
+                h = wid if k >= 2 else 0
+                out[:rows, :wid] = v[:, h : h + wid]
+                out[:rows, wid:] = v[:, wid - h : wid2 - h]
+            down = slice(rows, rows + half)
+            keep[down, :wid] = acc_d[:half, :wid].astype(BF16)
+            keep[down, wid:] = acc_d[half:, :wid].astype(BF16)
+            to2[down, :wid] = acc_d[:half, wid:].astype(BF16)
+            to2[down, wid:] = acc_d[half:, wid:].astype(BF16)
             w = w_s[...].astype(F32)
             rs[0:8, :] = col_sums(w * acc_u[...])
             rs[8:16, :] = col_sums(w * jnp.sum(ub[...], axis=0, keepdims=True))
+            if table is not None:
+                tbl[...] = t_r[...]
+                line = lambda v: jnp.sum(v, axis=0, keepdims=True)
+                ss = tbl[3:4, :] + line(rs[8:16, :])
+                sg = tbl[2:3, :] + line(rs[0:8, :])
+                tbl[2:3, :] = (sg - vec_r[3:4, :] * ss) / vec_r[2:3, :]
+                tbl[3:4, :] = ss
+                put_hidden_bias(tbl, s, wave, line(ub[...]))
+                write_table((keep, to1, to2, to3), tbl, wid2)
 
     row = pl.BlockSpec((blk, width), lambda i: (i, 0))
-    col = pl.BlockSpec((width, blk), lambda i: (0, i))
     mid = pl.BlockSpec((blk, wid2), lambda i: (i, 0))
 
     def fixed(dims, at=(0, 0)):
         return pl.BlockSpec(dims, lambda i: at)
 
-    grads = [(half, wid2)] * 4 if split else [(width, wid2)] * 2
+    more = 0 if table is None else 32
+    extra = [] if table is None else [table]
+    grads = [(rows + half + more, wid2), (rows + more, wid2)] * 2
     return pl.pallas_call(
         kern,
         grid=(4,),
-        in_specs=[SMEM, row, col, row, col]
+        in_specs=[SMEM, row, row]
         + [fixed((wid, width), (wave, 0)), fixed((16, width))]
-        + [fixed(t.shape) for t in srcs],
+        + [fixed(t.shape) for t in srcs + extra],
         out_specs=[mid, mid, fixed((width, wid2)), fixed((wid2, width)), fixed((8, wid2)), fixed((16, width))]
         + [fixed(g) for g in grads],
         out_shape=[shape((n_tok, wid2), BF16)] * 2
@@ -354,6 +370,7 @@
             pltpu.VMEM((8, wid2), F32),
             pltpu.VMEM((width, wid2), F32),
             pltpu.VMEM((width, wid2), F32),
+            pltpu.VMEM((16, width), F32),
         ],
         cost_estimate=pl.CostEstimate(
             flops=8 * n_tok * width * wid2,
@@ -361,7 +378,7 @@
             transcendentals=2 * n_tok * wid2,
         ),
         name="mlp_wave",
-    )(sc, nm, nmt, dy, dyt, down_own, vec, *srcs)
+    )(sc, nm, dy, down_own, vec, *srcs, *extra)
 
 
 def attention(sc, na, dy, weights, vec, waves_of, seg_rows, cgrad):
@@ -556,24 +573,24 @@
     )(sc, na, dy, vec, waves_of, seg_rows, cgrad, *weights)
 
 
-def attn_terms(sc, nat, dyt, o_all, gqs_all, wqs, vec, sums, ob, ubs, rss):
-    width, total = nat.shape
+def attn_terms(sc, na, dy, o_all, gqs_all, wqs, vec, sums, ob, ubs, rss):
+    total, width = na.shape
     wq = gqs_all.shape[1]
     wh = o_all.shape[1]
     blk = total // 4
-    half = width // 2
     o_rows = width // 4
     n_w = len(ubs)
-
-    def kern(sc_ref, nat_r, dyt_r, o_r, g_r, w_r, vec_r, s0, ob_r, *refs):
+    sizes = [(o_rows * 5 // 2, wq), (o_rows, wq)] * 2
+
+    def kern(sc_ref, na_r, dy_r, o_r, g_r, w_r, vec_r, s0, ob_r, *refs):
         ub_r, rs_r = refs[:n_w], refs[n_w : 2 * n_w]
-        keep, send, acc_q, acc_o, tbl = refs[2 * n_w :]
+        keep, to1, to2, to3, tbl, acc_q, acc_o = refs[2 * n_w :]
         s = sc_ref[0]
         c = jnp.bitwise_and(s, 1)
         y = jnp.right_shift(s, 1)
         i = pl.program_id(0)
-        pq = dnn(nat_r[...], g_r[...])
-        po = dnn(dyt_r[...], o_r[...])
+        pq = dtn(na_r[...], g_r[...])
+        po = dtn(dy_r[...], o_r[...])
 
         @pl.when(i == 0)
         def _():
@@ -587,15 +604,14 @@
 
         @pl.when(i == pl.num_programs(0) - 1)
         def _():
-            mine = pl.multiple_of(y * half, 16)
-            other = pl.multiple_of((1 - y) * half, 16)
-            keep[:half, :] = acc_q[pl.ds(mine, half), :].astype(BF16)
-            send[:half, :] = acc_q[pl.ds(other, half), :].astype(BF16)
+            for k, out in enumerate((keep, to1, to2, to3)):
+                at = pl.multiple_of(jnp.bitwise_xor(s, k) * o_rows, 16)
+                out[:o_rows, :] = acc_q[pl.ds(at, o_rows), :].astype(BF16)
             got = acc_o[...].T
             lower = got[:o_rows, :].astype(BF16)
             upper = got[o_rows:, :].astype(BF16)
-            fold(keep, half, o_rows, jnp.where(y == 0, lower, upper), wq)
-            fold(send, half, o_rows, jnp.where(y == 0, upper, lower), wq)
+            fold(keep, o_rows, o_rows, jnp.where(y == 0, lower, upper), wq)
+            fold(to2, o_rows, o_rows, jnp.where(y == 0, upper, lower), wq)
             line = lambda v: jnp.sum(v, axis=0, keepdims=True)
             w = w_r[...].astype(F32)
             both = s0[...]
@@ -606,46 +622,37 @@
             tbl[...] = jnp.zeros_like(tbl)
             tbl[0:1, :] = (fg - vec_r[1:2, :] * fs) / vec_r[0:1, :]
             tbl[1:2, :] = fs
-            tbl[2:3, :] = (sg - vec_r[3:4, :] * ss) / vec_r[2:3, :]
+            tbl[2:3, :] = sg
             tbl[3:4, :] = ss
             tbl[4:5, :] = line(ob_r[...])
             qb8 = jnp.broadcast_to(line(both[:, :wh]), (8, wh))
             tbl[5:6, :] = head_spread(qb8, c, width)[0:1, :]
             tbl[6:7, : wq - wh] = line(both[:, wh:])
             for w_i, ref in enumerate(ub_r):
-                u = line(ref[...])
-                wd = wq // 2
-                tbl[pl.ds(8 + s, 1), w_i * wd : (w_i + 1) * wd] = u[:, :wd]
-                tbl[pl.ds(8 + jnp.bitwise_xor(s, 2), 1), w_i * wd : (w_i + 1) * wd] = u[:, wd:]
-            at = half + o_rows * 3 // 2
-            for out in (keep, send):
-                out[at : at + 16, :] = tbl[:, :wq].astype(BF16)
-                out[at + 16 : at + 32, : width - wq] = tbl[:, wq:].astype(BF16)
-                out[at + 16 : at + 32, width - wq :] = jnp.zeros((16, 2 * wq - width), BF16)
-                out[at + 32 :, :] = jnp.zeros((width - at - 32, wq), BF16)
+                put_hidden_bias(tbl, s, w_i, line(ref[...]))
 
     def fixed(dims):
         return pl.BlockSpec(dims, lambda i: (0, 0))
 
-    col = pl.BlockSpec((width, blk), lambda i: (0, i))
+    row = pl.BlockSpec((blk, width), lambda i: (i, 0))
     return pl.pallas_call(
         kern,
         grid=(4,),
-        in_specs=[SMEM, col, col, pl.BlockSpec((blk, wh), lambda i: (i, 0)), pl.BlockSpec((blk, wq), lambda i: (i, 0))]
+        in_specs=[SMEM, row, row, pl.BlockSpec((blk, wh), lambda i: (i, 0)), pl.BlockSpec((blk, wq), lambda i: (i, 0))]
         + [fixed((width, wq)), fixed((16, width)), fixed((8, wq)), fixed((8, width))]
         + [fixed((8, wq))] * n_w
         + [fixed((16, width))] * n_w,
-        out_specs=[fixed((width, wq))] * 2,
-        out_shape=[shape((width, wq), BF16)] * 2,
-        scratch_shapes=[pltpu.VMEM((width, wq), F32), pltpu.VMEM((width, wh), F32), pltpu.VMEM((16, width), F32)],
+        out_specs=[fixed(g) for g in sizes] + [fixed((16, width))],
+        out_shape=[shape(g, BF16) for g in sizes] + [shape((16, width), F32)],
+        scratch_shapes=[pltpu.VMEM((width, wq), F32), pltpu.VMEM((width, wh), F32)],
         cost_estimate=pl.CostEstimate(
             flops=2 * total * width * (wq + wh), bytes_accessed=4 * total * width, transcendentals=0
         ),
         name="attn_terms",
-    )(sc, nat, dyt, o_all, gqs_all, wqs, vec, sums, ob, *ubs, *rss)
-
-
-def outputs(which, hids, gls, ups, downs, o_all, gqs_all, wo, wqs, vec):
+    )(sc, na, dy, o_all, gqs_all, wqs, vec, sums, ob, *ubs, *rss)
+
+
+def outputs(which, hids, gls, ups, downs, o_all, gqs_all, wo, wqs, vec, last=()):
     total, wid2 = hids[0].shape
     width = wqs.shape[0]
     n_w = len(hids)
@@ -654,7 +661,8 @@
 
     def kern(*refs):
         h_r, g_r, u_r, d_r = (refs[k * n_w : (k + 1) * n_w] for k in range(4))
-        o_r, q_r, wo_r, wq_r, vec_r, out, hp = refs[4 * n_w :]
+        o_r, q_r, wo_r, wq_r, vec_r = refs[4 * n_w : 4 * n_w + 5]
+        out, hp = refs[-2:]
         br = dnn(o_r[...], wo_r[...])
         ea = dnt(q_r[...], wq_r[...])
         em = None
@@ -662,8 +670,19 @@
             br = br + dnn(h_r[w][...], d_r[w][...])
             t = dnt(g_r[w][...], u_r[w][...])
             em = t if em is None else em + t
-        out[...] = br.astype(BF16)
-        hp[...] = (ea * vec_r[0:1, :] + em * vec_r[2:3, :]).astype(BF16)
+        h = ea * vec_r[0:1, :] + em * vec_r[2:3, :]
+        if not last:
+            out[...] = br.astype(BF16)
+            hp[...] = h.astype(BF16)
+        else:
+            tok_r, dy_r, oi, hi = refs[4 * n_w + 5 : 4 * n_w + 9]
+            x = tok_r[...].astype(F32)
+            xhat, rstd = normalize(x)
+            out[...] = (x + br + oi[...].astype(F32) + vec_r[4:5, :] + vec_r[5:6, :]).astype(BF16)
+            h = h + hi[...].astype(F32)
+            mean = jnp.mean(h, axis=-1, keepdims=True)
+            cov = jnp.mean(h * xhat, axis=-1, keepdims=True)
+            hp[...] = (dy_r[...].astype(F32) + rstd * (h - mean - xhat * cov)).astype(BF16)
 
     def rows(lanes):
         return pl.BlockSpec((blk, lanes), lambda i: (i + base, 0))
@@ -678,41 +697,51 @@
         in_specs=[rows(wid2)] * (2 * n_w)
         + [fixed((width, wid2))] * n_w
         + [fixed((wid2, width))] * n_w
-        + [rows(o_all.shape[1]), rows(gqs_all.shape[1]), fixed(wo.shape), fixed(wqs.shape), fixed((16, width))],
+        + [rows(o_all.shape[1]), rows(gqs_all.shape[1]), fixed(wo.shape), fixed(wqs.shape), fixed((16, width))]
+        + [res] * len(last),
         out_specs=[res, res],
         out_shape=[shape((total // 2, width), BF16)] * 2,
         cost_estimate=pl.CostEstimate(
             flops=total * width * (2 * n_w * wid2 + 900), bytes_accessed=12 * total * width, transcendentals=0
         ),
         name="outputs",
-    )(*hids, *gls, *ups, *downs, o_all, gqs_all, wo, wqs, vec)
-
-
-def finish(tok, dy, out_own, out_in, h_own, h_in, vec):
-    n_tok, width = tok.shape
-    blk = n_tok // 4
-
-    def kern(tok_r, dy_r, oo, oi, ho, hi, vec_r, out, tg):
-        x = tok_r[...].astype(F32)
-        xhat, rstd = normalize(x)
-        out[...] = (x + oo[...].astype(F32) + oi[...].astype(F32) + vec_r[4:5, :] + vec_r[5:6, :]).astype(BF16)
-        h = ho[...].astype(F32) + hi[...].astype(F32)
-        mean = jnp.mean(h, axis=-1, keepdims=True)
-        cov = jnp.mean(h * xhat, axis=-1, keepdims=True)
-        tg[...] = (dy_r[...].astype(F32) + rstd * (h - mean - xhat * cov)).astype(BF16)
-
-    row = pl.BlockSpec((blk, width), lambda i: (i, 0))
-    return pl.pallas_call(
-        kern,
-        grid=(4,),
-        in_specs=[row] * 6 + [pl.BlockSpec((16, width), lambda i: (0, 0))],
-        out_specs=[row, row],
-        out_shape=[shape((n_tok, width), BF16)] * 2,
-        cost_estimate=pl.CostEstimate(
-            flops=20 * n_tok * width, bytes_accessed=16 * n_tok * width, transcendentals=0
-        ),
-        name="finish",
-    )(tok, dy, out_own, out_in, h_own, h_in, vec)
+    )(*hids, *gls, *ups, *downs, o_all, gqs_all, wo, wqs, vec, *last)
+
+
+def first_sum(sc, sets, rows, table, planes):
+    lanes = sets[0][0].shape[1]
+    n = sets[0][0].shape[0] - rows - table
+    total = 2 * rows + n + table
+    high = total // planes
+    half = high // 2
+
+    def kern(sc_ref, *refs):
+        mine, away, tmp = refs[-3:]
+        f = lambda ref, at, m: ref[at : at + m, :].astype(F32)
+        for i in range(len(sets)):
+            k_r, r1, r2, r3 = refs[4 * i : 4 * i + 4]
+            tmp[:rows, :] = f(k_r, 0, rows) + f(r2, 0, rows)
+            tmp[rows : 2 * rows, :] = f(r1, 0, rows) + f(r3, 0, rows)
+            tmp[2 * rows : 2 * rows + n, :] = f(k_r, rows, n) + f(r2, rows, n)
+            if table:
+                near = f(k_r, rows + n, table) + f(r1, rows, table)
+                tmp[2 * rows + n :, :] = near + (f(r2, rows + n, table) + f(r3, rows, table))
+            for out, flip in ((mine, 0), (away, 1)):
+                b = jnp.bitwise_xor(sc_ref[1], flip)
+                for p in range(planes):
+                    at = pl.multiple_of(p * high + b * half, 8)
+                    out[i * planes + p] = tmp[pl.ds(at, half), :].astype(BF16)
+
+    flat = [v for keep, got in sets for v in (keep, *got)]
+    return pl.pallas_call(
+        kern,
+        in_specs=[SMEM] + [VM] * len(flat),
+        out_specs=[VM, VM],
+        out_shape=[shape((planes * len(sets), half, lanes), BF16)] * 2,
+        scratch_shapes=[pltpu.VMEM((total, lanes), F32)],
+        cost_estimate=pl.CostEstimate(flops=2 * total * lanes, bytes_accessed=8 * total * lanes, transcendentals=0),
+        name="first_sum",
+    )(sc, *flat)
 
 
 def piece_row(sc_ref, n, h):
@@ -720,83 +749,135 @@
     return pl.multiple_of(b0 * (h // 2) + b1 * (h // 4), 8)
 
 
-def mlp_grads(sc, pieces, width, ff):
-    prow, wid2 = pieces[0][0].shape[1:]
+def early_grads(sc, pieces, width, ff, count):
+    prow, wid2 = pieces[0].shape[1:]
     wid = wid2 // 2
     chunk = ff // 4
-    shard_rows = width // 4
-    flat = [p for ps in pieces for p in ps]
-    n_p = len(pieces[0])
+    part = width // 4
+    n_p = len(pieces)
 
     def kern(sc_ref, *refs):
+        ins = refs[:n_p]
         up, down, tmp = refs[-3:]
         s = sc_ref[0]
-        for w in range(WAVES):
+        for w in range(count):
             for n in range(n_p):
-                ref = refs[w * n_p + n]
-                at = piece_row(sc_ref, n, shard_rows)
+                at = piece_row(sc_ref, n, part)
                 for p in range(4):
                     for h in range(2):
-                        v = ref[p, :, h * wid : (h + 1) * wid].astype(F32)
+                        v = ins[n][4 * w + p, :, h * wid : (h + 1) * wid].astype(F32)
                         if p < 2:
                             t = jnp.bitwise_xor(s, p + 2 * h)
                             lanes = pl.multiple_of(t * chunk + w * wid, 256)
                             up[pl.ds(at, prow), pl.ds(lanes, wid)] = v
                         else:
-                            tmp[pl.ds((2 * h + p - 2) * shard_rows + at, prow), :] = v
+                            tmp[pl.ds((2 * h + p - 2) * part + at, prow), :] = v
             down[w * wid : (w + 1) * wid, :] = tmp[...].T
 
     return pl.pallas_call(
         kern,
-        in_specs=[SMEM] + [VM] * len(flat),
+        in_specs=[SMEM] + [VM] * n_p,
         out_specs=[VM, VM],
-        out_shape=[shape((shard_rows, ff), F32), shape((chunk, width), F32)],
+        out_shape=[shape((part, ff), F32), shape((chunk, width), F32)],
         scratch_shapes=[pltpu.VMEM((width, wid), F32)],
-        cost_estimate=pl.CostEstimate(flops=0, bytes_accessed=12 * shard_rows * ff, transcendentals=0),
-        name="mlp_grads",
-    )(sc, *flat)
+        cost_estimate=pl.CostEstimate(flops=0, bytes_accessed=12 * part * ff, transcendentals=0),
+        name="early_grads",
+    )(sc, *pieces)
+
+
+def late_grads(sc, pieces, width, ff, shared_w, prev):
+    n_p = len(pieces)
+    planes, prow, wid2 = pieces[0].shape
+    wid = wid2 // 2
+    chunk = ff // 4
+    part = width // 4
+    half = width // 2
+    high = prow * n_p
+    wave = WAVES - 1
+
+    def kern(sc_ref, *refs):
+        ins = refs[:n_p]
+        up, down = refs[n_p + len(prev) : n_p + len(prev) + 2]
+        lines = refs[n_p + len(prev) + 2 : -1]
+        full = refs[-1]
+        s = sc_ref[0]
+        i = pl.program_id(0)
+
+        @pl.when(i == 0)
+        def _():
+            for n in range(n_p):
+                at = piece_row(sc_ref, n, high)
+                for p in range(planes):
+                    full[pl.ds(p * high + at, prow), :] = ins[n][p].astype(F32)
+            d = 2 * part
+            down[...] = jnp.concatenate([full[d : d + half, :wid], full[d : d + half, wid:]], axis=0).T
+            at = d + half
+            tab = jnp.concatenate([full[at : at + 16, :], full[at + 16 : at + 32, : width - wid2]], axis=1)
+            left = pltpu.roll(tab, (width - s * part) % width, 1)
+            for out, k in zip(lines, (0, 1, 2, 3, 4, 5, 4)):
+                out[...] = left[k : k + 1, :part].reshape(part)
+            few = shared_w // 4
+            lines[7][...] = pltpu.roll(tab, (width - s * few) % width, 1)[6:7, :few].reshape(few)
+            row = jnp.concatenate(
+                [full[pl.ds(at + 8 + s, 1), :], full[pl.ds(at + 24 + s, 1), :][:, : width - wid2]], axis=1
+            )
+            lines[8][...] = row.reshape(width)
+
+        for k in range(4):
+
+            @pl.when(i == k)
+            def _(k=k):
+                r0, h = (k & 1) * part, (k >> 1) * wid
+                up[...] = full[r0 : r0 + part, h : h + wid]
+
+    line_shapes = [(part,)] * 7 + [(shared_w // 4,), (width,)]
+    spec = pltpu.PrefetchScalarGridSpec(
+        num_scalar_prefetch=1,
+        grid=(4,),
+        in_specs=[pl.BlockSpec(p.shape, lambda i, sc: (0, 0, 0)) for p in pieces] + [ANY] * len(prev),
+        out_specs=[
+            pl.BlockSpec((part, wid), lambda i, sc: (0, jnp.bitwise_xor(sc[0], i) * WAVES + wave)),
+            pl.BlockSpec((wid, width), lambda i, sc: (wave, 0)),
+        ]
+        + [pl.BlockSpec(d, lambda i, sc: (0,)) for d in line_shapes],
+        scratch_shapes=[pltpu.VMEM((planes * high, wid2), F32)],
+    )
+    return pl.pallas_call(
+        kern,
+        grid_spec=spec,
+        out_shape=[shape((part, ff), F32), shape((chunk, width), F32)] + [shape(d, F32) for d in line_shapes],
+        input_output_aliases={1 + n_p + i: i for i in range(len(prev))},
+        cost_estimate=pl.CostEstimate(flops=0, bytes_accessed=4 * part * ff, transcendentals=0),
+        name="late_grads",
+    )(sc, *pieces, *prev)
 
 
 def attn_grads(sc, pieces, width, shared_w):
     n_p = len(pieces)
-    _, prow, wq = pieces[0].shape
+    planes, prow, wq = pieces[0].shape
     part = width // 4
     wh = wq - shared_w
+    high = prow * n_p
 
     def kern(sc_ref, *refs):
-        full = refs[-1]
         ins = refs[:n_p]
-        gq, gs, go = refs[n_p : n_p + 3]
-        lines = refs[n_p + 3 : -1]
-        s = sc_ref[0]
-        c = jnp.bitwise_and(s, 1)
+        gq, gs, go, full = refs[n_p:]
+        c = jnp.bitwise_and(sc_ref[0], 1)
         for n in range(n_p):
-            at = piece_row(sc_ref, n, part // 2)
-            for p in range(8):
-                full[pl.ds(p * (part // 2) + at, prow), :] = ins[n][p].astype(F32)
+            at = piece_row(sc_ref, n, high)
+            for p in range(planes):
+                full[pl.ds(p * high + at, prow), :] = ins[n][p].astype(F32)
         gq[...] = head_spread(full[:part, :wh], c, width) + head_spread(full[part : 2 * part, :wh], 1 - c, width)
-        gs[...] = full[:part, wh:]
+        gs[...] = full[:part, wh:] + full[part : 2 * part, wh:]
         go[...] = unfold(full, 2 * part, part, wq)
-        at = 2 * part + part * 3 // 2
-        tab = jnp.concatenate([full[at : at + 16, :], full[at + 16 : at + 32, : width - wq]], axis=1)
-        left = pltpu.roll(tab, (width - s * part) % width, 1)
-        for out, i in zip(lines, (0, 1, 2, 3, 4, 5)):
-            out[...] = left[i : i + 1, :part]
-        few = shared_w // 4
-        lines[6][...] = pltpu.roll(tab, (width - s * few) % width, 1)[6:7, :few]
-        full[0:16, :] = tab[:, :wq]
-        full[16:32, : width - wq] = tab[:, wq:]
-        lines[7][:, :wq] = full[pl.ds(8 + s, 1), :]
-        lines[7][:, wq:] = full[pl.ds(24 + s, 1), : width - wq]
 
     return pl.pallas_call(
         kern,
         in_specs=[SMEM] + [VM] * n_p,
-        out_specs=[VM] * 11,
-        out_shape=[shape((part, width), F32), shape((part, shared_w), F32), shape((part, width), F32)]
-        + [shape((1, part), F32)] * 6
-        + [shape((1, shared_w // 4), F32), shape((1, width), F32)],
-        scratch_shapes=[pltpu.VMEM((width, wq), F32)],
+        out_specs=[VM] * 3,
+        out_shape=[shape((part, width), F32), shape((part, shared_w), F32), shape((part, width), F32)],
+        scratch_shapes=[pltpu.VMEM((planes * high, wq), F32)],
+        cost_estimate=pl.CostEstimate(flops=0, bytes_accessed=12 * part * width, transcendentals=0),
         name="attn_grads",
     )(sc, *pieces)
 
@@ -817,32 +898,26 @@
     return lax.optimization_barrier((value,) + others)[0]
 
 
-def send_y(value):
-    return to_shard(value, 2)
-
-
-def reduce_chain(keep, got, count, rank, mix, join):
-    def halve(mine, other, k):
-        h = mine.shape[1] // 2
-        b = (rank // k) & 1
-
-        def cut(which):
-            f = lambda v: lax.dynamic_slice_in_dim(v, which * h, h, axis=1)
-            return both_add(f(mine), f(other))
-
-        half, away = cut(b), cut(1 - b)
-        return half, to_replica(away, k, count)
-
-    half, got = halve(keep, got, 1)
-    half, got = halve(half, got, 2)
-    half = both_add(half, got)
+def send_terms(to1, to2, to3):
+    return [to_shard(v, k) for v, k in ((to1, 1), (to2, 2), (to3, 3))]
+
+
+def reduce_chain(half, away, count, rank):
+    got = to_replica(away, 1, count)
+    h = half.shape[1] // 2
+    b = (rank >> 1) & 1
+
+    def cut(which):
+        f = lambda v: lax.dynamic_slice_in_dim(v, which * h, h, axis=1)
+        return both_add(f(half), f(got))
+
+    quarter, away = cut(b), cut(1 - b)
+    quarter = both_add(quarter, to_replica(away, 2, count))
     k = 4
     while k < count:
-        half = both_add(half, to_replica(half, k, count))
+        quarter = both_add(quarter, to_replica(quarter, k, count))
         k *= 2
-    sent, kept = mix(half)
-    half = join(kept, to_shard(sent, 1))
-    return [half] + [to_replica(half, k, count) for k in (1, 2, 3)]
+    return [quarter] + [to_replica(quarter, k, count) for k in (1, 2, 3)]
 
 
 def shards(
@@ -856,7 +931,6 @@
     sw = shared_weight.shape[1]
     s = lax.axis_index("shard")
     r = lax.axis_index("replica")
-    c = s & 1
     sc = jnp.stack([s, r & 1, (r >> 1) & 1]).astype(jnp.int32)
 
     small = pack_small(
@@ -877,7 +951,7 @@
 
     prev, ob, vec = norm_pair(0, tokens, result_grad, near, [])
     prev, _, _ = norm_pair(1, tok_in, dy_in, near, prev)
-    nm, nmt, na, nat, dy, dyt = prev
+    nm, na, dy = prev
     own1, own2, ownq, y1, y2, ya = pack_rest(
         sc, up_weight, down_weight, query_weight, shared_weight, output_weight, after(core_got, vec)
     )
@@ -890,76 +964,53 @@
 
     rows = part
 
-    def mix_mlp(v):
-        mine = jnp.where(c == 0, v[0], v[1])
-        theirs = jnp.where(c == 0, v[1], v[0])
-        return theirs, (mine, v[2:])
-
-    def join_mlp(kept, got):
-        return jnp.concatenate([kept[0][None], got[None], kept[1]], axis=0)
-
-    wh = width // 2
-
-    def mix_attn(v):
-        mine = jnp.where(c == 0, v[:2], v[2:4])
-        theirs = jnp.where(c == 0, v[2:4], v[:2])
-        return jnp.concatenate([theirs, v[7:]], axis=0), (mine, v[4:7], v[7:])
-
-    def join_attn(kept, got):
-        mine, outs_rows, table = kept
-        front = jnp.concatenate([mine[:, :, :wh], both_add(mine[:, :, wh:], got[:2, :, wh:])], axis=2)
-        return jnp.concatenate([front, got[:2], outs_rows, both_add(table, got[2:])], axis=0)
-
-    def wave(w, pieces, down_at, split):
-        return mlp_wave(w, sc, nm, nmt, dy, dyt, pieces, down_at, down_weight, vec, split)
+    def wave(w, pieces, down_at, table=None):
+        return mlp_wave(w, sc, nm, dy, pieces, down_at, down_weight, vec, table)
 
     m1 = to_shard(y1, 2)
-    hid0, gl0, wu0, wd0, ub0, rs0, keep0, send0 = wave(0, [(own0, 0), (k1, 0), (m2, 0), (k3, 0)], (m2, rows), False)
+    hid0, gl0, wu0, wd0, ub0, rs0, keep0, *send0 = wave(0, [(own0, 0), (k1, 0), (m2, 0), (k3, 0)], (m2, rows))
     ma = to_shard(after(ya, m1), 2)
-    hid1, gl1, wu1, wd1, ub1, rs1, keep1, send1 = wave(
-        1, [(own1, 0), (core_got, 0), (m1, 0), (m1, rows)], (m1, 2 * rows), False
+    hid1, gl1, wu1, wd1, ub1, rs1, keep1, *send1 = wave(
+        1, [(own1, 0), (core_got, 0), (m1, 0), (m1, rows)], (m1, 2 * rows)
     )
     m2b = to_shard(after(y2, ma), 2)
-    got0 = send_y(after(send0, ma))
-    got1 = send_y(after(send1, ma))
+    got0 = send_terms(*[after(v, ma) for v in send0])
+    got1 = send_terms(*[after(v, ma) for v in send1])
     o_all, gqs_all, cache, sums, wqs, wo = attention(
         sc, na, dy, (ownq, core_got, ma, output_weight), vec, angles, segs, shared_grad
     )
-    hid2, gl2, wu2, wd2, ub2, rs2, keep2, send2 = wave(
-        2, [(own2, 0), (core_got, 2 * rows), (m2b, 0), (m2b, rows)], (m2b, 2 * rows), False
+    keepa, ta1, ta2, ta3, table = attn_terms(
+        sc, na, dy, o_all, gqs_all, wqs, vec, sums, ob, (ub0, ub1), (rs0, rs1)
     )
-    keepa, senda = attn_terms(
-        sc, nat, dyt, o_all, gqs_all, wqs, vec, sums, ob, (ub0, ub1, ub2), (rs0, rs1, rs2)
+    hid2, gl2, wu2, wd2, _, _, keep2, *send2 = wave(
+        2, [(own2, 0), (core_got, 2 * rows), (m2b, 0), (m2b, rows)], (m2b, 2 * rows), table
     )
 
-    def chain(keep, got, planes, mix, join):
-        lanes = keep.shape[1]
-        return reduce_chain(keep.reshape(planes, -1, lanes), got.reshape(planes, -1, lanes), replicas, r, mix, join)
-
-    p0 = chain(keep0, got0, 4, mix_mlp, join_mlp)
-    p1 = chain(keep1, got1, 4, mix_mlp, join_mlp)
-    p2 = chain(keep2, send_y(send2), 4, mix_mlp, join_mlp)
-    pa = chain(keepa, send_y(senda), 8, mix_attn, join_attn)
+    def chain(sets, table_rows, planes):
+        return reduce_chain(*first_sum(sc, sets, part, table_rows, planes), replicas, r)
+
+    p01 = chain([(keep0, got0), (keep1, got1)], 0, 4)
+    pa = chain([(keepa, send_terms(ta1, ta2, ta3))], 0, 21)
+    p2 = chain([(keep2, send_terms(*send2))], 32, 25)
 
     hids, gls, wus, wds = (hid0, hid1, hid2), (gl0, gl1, gl2), (wu0, wu1, wu2), (wd0, wd1, wd2)
 
-    def outs(which):
-        return outputs(which, hids, gls, wus, wds, o_all, gqs_all, wo, wqs, vec)
+    def outs(which, last=()):
+        return outputs(which, hids, gls, wus, wds, o_all, gqs_all, wo, wqs, vec, last)
 
     out_p, h_p = outs(1)
     out_in = to_shard(out_p, 1)
     h_in = to_shard(h_p, 1)
-    out_o, h_o = outs(0)
-    block_output, tokens_grad = finish(tokens, result_grad, out_o, out_in, h_o, h_in, vec)
-
-    grad_up, grad_down = mlp_grads(sc, [p0, p1, p2], width, ff)
-    out = attn_grads(sc, pa, width, sw)
-    grad_q, grad_s, grad_o = out[:3]
-    fg, fs, sg, ss, ob_g, qb_g, sb_g, ub_g = [v.reshape(-1) for v in out[3:]]
+    block_output, tokens_grad = outs(0, (tokens, result_grad, out_in, h_in))
+
+    grads = early_grads(sc, p01, width, ff, WAVES - 1)
+    grad_q, grad_s, grad_o = attn_grads(sc, pa, width, sw)
+    out = late_grads(sc, p2, width, ff, sw, grads)
+    grad_up, grad_down, fg, fs, sg, ss, ob_g, qb_g, db_g, sb_g, ub_g = out
     return (
         block_output, cache, tokens_grad,
         fg, fs, grad_q, qb_g, grad_s, sb_g, grad_o, ob_g,
-        sg, ss, grad_up, ub_g, grad_down, ob_g,
+        sg, ss, grad_up, ub_g, grad_down, db_g,
     )
 
 

time: 310 us -> 302 us (0.974)
  waiting for transfers between devices: 83.8 us -> 71.5 us
  starting transfers between devices: 45.9 us -> 51.4 us
  other arithmetic: 12.8 us -> 9.24 us
    ppermute x24 -> x18, waiting for transfers between devices: 54.6 us -> 28.7 us  [to_replica(): return lax.ppermute(value, 'replica', [(r, r ^ k) for r in range(count)])]
    ppermute x23 -> x27, waiting for transfers between devices: 29.2 us -> 42.8 us  [to_shard(): return lax.ppermute(value, 'shard', [(s, s ^ k) for s in range(4)])]
    pallas_call x2, Pallas kernels: 12.5 us -> 9.26 us  [norm_pair(): pl.pallas_call(kern, grid=(2,), in_specs=[src, src] + [small] * n_near +...]
    pallas_call x7 -> x10, Pallas kernels: 65.8 us -> 68.8 us  [the longest x3 39.1 us: mlp_wave(): pl.pallas_call(kern, grid=(4,), in_specs=[SMEM, row, row] + [fixed((wid,...]
    ppermute x23 -> x27, starting transfers between devices: 18.6 us -> 21.5 us  [to_shard(): return lax.ppermute(value, 'shard', [(s, s ^ k) for s in range(4)])]
    ppermute x24 -> x18, starting transfers between devices: 27.3 us -> 29.9 us  [to_replica(): return lax.ppermute(value, 'replica', [(r, r ^ k) for r in range(count)])]
    convert_element_type x18 -> x9, other arithmetic: 8.47 us -> 6.97 us  [both_add(): return (a.astype(F32) + b.astype(F32)).astype(BF16)]
  transfers between devices with their start and end apart: 47 -> 45, of which waited for: 19 -> 12; matrix products, arithmetic and copies ran while one was open for 4% -> 3% of each run, Pallas kernels for 52% -> 53%
where the time goes in v1:
time: 302 us; the launch traced here: 301 us
  Pallas kernels  164 us (54%)
  waiting for transfers between devices  71.5 us (24%)
  starting transfers between devices  51.4 us (17%)
  other arithmetic  9.24 us (3%)
  local copies, waits for them, and re-layouts  3.65 us (1%)
    pallas_call x1, Pallas kernels, attention(): pl.pallas_call(kern, grid=(2,), in_specs=[SMEM, seq(width), seq(width), f...  49.8 us
    ppermute x27, waiting for transfers between devices, to_shard(): return lax.ppermute(value, 'shard', [(s, s ^ k) for s in range(4)])  42.8 us
    pallas_call x3, Pallas kernels, mlp_wave(): pl.pallas_call(kern, grid=(4,), in_specs=[SMEM, row, row] + [fixed((wid,...  39.1 us
    ppermute x18, starting transfers between devices, to_replica(): return lax.ppermute(value, 'replica', [(r, r ^ k) for r in range(count)])  29.9 us
    ppermute x18, waiting for transfers between devices, to_replica(): return lax.ppermute(value, 'replica', [(r, r ^ k) for r in range(count)])  28.7 us
    pallas_call x2, Pallas kernels, outputs(): pl.pallas_call(kern, grid=(4,), in_specs=[rows(wid2)] * (2 * n_w) + [fixe...  25.7 us
    ppermute x27, starting transfers between devices, to_shard(): return lax.ppermute(value, 'shard', [(s, s ^ k) for s in range(4)])  21.5 us
    pallas_call x1, Pallas kernels, attn_terms(): pl.pallas_call(kern, grid=(4,), in_specs=[SMEM, row, row, pl.BlockSpec((b...  9.7 us
  transfers between devices with their start and end apart: 45, of which 12 were waited for; matrix products, arithmetic and copies ran while one was open for 3% of the time, Pallas kernels for 53%

profile of v1, /device:TPU:0, one launch (start us, length us, event | category | flops | bytes accessed | tf_op | source)
XLA Modules:
  0.0 301.3 jit_solution(536796935471841925)
XLA Ops:
  1.9 1.6 pack_small.1.refs_0_
  3.5 2.6 pack_first.1
  6.0 2.6 pack_core.1
  9.3 2.9 collective-permute-start.3
  12.2 1.6 collective-permute-done.2.refs_1_
  13.8 2.6 collective-permute-start.4
  16.6 1.4 collective-permute-done.4.refs_3_
  18.6 4.6 %norm_pair.2 = (bf16[2048,768]{1,0:T(8,128)(2,1)}, bf16[2048,768]{1,0:T(8,128)(2,1)}, bf16[2048,768]{1,0:T(8,128)(2,1)}, f32[8,768]{1,0:T(8,128)}, f32[16,768]{1,0:T(8,128)}) custom-call(bf16[1024,768]{1,0:T(8,128)(2,1)} %refs_17_.1, bf16[1024,768]{1,0:T(8,128)(2,1)} %refs_18_.1, bf16[16,768]{1,0:T(8,128)(2,1)} %pack_small.1.refs_0_, ...), custom_call_target="tpu_custom_call" | custom-call | flops 15728640 | bytes 12582912 | tf_op jit(solution)/shard_map/norm_pair/pallas_call | solution.py:234
  23.2 1.8 collective-permute-start.6
  25.1 3.9 %pack_rest.1 = (bf16[192,512]{1,0:T(8,128)(2,1)}, bf16[192,512]{1,0:T(8,128)(2,1)}, bf16[192,512]{1,0:T(8,128)(2,1)}, bf16[768,512]{1,0:T(8,128)(2,1)}, bf16[768...) custom-call(s32[3]{0:T(128)} %pad_add_fusion.2.sc_ref, bf16[192,3072]{1,0:T(8,128)(2,1)} %w_ref.3, bf16[768,768]{1,0:T(8,128)(2,1)} %d0.5, ...), custom_call_target="tpu_custom_call" | custom-call | tf_op jit(solution)/shard_map/pack_rest/pallas_call | solution.py:196
  29.7 1.2 collective-permute-start.7
  31.5 0.7 pad_maximum_fusion.cs_r
  32.2 4.6 %norm_pair.3 = (bf16[2048,768]{1,0:T(8,128)(2,1)}, bf16[2048,768]{1,0:T(8,128)(2,1)}, bf16[2048,768]{1,0:T(8,128)(2,1)}, f32[8,768]{1,0:T(8,128)}, f32[16,768]{1,0:T(8,128)}) custom-call(bf16[1024,768]{1,0:T(8,128)(2,1)} %copy-done.1, bf16[1024,768]{1,0:T(8,128)(2,1)} %collective-permute-done.1.dy_ref, ...), custom_call_target="tpu_custom_call", output_to_operand_aliasing={{0}: (6, {}), {1}: (7, {}), {2}: (8, {})} | custom-call | flops 15728640 | bytes 12582912 | tf_op jit(solution)/shard_map/norm_pair/pallas_call | solution.py:234
  36.8 19.9 %collective-permute-done.9.refs_2_ = bf16[768,512]{1,0:T(8,128)(2,1)} collective-permute-done((bf16[768,512]{1,0:T(8,128)(2,1)}, bf16[768,512]{1,0:T(8,128)(2,1)}, u32[]{:S(2)}, u32[]{:S(2)}) %collective-permute-start.9) | collective-permute-done | bytes 786464 | tf_op jit(solution)/shard_map/ppermute | solution.py:886
  56.7 1.8 collective-permute-start.10
  58.4 1.6 collective-permute-done.7.refs_3_
  60.1 12.7 %mlp_wave.3 = (bf16[2048,512]{1,0:T(8,128)(2,1)}, bf16[2048,512]{1,0:T(8,128)(2,1)}, bf16[768,512]{1,0:T(8,128)(2,1)}, bf16[512,768]{1,0:T(8,128)(2,1)}, f32[8,5...) custom-call(s32[3]{0:T(128)} %pad_add_fusion.2.sc_ref, ...), custom_call_target="tpu_custom_call" | custom-call | flops 6442450944 | bytes 15728640 | tf_op jit(solution)/shard_map/mlp_wave/pallas_call | solution.py:358
  72.8 13.0 %mlp_wave.4 = (bf16[2048,512]{1,0:T(8,128)(2,1)}, bf16[2048,512]{1,0:T(8,128)(2,1)}, bf16[768,512]{1,0:T(8,128)(2,1)}, bf16[512,768]{1,0:T(8,128)(2,1)}, f32[8,5...) custom-call(s32[3]{0:T(128)} %pad_add_fusion.2.sc_ref, ...), custom_call_target="tpu_custom_call" | custom-call | flops 6442450944 | bytes 15728640 | tf_op jit(solution)/shard_map/mlp_wave/pallas_call | solution.py:358
  85.8 1.5 collective-permute-start.11
  88.4 1.0 collective-permute-start.26
  89.4 0.8 collective-permute-start.27
  90.2 49.8 %attention.1 = (bf16[2048,384]{1,0:T(8,128)(2,1)}, bf16[2048,512]{1,0:T(8,128)(2,1)}, bf16[1024,128]{1,0:T(8,128)(2,1)}, f32[8,512]{1,0:T(8,128)}, bf16[768,512]{1,0:T(8,128)(2,1)}, /*index=5*/bf16[384,768]{1,0:T(8,128)(2,1)}) custom-call(s32[3]{0:T(128)} %pad_add_fusion.2.sc_ref, bf16[2048,768]{1,0:T(8,128)(2,1)} %get-tuple-element.133.na_r, ...), custom_call_target="tpu_custom_call" | custom-call | flops 12482248704 | bytes 9437184 | tf_op jit(solution)/shard_map/attention/pallas_call | solution.py:547
  140.4 9.7 %attn_terms.1 = (bf16[480,512]{1,0:T(8,128)(2,1)}, bf16[192,512]{1,0:T(8,128)(2,1)}, bf16[480,512]{1,0:T(8,128)(2,1)}, bf16[192,512]{1,0:T(8,128)(2,1)}, f32[16,768]{1,0:T(8,128)}) custom-call(s32[3]{0:T(128)} %pad_add_fusion.2.sc_ref, bf16[2048,768]{1,0:T(8,128)(2,1)} %get-tuple-element.133.na_r, bf16[2048,768]{1,0:T(8,128)(2,1)} %get-tuple-element.115.dy_r, ...), custom_call_target="tpu_custom_call" | custom-call | flops 2818572288 | bytes 6291456 | tf_op jit(solution)/shard_map/attn_terms/pallas_call | solution.py:638
  150.1 1.7 collective-permute-start.37
  151.9 17.3 %collective-permute-done.29.refs_7_ = bf16[192,512]{1,0:T(8,128)(2,1)S(1)} collective-permute-done((bf16[192,512]{1,0:T(8,128)(2,1)S(1)}, bf16[192,512]{1,0:T(8,128)(2,1)S(1)}, u32[]{:S(2)}, u32[]{:S(2)}) %collective-permute-start.29) | collective-permute-done | bytes 196640 | tf_op jit(solution)/shard_map/ppermute | solution.py:886
  169.3 0.8 collective-permute-start.36
  170.2 0.7 copy-done.8
  171.1 3.7 %first_sum.4 = (bf16[8,96,512]{2,1,0:T(8,128)(2,1)}, bf16[8,96,512]{2,1,0:T(8,128)(2,1)}) custom-call(s32[3]{0:T(128)} %pad_add_fusion.2.sc_ref, bf16[576,512]{1,0:T(8,128)(2,1)} %get-tuple-element.167.refs_0_, bf16[192,512]{1,0:T(8,128)(2,1)} %copy-done.19, bf16[576,512]{1,0:T(8,128)(2,1)} %copy-done.8, bf16[192,512]{1,0:T(8,128)(2,1)} %copy-done.20, ...), custom_call_target="tpu_custom_call" | custom-call | flops 786432 | bytes 3145728 | tf_op jit(solution)/shard_map/first_sum/pallas_call | solution.py:736
  174.7 1.5 collective-permute-start.30
  176.3 0.9 collective-permute-done.38.refs_3_
  177.2 0.7 copy-done.18
  178.1 2.4 first_sum.5
  180.5 1.5 collective-permute-start.39
  182.0 13.3 %mlp_wave.5 = (bf16[2048,512]{1,0:T(8,128)(2,1)}, bf16[2048,512]{1,0:T(8,128)(2,1)}, bf16[768,512]{1,0:T(8,128)(2,1)}, bf16[512,768]{1,0:T(8,128)(2,1)}, f32[8,5...) custom-call(s32[3]{0:T(128)} %pad_add_fusion.2.sc_ref, ...), custom_call_target="tpu_custom_call" | custom-call | flops 6442450944 | bytes 15728640 | tf_op jit(solution)/shard_map/mlp_wave/pallas_call | solution.py:358
  196.0 1.3 collective-permute-start.17
  197.3 4.8 %collective-permute-done.39 = bf16[21,16,512]{2,1,0:T(8,128)(2,1)S(1)} collective-permute-done((bf16[21,16,512]{2,1,0:T(8,128)(2,1)}, bf16[21,16,512]{2,1,0:T(8,128)(2,1)S(1)}, u32[]{:S(2)}, u32[]{:S(2)}) %collective-permute-start.39) | collective-permute-done | bytes 344096 | tf_op jit(solution)/shard_map/ppermute | solution.py:890
  202.1 0.8 add_convert_fusion.10
  202.9 1.7 collective-permute-start.40
  204.7 1.0 add_convert_fusion.2
  205.9 12.0 %outputs.2 = (bf16[1024,768]{1,0:T(8,128)(2,1)}, bf16[1024,768]{1,0:T(8,128)(2,1)}) custom-call(bf16[2048,512]{1,0:T(8,128)(2,1)} %get-tuple-element.122.refs_0_, bf16[2048,512]{1,0:T(8,128)(2,1)} %get-tuple-element.127.refs_1_, bf16[2048,512]{1,0:T(8,128)(2,1)} %get-tuple-element.145.refs_2_, bf16[2048,512]{1,0:T(8,128)(2,1)} %get-tuple-element.146.refs_3_, ...), custom_call_target="tpu_custom_call" | custom-call | flops 6247415808 | bytes 18874368 | tf_op jit(solution)/shard_map/outputs/pallas_call | solution.py:694
  218.6 0.7 copy-done.15
  219.3 2.6 first_sum.3
  222.0 1.6 collective-permute-start.18
  223.6 1.1 add_convert_fusion.9
  224.7 2.7 collective-permute-start.41
  227.5 1.3 add_convert_fusion.1
  229.1 5.0 %collective-permute-done.18 = bf16[25,16,512]{2,1,0:T(8,128)(2,1)S(1)} collective-permute-done((bf16[25,16,512]{2,1,0:T(8,128)(2,1)}, bf16[25,16,512]{2,1,0:T(8,128)(2,1)S(1)}, u32[]{:S(2)}, u32[]{:S(2)}) %collective-permute-start.18) | collective-permute-done | bytes 409632 | tf_op jit(solution)/shard_map/ppermute | solution.py:890
  234.2 1.8 collective-permute-start.19
  236.0 9.1 %collective-permute-done.41 = bf16[21,8,512]{2,1,0:T(8,128)(2,1)S(1)} collective-permute-done((bf16[21,8,512]{2,1,0:T(8,128)(2,1)S(1)}, bf16[21,8,512]{2,1,0:T(8,128)(2,1)S(1)}, u32[]{:S(2)}, u32[]{:S(2)}) %collective-permute-start.41) | collective-permute-done | bytes 172064 | tf_op jit(solution)/shard_map/ppermute | solution.py:890
  245.7 1.1 collective-permute-start.43
  246.8 0.8 add_convert_fusion.5
  247.6 3.0 collective-permute-done.42.refs_1_
  250.6 5.1 %collective-permute-start.44 = (bf16[21,8,512]{2,1,0:T(8,128)(2,1)S(1)}, bf16[21,8,512]{2,1,0:T(8,128)(2,1)}, u32[]{:S(2)}, u32[]{:S(2)}) collective-permute-start(bf16[21,8,512]{2,1,0:T(8,128)(2,1)S(1)} %add_convert_fusion.8.refs_0_), channel_id=1, source_target_pairs={{0,12},{4,8},{8,4},{12,0},{16,28},{20,24},{24,20},{28,16},{1,13},{... | collective-permute-start | bytes 516104 | tf_op jit(solution)/shard_map/ppermute | solution.py:890
  255.7 4.4 %collective-permute-start.20 = (bf16[25,8,512]{2,1,0:T(8,128)(2,1)}, bf16[25,8,512]{2,1,0:T(8,128)(2,1)}, u32[]{:S(2)}, u32[]{:S(2)}) collective-permute-start(bf16[25,8,512]{2,1,0:T(8,128)(2,1)} %add_convert_fusion.5), channel_id=1, source_target_pairs={{0,16},{4,20},{8,24},{12,28},{16,0},{20,4},{24,8},{28,12},{1,17},{... | collective-permute-start | bytes 614408 | tf_op jit(solution)/shard_map/ppermute | solution.py:890
  260.2 0.9 collective-permute-start.33
  261.2 3.7 %collective-permute-done.44.refs_3_ = bf16[21,8,512]{2,1,0:T(8,128)(2,1)} collective-permute-done((bf16[21,8,512]{2,1,0:T(8,128)(2,1)S(1)}, bf16[21,8,512]{2,1,0:T(8,128)(2,1)}, u32[]{:S(2)}, u32[]{:S(2)}) %collective-permute-start.44) | collective-permute-done | bytes 172064 | tf_op jit(solution)/shard_map/ppermute | solution.py:890
  264.8 3.1 %attn_grads.1 = (f32[192,768]{1,0:T(8,128)}, f32[192,128]{1,0:T(8,128)}, f32[192,768]{1,0:T(8,128)}) custom-call(s32[3]{0:T(128)} %pad_add_fusion.2.sc_ref, bf16[21,8,512]{2,1,0:T(8,128)(2,1)} %copy-done.7, bf16[21,8,512]{2,1,0:T(8,128)(2,1)} %copy-done.23, bf16[21,8,512]{2,1,0:T(8,128)(2,1)} %copy-done.24, bf16[21,8,512]{2,1,0:T(8,128)(2,1)} %collective-permute-done.44.refs_3_), custom_call_target="tpu_custom_call" | custom-call | bytes 1769472 | tf_op jit(solution)/shard_map/attn_grads/pallas_call | solution.py:874
  267.9 2.9 collective-permute-start.35
  270.8 1.8 add_convert_fusion.4.refs_0_
  273.2 2.8 collective-permute-start.23
  276.0 13.7 %outputs.3 = (bf16[1024,768]{1,0:T(8,128)(2,1)}, bf16[1024,768]{1,0:T(8,128)(2,1)}) custom-call(bf16[2048,512]{1,0:T(8,128)(2,1)} %get-tuple-element.122.refs_0_, bf16[2048,512]{1,0:T(8,128)(2,1)} %get-tuple-element.127.refs_1_, bf16[2048,512]{1,0:T(8,128)(2,1)} %get-tuple-element.145.refs_2_, bf16[2048,512]{1,0:T(8,128)(2,1)} %get-tuple-element.146.refs_3_, ...), custom_call_target="tpu_custom_call" | custom-call | flops 6247415808 | bytes 18874368 | tf_op jit(solution)/shard_map/outputs/pallas_call | solution.py:694
  289.8 4.1 %early_grads.1 = (f32[192,3072]{1,0:T(8,128)}, f32[768,768]{1,0:T(8,128)}) custom-call(s32[3]{0:T(128)} %pad_add_fusion.2.sc_ref, bf16[8,48,512]{2,1,0:T(8,128)(2,1)} %copy-done.2, bf16[8,48,512]{2,1,0:T(8,128)(2,1)} %collective-permute-done.33.refs_1_, bf16[8,48,512]{2,1,0:T(8,128)(2,1)} %collective-permute-done.34.refs_2_, ...), custom_call_target="tpu_custom_call" | custom-call | bytes 7077888 | tf_op jit(solution)/shard_map/early_grads/pallas_call | solution.py:777
  293.9 3.1 %collective-permute-done.23.refs_3_ = bf16[25,8,512]{2,1,0:T(8,128)(2,1)} collective-permute-done((bf16[25,8,512]{2,1,0:T(8,128)(2,1)}, bf16[25,8,512]{2,1,0:T(8,128)(2,1)}, u32[]{:S(2)}, u32[]{:S(2)}) %collective-permute-start.23) | collective-permute-done | bytes 204832 | tf_op jit(solution)/shard_map/ppermute | solution.py:890
  297.0 4.1 %late_grads.1 = (f32[192,3072]{1,0:T(8,128)}, f32[768,768]{1,0:T(8,128)}, f32[192]{0:T(256)}, f32[192]{0:T(256)}, f32[192]{0:T(256)}, /*index=5*/f32[192]{0:T(25...) custom-call(s32[3]{0:T(128)} %pad_add_fusion.2.sc_ref, ...), custom_call_target="tpu_custom_call", output_to_operand_aliasing={{0}: (5, {}), {1}: (6, {})} | custom-call | bytes 2359296 | tf_op jit(solution)/shard_map/late_grads/pallas_call | solution.py:845
  (132 shorter events, 9.3 us)
Async XLA Ops:
  0.7 29.0 %collective-permute-start = (bf16[1024,768]{1,0:T(8,128)(2,1)}, bf16[1024,768]{1,0:T(8,128)(2,1)S(1)}, u32[]{:S(2)}, u32[]{:S(2)}) collective-permute-start(bf16[1024,768]{1,0:T(8,128)(2,1)} %refs_17_.1), channel_id=1, source_target_pairs={{0,1},{1,0},{2,3},{3,2},{4,5},{5,4},{6,7},{7,6},{8,9},{9,8},{10,11... | collective-permute-start | bytes 4718600 | tf_op jit(solution)/shard_map/ppermute | solution.py:886
  3.5 5.2 %copy-start = (bf16[1024,768]{1,0:T(8,128)(2,1)S(1)}, bf16[1024,768]{1,0:T(8,128)(2,1)}, u32[]{:S(2)}) copy-start(bf16[1024,768]{1,0:T(8,128)(2,1)} %refs_18_.1) | copy-start | bytes 4718596
  3.5 5.7 %copy-start.16 = (bf16[16,768]{1,0:T(8,128)(2,1)S(1)}, bf16[16,768]{1,0:T(8,128)(2,1)}, u32[]{:S(2)}) copy-start(bf16[16,768]{1,0:T(8,128)(2,1)} %pack_small.1.refs_0_) | copy-start | bytes 73732
  3.5 8.7 %copy-start.28 = (s32[1,1024]{1,0:T(1,128)S(1)}, s32[1,1024]{1,0:T(1,128)}, u32[]{:S(2)}) copy-start(s32[1,1024]{1,0:T(1,128)} %param.21) | copy-start | bytes 12292
  3.5 8.7 %copy-start.29 = (s32[1,1024]{1,0:T(1,128)S(1)}, s32[1,1024]{1,0:T(1,128)}, u32[]{:S(2)}) copy-start(s32[1,1024]{1,0:T(1,128)} %param.20) | copy-start | bytes 12292
  8.7 14.5 %collective-permute-start.8 = (bf16[960,512]{1,0:T(8,128)(2,1)}, bf16[960,512]{1,0:T(8,128)(2,1)}, u32[]{:S(2)}, u32[]{:S(2)}) collective-permute-start(bf16[960,512]{1,0:T(8,128)(2,1)} %pack_core.1), channel_id=1, source_target_pairs={{0,1},{1,0},{2,3},{3,2},{4,5},{5,4},{6,7},{7,6},{8,9},{9,8},{10,11... | collective-permute-start | bytes 2949128 | tf_op jit(solution)/shard_map/ppermute | solution.py:886
  8.7 23.4 %collective-permute-start.1 = (bf16[1024,768]{1,0:T(8,128)(2,1)S(1)}, bf16[1024,768]{1,0:T(8,128)(2,1)}, u32[]{:S(2)}, u32[]{:S(2)}) collective-permute-start(bf16[1024,768]{1,0:T(8,128)(2,1)S(1)} %copy-done), channel_id=1, source_target_pairs={{0,1},{1,0},{2,3},{3,2},{4,5},{5,4},{6,7},{7,6},{8,9},{9,8},{10,11... | collective-permute-start | bytes 4718600 | tf_op jit(solution)/shard_map/ppermute | solution.py:886
  9.2 4.6 %collective-permute-start.2 = (bf16[16,768]{1,0:T(8,128)(2,1)S(1)}, bf16[16,768]{1,0:T(8,128)(2,1)S(1)}, u32[]{:S(2)}, u32[]{:S(2)}) collective-permute-start(bf16[16,768]{1,0:T(8,128)(2,1)S(1)} %copy-done.16), channel_id=1, source_target_pairs={{0,1},{1,0},{2,3},{3,2},{4,5},{5,4},{6,7},{7,6},{8,9},{9,8},{10,11... | collective-permute-start | bytes 73736 | tf_op jit(solution)/shard_map/ppermute | solution.py:886
  9.3 7.2 %collective-permute-start.3 = (bf16[16,768]{1,0:T(8,128)(2,1)S(1)}, bf16[16,768]{1,0:T(8,128)(2,1)S(1)}, u32[]{:S(2)}, u32[]{:S(2)}) collective-permute-start(bf16[16,768]{1,0:T(8,128)(2,1)S(1)} %copy-done.16), channel_id=1, source_target_pairs={{0,2},{1,3},{2,0},{3,1},{4,6},{5,7},{6,4},{7,5},{8,10},{9,11},{10,... | collective-permute-start | bytes 73736 | tf_op jit(solution)/shard_map/ppermute | solution.py:886
  13.8 4.1 %collective-permute-start.4 = (bf16[16,768]{1,0:T(8,128)(2,1)S(1)}, bf16[16,768]{1,0:T(8,128)(2,1)S(1)}, u32[]{:S(2)}, u32[]{:S(2)}) collective-permute-start(bf16[16,768]{1,0:T(8,128)(2,1)S(1)} %copy-done.16), channel_id=1, source_target_pairs={{0,3},{1,2},{2,1},{3,0},{4,7},{5,6},{6,5},{7,4},{8,11},{9,10},{10,... | collective-permute-start | bytes 73736 | tf_op jit(solution)/shard_map/ppermute | solution.py:886
  16.5 12.5 %collective-permute-start.12 = (s32[2,1024]{1,0:T(2,128)S(1)}, s32[2,1024]{1,0:T(2,128)S(1)}, u32[]{:S(2)}, u32[]{:S(2)}) collective-permute-start(s32[2,1024]{1,0:T(2,128)S(1)} %pad_add_fusion), channel_id=1, source_target_pairs={{0,1},{1,0},{2,3},{3,2},{4,5},{5,4},{6,7},{7,6},{8,9},{9,8},{10,11... | collective-permute-start | bytes 24584 | tf_op jit(solution)/shard_map/ppermute | solution.py:886
  18.0 40.4 %collective-permute-start.5 = (bf16[192,512]{1,0:T(8,128)(2,1)}, bf16[192,512]{1,0:T(8,128)(2,1)}, u32[]{:S(2)}, u32[]{:S(2)}) collective-permute-start(bf16[192,512]{1,0:T(8,128)(2,1)} %get-tuple-element.119), channel_id=1, source_target_pairs={{0,1},{1,0},{2,3},{3,2},{4,5},{5,4},{6,7},{7,6},{8,9},{9,8},{10,11... | collective-permute-start | bytes 589832 | tf_op jit(solution)/shard_map/ppermute | solution.py:886
  23.2 6.4 %copy-start.33 = (bf16[192,512]{1,0:T(8,128)(2,1)S(1)}, bf16[192,512]{1,0:T(8,128)(2,1)}, u32[]{:S(2)}) copy-start(bf16[192,512]{1,0:T(8,128)(2,1)} %get-tuple-element.121) | copy-start | bytes 589828
  23.2 36.8 %collective-permute-start.6 = (bf16[576,512]{1,0:T(8,128)(2,1)}, bf16[576,512]{1,0:T(8,128)(2,1)}, u32[]{:S(2)}, u32[]{:S(2)}) collective-permute-start(bf16[576,512]{1,0:T(8,128)(2,1)} %get-tuple-element.120), channel_id=1, source_target_pairs={{0,2},{1,3},{2,0},{3,1},{4,6},{5,7},{6,4},{7,5},{8,10},{9,11},{10,... | collective-permute-start | bytes 1769480 | tf_op jit(solution)/shard_map/ppermute | solution.py:886
  29.0 27.7 %collective-permute-start.9 = (bf16[768,512]{1,0:T(8,128)(2,1)}, bf16[768,512]{1,0:T(8,128)(2,1)}, u32[]{:S(2)}, u32[]{:S(2)}) collective-permute-start(bf16[768,512]{1,0:T(8,128)(2,1)} %get-tuple-element.126), channel_id=1, source_target_pairs={{0,2},{1,3},{2,0},{3,1},{4,6},{5,7},{6,4},{7,5},{8,10},{9,11},{10,... | collective-permute-start | bytes 2359304 | tf_op jit(solution)/shard_map/ppermute | solution.py:886
  29.7 30.4 %collective-permute-start.7 = (bf16[192,512]{1,0:T(8,128)(2,1)S(1)}, bf16[192,512]{1,0:T(8,128)(2,1)}, u32[]{:S(2)}, u32[]{:S(2)}) collective-permute-start(bf16[192,512]{1,0:T(8,128)(2,1)S(1)} %copy-done.33), channel_id=1, source_target_pairs={{0,3},{1,2},{2,1},{3,0},{4,7},{5,6},{6,5},{7,4},{8,11},{9,10},{10,... | collective-permute-start | bytes 589832 | tf_op jit(solution)/shard_map/ppermute | solution.py:886
  32.2 24.5 %copy-start.31 = (bf16[672,512]{1,0:T(8,128)(2,1)S(1)}, bf16[672,512]{1,0:T(8,128)(2,1)}, u32[]{:S(2)}) copy-start(bf16[672,512]{1,0:T(8,128)(2,1)} %get-tuple-element.131) | copy-start | bytes 2064388
  56.7 29.1 %collective-permute-start.10 = (bf16[672,512]{1,0:T(8,128)(2,1)S(1)}, bf16[672,512]{1,0:T(8,128)(2,1)S(1)}, u32[]{:S(2)}, u32[]{:S(2)}) collective-permute-start(bf16[672,512]{1,0:T(8,128)(2,1)S(1)} %copy-done.31), channel_id=1, source_target_pairs={{0,2},{1,3},{2,0},{3,1},{4,6},{5,7},{6,4},{7,5},{8,10},{9,11},{10,... | collective-permute-start | bytes 2064392 | tf_op jit(solution)/shard_map/ppermute | solution.py:886
  72.7 13.1 %copy-start.30 = (bf16[768,512]{1,0:T(8,128)(2,1)S(1)}, bf16[768,512]{1,0:T(8,128)(2,1)}, u32[]{:S(2)}) copy-start(bf16[768,512]{1,0:T(8,128)(2,1)} %get-tuple-element.132) | copy-start | bytes 2359300
  85.8 96.2 %collective-permute-start.11 = (bf16[768,512]{1,0:T(8,128)(2,1)S(1)}, bf16[768,512]{1,0:T(8,128)(2,1)}, u32[]{:S(2)}, u32[]{:S(2)}) collective-permute-start(bf16[768,512]{1,0:T(8,128)(2,1)S(1)} %copy-done.30), channel_id=1, source_target_pairs={{0,2},{1,3},{2,0},{3,1},{4,6},{5,7},{6,4},{7,5},{8,10},{9,11},{10,... | collective-permute-start | bytes 2359304 | tf_op jit(solution)/shard_map/ppermute | solution.py:886
  87.4 52.6 %collective-permute-start.24 = (bf16[192,512]{1,0:T(8,128)(2,1)}, bf16[192,512]{1,0:T(8,128)(2,1)S(1)}, u32[]{:S(2)}, u32[]{:S(2)}) collective-permute-start(bf16[192,512]{1,0:T(8,128)(2,1)} %get-tuple-element.169), channel_id=1, source_target_pairs={{0,1},{1,0},{2,3},{3,2},{4,5},{5,4},{6,7},{7,6},{8,9},{9,8},{10,11... | collective-permute-start | bytes 589832 | tf_op jit(solution)/shard_map/ppermute | solution.py:886
  88.0 82.0 %collective-permute-start.25 = (bf16[576,512]{1,0:T(8,128)(2,1)}, bf16[576,512]{1,0:T(8,128)(2,1)S(1)}, u32[]{:S(2)}, u32[]{:S(2)}) collective-permute-start(bf16[576,512]{1,0:T(8,128)(2,1)} %get-tuple-element.171), channel_id=1, source_target_pairs={{0,2},{1,3},{2,0},{3,1},{4,6},{5,7},{6,4},{7,5},{8,10},{9,11},{10,... | collective-permute-start | bytes 1769480 | tf_op jit(solution)/shard_map/ppermute | solution.py:886
  88.4 61.7 %collective-permute-start.26 = (bf16[192,512]{1,0:T(8,128)(2,1)}, bf16[192,512]{1,0:T(8,128)(2,1)S(1)}, u32[]{:S(2)}, u32[]{:S(2)}) collective-permute-start(bf16[192,512]{1,0:T(8,128)(2,1)} %get-tuple-element.173), channel_id=1, source_target_pairs={{0,3},{1,2},{2,1},{3,0},{4,7},{5,6},{6,5},{7,4},{8,11},{9,10},{10,... | collective-permute-start | bytes 589832 | tf_op jit(solution)/shard_map/ppermute | solution.py:886
  89.4 62.5 %collective-permute-start.27 = (bf16[192,512]{1,0:T(8,128)(2,1)}, bf16[192,512]{1,0:T(8,128)(2,1)S(1)}, u32[]{:S(2)}, u32[]{:S(2)}) collective-permute-start(bf16[192,512]{1,0:T(8,128)(2,1)} %get-tuple-element.176), channel_id=1, source_target_pairs={{0,1},{1,0},{2,3},{3,2},{4,5},{5,4},{6,7},{7,6},{8,9},{9,8},{10,11... | collective-permute-start | bytes 589832 | tf_op jit(solution)/shard_map/ppermute | solution.py:886
  140.0 10.1 %copy-start.19 = (bf16[192,512]{1,0:T(8,128)(2,1)}, bf16[192,512]{1,0:T(8,128)(2,1)S(1)}, u32[]{:S(2)}) copy-start(bf16[192,512]{1,0:T(8,128)(2,1)S(1)} %collective-permute-done.24.refs_1_) | copy-start | bytes 589828
  140.0 30.2 %collective-permute-start.28 = (bf16[576,512]{1,0:T(8,128)(2,1)}, bf16[576,512]{1,0:T(8,128)(2,1)S(1)}, u32[]{:S(2)}, u32[]{:S(2)}) collective-permute-start(bf16[576,512]{1,0:T(8,128)(2,1)} %get-tuple-element.178), channel_id=1, source_target_pairs={{0,2},{1,3},{2,0},{3,1},{4,6},{5,7},{6,4},{7,5},{8,10},{9,11},{10,... | collective-permute-start | bytes 1769480 | tf_op jit(solution)/shard_map/ppermute | solution.py:886
  140.4 11.5 %copy-start.34 = (bf16[192,512]{1,0:T(8,128)(2,1)S(1)}, bf16[192,512]{1,0:T(8,128)(2,1)}, u32[]{:S(2)}) copy-start(bf16[192,512]{1,0:T(8,128)(2,1)} %get-tuple-element.180) | copy-start | bytes 589828
  150.1 20.0 %copy-start.20 = (bf16[192,512]{1,0:T(8,128)(2,1)}, bf16[192,512]{1,0:T(8,128)(2,1)S(1)}, u32[]{:S(2)}) copy-start(bf16[192,512]{1,0:T(8,128)(2,1)S(1)} %collective-permute-done.26.refs_3_) | copy-start | bytes 589828
  150.1 27.1 %collective-permute-start.37 = (bf16[480,512]{1,0:T(8,128)(2,1)}, bf16[480,512]{1,0:T(8,128)(2,1)S(1)}, u32[]{:S(2)}, u32[]{:S(2)}) collective-permute-start(bf16[480,512]{1,0:T(8,128)(2,1)} %get-tuple-element.189), channel_id=1, source_target_pairs={{0,2},{1,3},{2,0},{3,1},{4,6},{5,7},{6,4},{7,5},{8,10},{9,11},{10,... | collective-permute-start | bytes 1474568 | tf_op jit(solution)/shard_map/ppermute | solution.py:886
  151.9 18.3 %copy-start.21 = (bf16[192,512]{1,0:T(8,128)(2,1)}, bf16[192,512]{1,0:T(8,128)(2,1)S(1)}, u32[]{:S(2)}) copy-start(bf16[192,512]{1,0:T(8,128)(2,1)S(1)} %collective-permute-done.27.refs_5_) | copy-start | bytes 589828
  151.9 17.4 %collective-permute-start.29 = (bf16[192,512]{1,0:T(8,128)(2,1)S(1)}, bf16[192,512]{1,0:T(8,128)(2,1)S(1)}, u32[]{:S(2)}, u32[]{:S(2)}) collective-permute-start(bf16[192,512]{1,0:T(8,128)(2,1)S(1)} %copy-done.34), channel_id=1, source_target_pairs={{0,3},{1,2},{2,1},{3,0},{4,7},{5,6},{6,5},{7,4},{8,11},{9,10},{10,... | collective-permute-start | bytes 589832 | tf_op jit(solution)/shard_map/ppermute | solution.py:886
  169.3 7.0 %collective-permute-start.36 = (bf16[192,512]{1,0:T(8,128)(2,1)}, bf16[192,512]{1,0:T(8,128)(2,1)S(1)}, u32[]{:S(2)}, u32[]{:S(2)}) collective-permute-start(bf16[192,512]{1,0:T(8,128)(2,1)} %get-tuple-element.188), channel_id=1, source_target_pairs={{0,1},{1,0},{2,3},{3,2},{4,5},{5,4},{6,7},{7,6},{8,9},{9,8},{10,11... | collective-permute-start | bytes 589832 | tf_op jit(solution)/shard_map/ppermute | solution.py:886
  170.1 7.1 %collective-permute-start.38 = (bf16[192,512]{1,0:T(8,128)(2,1)}, bf16[192,512]{1,0:T(8,128)(2,1)S(1)}, u32[]{:S(2)}, u32[]{:S(2)}) collective-permute-start(bf16[192,512]{1,0:T(8,128)(2,1)} %get-tuple-element.190), channel_id=1, source_target_pairs={{0,3},{1,2},{2,1},{3,0},{4,7},{5,6},{6,5},{7,4},{8,11},{9,10},{10,... | collective-permute-start | bytes 589832 | tf_op jit(solution)/shard_map/ppermute | solution.py:886
  174.7 29.9 %collective-permute-start.30 = (bf16[8,96,512]{2,1,0:T(8,128)(2,1)}, bf16[8,96,512]{2,1,0:T(8,128)(2,1)S(1)}, u32[]{:S(2)}, u32[]{:S(2)}) collective-permute-start(bf16[8,96,512]{2,1,0:T(8,128)(2,1)} %get-tuple-element.182), channel_id=1, source_target_pairs={{0,4},{4,0},{8,12},{12,8},{16,20},{20,16},{24,28},{28,24},{1,5},{5... | collective-permute-start | bytes 2359304 | tf_op jit(solution)/shard_map/ppermute | solution.py:890
  180.5 21.6 %collective-permute-start.39 = (bf16[21,16,512]{2,1,0:T(8,128)(2,1)}, bf16[21,16,512]{2,1,0:T(8,128)(2,1)S(1)}, u32[]{:S(2)}, u32[]{:S(2)}) collective-permute-start(bf16[21,16,512]{2,1,0:T(8,128)(2,1)} %get-tuple-element.192), channel_id=1, source_target_pairs={{0,4},{4,0},{8,12},{12,8},{16,20},{20,16},{24,28},{28,24},{1,5},{5... | collective-permute-start | bytes 1032200 | tf_op jit(solution)/shard_map/ppermute | solution.py:890
  182.0 20.1 %copy-start.12 = (bf16[21,16,512]{2,1,0:T(8,128)(2,1)S(1)}, bf16[21,16,512]{2,1,0:T(8,128)(2,1)}, u32[]{:S(2)}) copy-start(bf16[21,16,512]{2,1,0:T(8,128)(2,1)} %get-tuple-element.191) | copy-start | bytes 1032196
  182.0 22.6 %copy-start.5 = (bf16[8,96,512]{2,1,0:T(8,128)(2,1)S(1)}, bf16[8,96,512]{2,1,0:T(8,128)(2,1)}, u32[]{:S(2)}) copy-start(bf16[8,96,512]{2,1,0:T(8,128)(2,1)} %get-tuple-element.181) | copy-start | bytes 2359300
  195.4 22.6 %collective-permute-start.15 = (bf16[224,512]{1,0:T(8,128)(2,1)}, bf16[224,512]{1,0:T(8,128)(2,1)S(1)}, u32[]{:S(2)}, u32[]{:S(2)}) collective-permute-start(bf16[224,512]{1,0:T(8,128)(2,1)} %get-tuple-element.162), channel_id=1, source_target_pairs={{0,1},{1,0},{2,3},{3,2},{4,5},{5,4},{6,7},{7,6},{8,9},{9,8},{10,11... | collective-permute-start | bytes 688136 | tf_op jit(solution)/shard_map/ppermute | solution.py:886
  195.4 23.9 %collective-permute-start.16 = (bf16[608,512]{1,0:T(8,128)(2,1)}, bf16[608,512]{1,0:T(8,128)(2,1)}, u32[]{:S(2)}, u32[]{:S(2)}) collective-permute-start(bf16[608,512]{1,0:T(8,128)(2,1)} %get-tuple-element.163), channel_id=1, source_target_pairs={{0,2},{1,3},{2,0},{3,1},{4,6},{5,7},{6,4},{7,5},{8,10},{9,11},{10,... | collective-permute-start | bytes 1867784 | tf_op jit(solution)/shard_map/ppermute | solution.py:886
  196.0 22.1 %collective-permute-start.17 = (bf16[224,512]{1,0:T(8,128)(2,1)}, bf16[224,512]{1,0:T(8,128)(2,1)S(1)}, u32[]{:S(2)}, u32[]{:S(2)}) collective-permute-start(bf16[224,512]{1,0:T(8,128)(2,1)} %get-tuple-element.164), channel_id=1, source_target_pairs={{0,3},{1,2},{2,1},{3,0},{4,7},{5,6},{6,5},{7,4},{8,11},{9,10},{10,... | collective-permute-start | bytes 688136 | tf_op jit(solution)/shard_map/ppermute | solution.py:886
  202.1 15.8 %copy-start.13 = (bf16[21,16,512]{2,1,0:T(8,128)(2,1)}, bf16[21,16,512]{2,1,0:T(8,128)(2,1)S(1)}, u32[]{:S(2)}) copy-start(bf16[21,16,512]{2,1,0:T(8,128)(2,1)S(1)} %collective-permute-done.39) | copy-start | bytes 1032196
  202.9 20.7 %collective-permute-start.40 = (bf16[21,8,512]{2,1,0:T(8,128)(2,1)}, bf16[21,8,512]{2,1,0:T(8,128)(2,1)}, u32[]{:S(2)}, u32[]{:S(2)}) collective-permute-start(bf16[21,8,512]{2,1,0:T(8,128)(2,1)} %add_convert_fusion.10), channel_id=1, source_target_pairs={{0,8},{4,12},{8,0},{12,4},{16,24},{20,28},{24,16},{28,20},{1,9},{5... | collective-permute-start | bytes 516104 | tf_op jit(solution)/shard_map/ppermute | solution.py:890
  204.7 13.3 %copy-start.6 = (bf16[8,96,512]{2,1,0:T(8,128)(2,1)}, bf16[8,96,512]{2,1,0:T(8,128)(2,1)S(1)}, u32[]{:S(2)}) copy-start(bf16[8,96,512]{2,1,0:T(8,128)(2,1)S(1)} %collective-permute-done.30) | copy-start | bytes 2359300
  205.6 21.8 %collective-permute-start.31 = (bf16[8,48,512]{2,1,0:T(8,128)(2,1)}, bf16[8,48,512]{2,1,0:T(8,128)(2,1)S(1)}, u32[]{:S(2)}, u32[]{:S(2)}) collective-permute-start(bf16[8,48,512]{2,1,0:T(8,128)(2,1)} %add_convert_fusion.2), channel_id=1, source_target_pairs={{0,8},{4,12},{8,0},{12,4},{16,24},{20,28},{24,16},{28,20},{1,9},{5... | collective-permute-start | bytes 1179656 | tf_op jit(solution)/shard_map/ppermute | solution.py:890
  217.9 54.6 %collective-permute-start.13 = (bf16[1024,768]{1,0:T(8,128)(2,1)}, bf16[1024,768]{1,0:T(8,128)(2,1)S(1)}, u32[]{:S(2)}, u32[]{:S(2)}) collective-permute-start(bf16[1024,768]{1,0:T(8,128)(2,1)} %get-tuple-element.156), channel_id=1, source_target_pairs={{0,1},{1,0},{2,3},{3,2},{4,5},{5,4},{6,7},{7,6},{8,9},{9,8},{10,11... | collective-permute-start | bytes 4718600 | tf_op jit(solution)/shard_map/ppermute | solution.py:886
  219.3 53.8 %collective-permute-start.14 = (bf16[1024,768]{1,0:T(8,128)(2,1)}, bf16[1024,768]{1,0:T(8,128)(2,1)S(1)}, u32[]{:S(2)}, u32[]{:S(2)}) collective-permute-start(bf16[1024,768]{1,0:T(8,128)(2,1)} %get-tuple-element.157), channel_id=1, source_target_pairs={{0,1},{1,0},{2,3},{3,2},{4,5},{5,4},{6,7},{7,6},{8,9},{9,8},{10,11... | collective-permute-start | bytes 4718600 | tf_op jit(solution)/shard_map/ppermute | solution.py:886
  222.0 12.1 %copy-start.11 = (bf16[25,16,512]{2,1,0:T(8,128)(2,1)S(1)}, bf16[25,16,512]{2,1,0:T(8,128)(2,1)}, u32[]{:S(2)}) copy-start(bf16[25,16,512]{2,1,0:T(8,128)(2,1)} %get-tuple-element.165) | copy-start | bytes 1228804
  222.0 12.1 %collective-permute-start.18 = (bf16[25,16,512]{2,1,0:T(8,128)(2,1)}, bf16[25,16,512]{2,1,0:T(8,128)(2,1)S(1)}, u32[]{:S(2)}, u32[]{:S(2)}) collective-permute-start(bf16[25,16,512]{2,1,0:T(8,128)(2,1)} %get-tuple-element.166), channel_id=1, source_target_pairs={{0,4},{4,0},{8,12},{12,8},{16,20},{20,16},{24,28},{28,24},{1,5},{5... | collective-permute-start | bytes 1228808 | tf_op jit(solution)/shard_map/ppermute | solution.py:890
  224.7 20.3 %collective-permute-start.41 = (bf16[21,8,512]{2,1,0:T(8,128)(2,1)S(1)}, bf16[21,8,512]{2,1,0:T(8,128)(2,1)S(1)}, u32[]{:S(2)}, u32[]{:S(2)}) collective-permute-start(bf16[21,8,512]{2,1,0:T(8,128)(2,1)S(1)} %add_convert_fusion.9), channel_id=1, source_target_pairs={{0,16},{4,20},{8,24},{12,28},{16,0},{20,4},{24,8},{28,12},{1,17},{... | collective-permute-start | bytes 516104 | tf_op jit(solution)/shard_map/ppermute | solution.py:890
  228.7 27.0 %collective-permute-start.32 = (bf16[8,48,512]{2,1,0:T(8,128)(2,1)S(1)}, bf16[8,48,512]{2,1,0:T(8,128)(2,1)S(1)}, u32[]{:S(2)}, u32[]{:S(2)}) collective-permute-start(bf16[8,48,512]{2,1,0:T(8,128)(2,1)S(1)} %add_convert_fusion.1), channel_id=1, source_target_pairs={{0,16},{4,20},{8,24},{12,28},{16,0},{20,4},{24,8},{28,12},{1,17},{... | collective-permute-start | bytes 1179656 | tf_op jit(solution)/shard_map/ppermute | solution.py:890
  234.2 11.6 %collective-permute-start.19 = (bf16[25,8,512]{2,1,0:T(8,128)(2,1)S(1)}, bf16[25,8,512]{2,1,0:T(8,128)(2,1)S(1)}, u32[]{:S(2)}, u32[]{:S(2)}) collective-permute-start(bf16[25,8,512]{2,1,0:T(8,128)(2,1)S(1)} %add_convert_fusion.6), channel_id=1, source_target_pairs={{0,8},{4,12},{8,0},{12,4},{16,24},{20,28},{24,16},{28,20},{1,9},{5... | collective-permute-start | bytes 614408 | tf_op jit(solution)/shard_map/ppermute | solution.py:890
  245.1 15.0 %copy-start.7 = (bf16[21,8,512]{2,1,0:T(8,128)(2,1)}, bf16[21,8,512]{2,1,0:T(8,128)(2,1)S(1)}, u32[]{:S(2)}) copy-start(bf16[21,8,512]{2,1,0:T(8,128)(2,1)S(1)} %add_convert_fusion.8.refs_0_) | copy-start | bytes 516100
  245.1 5.5 %collective-permute-start.42 = (bf16[21,8,512]{2,1,0:T(8,128)(2,1)S(1)}, bf16[21,8,512]{2,1,0:T(8,128)(2,1)S(1)}, u32[]{:S(2)}, u32[]{:S(2)}) collective-permute-start(bf16[21,8,512]{2,1,0:T(8,128)(2,1)S(1)} %add_convert_fusion.8.refs_0_), channel_id=1, source_target_pairs={{0,4},{4,0},{8,12},{12,8},{16,20},{20,16},{24,28},{28,24},{1,5},{5... | collective-permute-start | bytes 516104 | tf_op jit(solution)/shard_map/ppermute | solution.py:890
  245.7 14.5 %collective-permute-start.43 = (bf16[21,8,512]{2,1,0:T(8,128)(2,1)S(1)}, bf16[21,8,512]{2,1,0:T(8,128)(2,1)S(1)}, u32[]{:S(2)}, u32[]{:S(2)}) collective-permute-start(bf16[21,8,512]{2,1,0:T(8,128)(2,1)S(1)} %add_convert_fusion.8.refs_0_), channel_id=1, source_target_pairs={{0,8},{4,12},{8,0},{12,4},{16,24},{20,28},{24,16},{28,20},{1,9},{5... | collective-permute-start | bytes 516104 | tf_op jit(solution)/shard_map/ppermute | solution.py:890
  250.6 9.6 %copy-start.23 = (bf16[21,8,512]{2,1,0:T(8,128)(2,1)}, bf16[21,8,512]{2,1,0:T(8,128)(2,1)S(1)}, u32[]{:S(2)}) copy-start(bf16[21,8,512]{2,1,0:T(8,128)(2,1)S(1)} %collective-permute-done.42.refs_1_) | copy-start | bytes 516100
  250.6 14.2 %collective-permute-start.44 = (bf16[21,8,512]{2,1,0:T(8,128)(2,1)S(1)}, bf16[21,8,512]{2,1,0:T(8,128)(2,1)}, u32[]{:S(2)}, u32[]{:S(2)}) collective-permute-start(bf16[21,8,512]{2,1,0:T(8,128)(2,1)S(1)} %add_convert_fusion.8.refs_0_), channel_id=1, source_target_pairs={{0,12},{4,8},{8,4},{12,0},{16,28},{20,24},{24,20},{28,16},{1,13},{... | collective-permute-start | bytes 516104 | tf_op jit(solution)/shard_map/ppermute | solution.py:890
  255.7 12.2 %collective-permute-start.20 = (bf16[25,8,512]{2,1,0:T(8,128)(2,1)}, bf16[25,8,512]{2,1,0:T(8,128)(2,1)}, u32[]{:S(2)}, u32[]{:S(2)}) collective-permute-start(bf16[25,8,512]{2,1,0:T(8,128)(2,1)} %add_convert_fusion.5), channel_id=1, source_target_pairs={{0,16},{4,20},{8,24},{12,28},{16,0},{20,4},{24,8},{28,12},{1,17},{... | collective-permute-start | bytes 614408 | tf_op jit(solution)/shard_map/ppermute | solution.py:890
  260.2 29.6 %copy-start.2 = (bf16[8,48,512]{2,1,0:T(8,128)(2,1)}, bf16[8,48,512]{2,1,0:T(8,128)(2,1)S(1)}, u32[]{:S(2)}) copy-start(bf16[8,48,512]{2,1,0:T(8,128)(2,1)S(1)} %add_convert_fusion.refs_0_) | copy-start | bytes 1179652
  260.2 13.0 %collective-permute-start.33 = (bf16[8,48,512]{2,1,0:T(8,128)(2,1)S(1)}, bf16[8,48,512]{2,1,0:T(8,128)(2,1)}, u32[]{:S(2)}, u32[]{:S(2)}) collective-permute-start(bf16[8,48,512]{2,1,0:T(8,128)(2,1)S(1)} %add_convert_fusion.refs_0_), channel_id=1, source_target_pairs={{0,4},{4,0},{8,12},{12,8},{16,20},{20,16},{24,28},{28,24},{1,5},{5... | collective-permute-start | bytes 1179656 | tf_op jit(solution)/shard_map/ppermute | solution.py:890
  267.9 21.9 %collective-permute-start.34 = (bf16[8,48,512]{2,1,0:T(8,128)(2,1)S(1)}, bf16[8,48,512]{2,1,0:T(8,128)(2,1)}, u32[]{:S(2)}, u32[]{:S(2)}) collective-permute-start(bf16[8,48,512]{2,1,0:T(8,128)(2,1)S(1)} %add_convert_fusion.refs_0_), channel_id=1, source_target_pairs={{0,8},{4,12},{8,0},{12,4},{16,24},{20,28},{24,16},{28,20},{1,9},{5... | collective-permute-start | bytes 1179656 | tf_op jit(solution)/shard_map/ppermute | solution.py:890
  267.9 21.9 %collective-permute-start.35 = (bf16[8,48,512]{2,1,0:T(8,128)(2,1)S(1)}, bf16[8,48,512]{2,1,0:T(8,128)(2,1)}, u32[]{:S(2)}, u32[]{:S(2)}) collective-permute-start(bf16[8,48,512]{2,1,0:T(8,128)(2,1)S(1)} %add_convert_fusion.refs_0_), channel_id=1, source_target_pairs={{0,12},{4,8},{8,4},{12,0},{16,28},{20,24},{24,20},{28,16},{1,13},{... | collective-permute-start | bytes 1179656 | tf_op jit(solution)/shard_map/ppermute | solution.py:890
  272.5 21.3 %collective-permute-start.21 = (bf16[25,8,512]{2,1,0:T(8,128)(2,1)}, bf16[25,8,512]{2,1,0:T(8,128)(2,1)}, u32[]{:S(2)}, u32[]{:S(2)}) collective-permute-start(bf16[25,8,512]{2,1,0:T(8,128)(2,1)} %add_convert_fusion.4.refs_0_), channel_id=1, source_target_pairs={{0,4},{4,0},{8,12},{12,8},{16,20},{20,16},{24,28},{28,24},{1,5},{5... | collective-permute-start | bytes 614408 | tf_op jit(solution)/shard_map/ppermute | solution.py:890
  273.2 20.7 %collective-permute-start.22 = (bf16[25,8,512]{2,1,0:T(8,128)(2,1)}, bf16[25,8,512]{2,1,0:T(8,128)(2,1)}, u32[]{:S(2)}, u32[]{:S(2)}) collective-permute-start(bf16[25,8,512]{2,1,0:T(8,128)(2,1)} %add_convert_fusion.4.refs_0_), channel_id=1, source_target_pairs={{0,8},{4,12},{8,0},{12,4},{16,24},{20,28},{24,16},{28,20},{1,9},{5... | collective-permute-start | bytes 614408 | tf_op jit(solution)/shard_map/ppermute | solution.py:890
  273.2 23.7 %collective-permute-start.23 = (bf16[25,8,512]{2,1,0:T(8,128)(2,1)}, bf16[25,8,512]{2,1,0:T(8,128)(2,1)}, u32[]{:S(2)}, u32[]{:S(2)}) collective-permute-start(bf16[25,8,512]{2,1,0:T(8,128)(2,1)} %add_convert_fusion.4.refs_0_), channel_id=1, source_target_pairs={{0,12},{4,8},{8,4},{12,0},{16,28},{20,24},{24,20},{28,16},{1,13},{... | collective-permute-start | bytes 614408 | tf_op jit(solution)/shard_map/ppermute | solution.py:890
  (16 other events, 27.3 us)

commit v2 on v1

--- a/solution.py
+++ b/solution.py
@@ -247,13 +247,26 @@
     return res[:3], res[3], res[4]
 
 
-def write_table(outs, tbl, lanes):
+MOVES = [(k, j) for k in range(4) for j in range(2)]
+
+
+def message_rows(k, sizes):
+    first, more, table = sizes
+    return (first + (more if k in (0, 2) else 0) + table) // 2
+
+
+def put_half(out, at, src, rows, high, b):
+    half = high // 2
+    for p in range(rows // high):
+        v = src(pl.multiple_of(p * high + b * half, 8), half)
+        out[at + p * half : at + (p + 1) * half, :] = v.astype(BF16)
+
+
+def fold_table(dst, tbl, lanes):
     width = tbl.shape[1]
-    for out in outs:
-        at = out.shape[0] - 32
-        out[at : at + 16, :] = tbl[:, :lanes].astype(BF16)
-        out[at + 16 :, : width - lanes] = tbl[:, lanes:].astype(BF16)
-        out[at + 16 :, width - lanes :] = jnp.zeros((16, 2 * lanes - width), BF16)
+    dst[:16, :] = tbl[:, :lanes]
+    dst[16:, : width - lanes] = tbl[:, lanes:]
+    dst[16:, width - lanes :] = jnp.zeros((16, 2 * lanes - width), F32)
 
 
 def put_hidden_bias(tbl, s, w, u):
@@ -269,7 +282,7 @@
     return sum8(part.T)
 
 
-def mlp_wave(wave, sc, nm, dy, pieces, down_at, down_own, vec, table=None):
+def mlp_wave(wave, sc, nm, dy, pieces, down_at, down_own, vec, high, slot=None, prev=(), table=None):
     n_tok, width = nm.shape
     blk = n_tok // 4
     rows = width // 4
@@ -288,9 +301,10 @@
         got, refs = refs[:n_src], refs[n_src:]
         if table is not None:
             t_r, refs = refs[0], refs[1:]
+        refs = refs[len(prev) :]
         hid_o, gl_o, w_s, wd_s, ub, rs = refs[:6]
-        b_s, acc_u, acc_d, tbl = refs[-4:]
-        keep, to1, to2, to3 = refs[6:-4]
+        b_s, acc_u, acc_d, tbl, t_f = refs[-5:]
+        outs = refs[6:-5]
         i = pl.program_id(0)
         s = sc_ref[0]
 
@@ -323,16 +337,6 @@
 
         @pl.when(i == pl.num_programs(0) - 1)
         def _():
-            for k, out in enumerate((keep, to1, to2, to3)):
-                v = acc_u[pl.ds(pl.multiple_of(jnp.bitwise_xor(s, k) * rows, 16), rows), :].astype(BF16)
-                h = wid if k >= 2 else 0
-                out[:rows, :wid] = v[:, h : h + wid]
-                out[:rows, wid:] = v[:, wid - h : wid2 - h]
-            down = slice(rows, rows + half)
-            keep[down, :wid] = acc_d[:half, :wid].astype(BF16)
-            keep[down, wid:] = acc_d[half:, :wid].astype(BF16)
-            to2[down, :wid] = acc_d[:half, wid:].astype(BF16)
-            to2[down, wid:] = acc_d[half:, wid:].astype(BF16)
             w = w_s[...].astype(F32)
             rs[0:8, :] = col_sums(w * acc_u[...])
             rs[8:16, :] = col_sums(w * jnp.sum(ub[...], axis=0, keepdims=True))
@@ -344,7 +348,28 @@
                 tbl[2:3, :] = (sg - vec_r[3:4, :] * ss) / vec_r[2:3, :]
                 tbl[3:4, :] = ss
                 put_hidden_bias(tbl, s, wave, line(ub[...]))
-                write_table((keep, to1, to2, to3), tbl, wid2)
+                fold_table(t_f, tbl, wid2)
+            for (k, j), out in zip(MOVES, outs):
+                b = jnp.bitwise_xor(sc_ref[1], j)
+                r0 = jnp.bitwise_xor(s, k) * rows
+                h = wid if k >= 2 else 0
+
+                def up_rows(at, n, r0=r0, h=h):
+                    v = acc_u[pl.ds(pl.multiple_of(r0 + at, 8), n), :]
+                    return jnp.concatenate([v[:, h : h + wid], v[:, wid - h : wid2 - h]], axis=1)
+
+                def down_rows(at, n, h=h):
+                    low = acc_d[pl.ds(pl.multiple_of(at, 8), n), :]
+                    top = acc_d[pl.ds(pl.multiple_of(half + at, 8), n), :]
+                    return jnp.concatenate([low[:, h : h + wid], top[:, h : h + wid]], axis=1)
+
+                put_half(out, 0, up_rows, rows, high, b)
+                end = rows // 2
+                if k in (0, 2):
+                    put_half(out, end, down_rows, half, high, b)
+                    end += half // 2
+                if table is not None:
+                    put_half(out, end, lambda at, n: t_f[pl.ds(at, n), :], 32, 32, b)
 
     row = pl.BlockSpec((blk, width), lambda i: (i, 0))
     mid = pl.BlockSpec((blk, wid2), lambda i: (i, 0))
@@ -352,33 +377,38 @@
     def fixed(dims, at=(0, 0)):
         return pl.BlockSpec(dims, lambda i: at)
 
-    more = 0 if table is None else 32
     extra = [] if table is None else [table]
-    grads = [(rows + half + more, wid2), (rows + more, wid2)] * 2
+    sizes = (rows, half, 0 if table is None else 32)
+    n_out = [message_rows(k, sizes) for k, _ in MOVES]
+    at = 0 if slot is None else slot
+    times = 1 if slot is None else 2
     return pl.pallas_call(
         kern,
         grid=(4,),
         in_specs=[SMEM, row, row]
         + [fixed((wid, width), (wave, 0)), fixed((16, width))]
-        + [fixed(t.shape) for t in srcs + extra],
+        + [fixed(t.shape) for t in srcs + extra]
+        + [ANY] * len(prev),
         out_specs=[mid, mid, fixed((width, wid2)), fixed((wid2, width)), fixed((8, wid2)), fixed((16, width))]
-        + [fixed(g) for g in grads],
+        + [fixed((n, wid2), (at, 0)) for n in n_out],
         out_shape=[shape((n_tok, wid2), BF16)] * 2
         + [shape((width, wid2), BF16), shape((wid2, width), BF16), shape((8, wid2), F32), shape((16, width), F32)]
-        + [shape(g, BF16) for g in grads],
+        + [shape((times * n, wid2), BF16) for n in n_out],
         scratch_shapes=[
             pltpu.VMEM((8, wid2), F32),
             pltpu.VMEM((width, wid2), F32),
             pltpu.VMEM((width, wid2), F32),
             pltpu.VMEM((16, width), F32),
+            pltpu.VMEM((32, wid2), F32),
         ],
+        input_output_aliases={5 + n_src + len(extra) + i: 6 + i for i in range(len(prev))},
         cost_estimate=pl.CostEstimate(
             flops=8 * n_tok * width * wid2,
             bytes_accessed=10 * n_tok * width,
             transcendentals=2 * n_tok * wid2,
         ),
         name="mlp_wave",
-    )(sc, nm, dy, down_own, vec, *srcs, *extra)
+    )(sc, nm, dy, down_own, vec, *srcs, *extra, *prev)
 
 
 def attention(sc, na, dy, weights, vec, waves_of, seg_rows, cgrad):
@@ -398,7 +428,8 @@
         blocks.append((at, chunk, 0, at + chunk, False))
         at += chunk
     blocks.append((at, FIRST_DOC - at, 0, FIRST_DOC, False))
-    blocks.append((FIRST_DOC, tail, FIRST_DOC, tail, True))
+    k_last = FIRST_DOC // 128 * 128
+    blocks.append((FIRST_DOC, tail, k_last, length - k_last, True))
 
     def kern(sc_ref, na_r, dy_r, vec_r, cs_r, sr_r, cg_r, *refs):
         q0, cg_in, mg_in, o0 = refs[:4]
@@ -443,9 +474,8 @@
         tc_r[...] = spread(cs[0:8, :], 0, ROT) + jnp.where(still, 1.0, 0.0)
         ta_r[...] = spread(-cs[8:16, :], 0, ROT // 2)
         tb_r[...] = spread(cs[8:16, :], ROT // 2, ROT)
-        last = jnp.broadcast_to(sr_r[0].astype(F32), (8, length))
-        sg_s[...] = pltpu.roll(last, length - FIRST_DOC, 1)[:, : sg_s.shape[1]]
-        seg_cols = sg_s[...].T[:tail, 0:1]
+        sg_s[...] = jnp.broadcast_to(sr_r[0].astype(F32), (8, length))[:, k_last:]
+        seg_cols = sg_s[...].T[FIRST_DOC - k_last :, 0:1]
 
         def turn(v, c, a, b, sign):
             return v * c + sign * (pltpu.roll(v, 120, 1) * a + pltpu.roll(v, 8, 1) * b)
@@ -494,7 +524,7 @@
                 ki = lax.broadcasted_iota(jnp.int32, (rn, kn - free), 1) + k0 + free
                 allowed = ki <= qi
                 if segs:
-                    allowed = allowed & (seg_cols == sg_s[0:1, :tail])
+                    allowed = allowed & (seg_cols == sg_s[0:1, :])
                 exps, invs = [], []
                 for kk in keys:
                     logit = dnt(q2, kk)
@@ -508,15 +538,17 @@
                 exb = [ex.astype(BF16) for ex in exps]
                 o2 = (dnn(exb[0], vals[0]) + dnn(exb[1], vals[1])) * scale
                 o_s[r0 : r0 + rn, cols] = o2.astype(BF16)
+                prod = o2 * dof
+                m0 = jnp.sum(jnp.where(low, prod, 0.0), axis=-1, keepdims=True)
+                m1 = jnp.sum(jnp.where(low, 0.0, prod), axis=-1, keepdims=True)
                 dsb = []
-                for e in range(2):
+                for e, mm in enumerate((m0, m1)):
                     dp = dnt(dos, vals[e])
-                    mean = jnp.sum(exps[e] * dp, axis=-1, keepdims=True) * invs[e]
-                    dsb.append((exps[e] * (dp - mean)).astype(BF16))
+                    dsb.append((exps[e] * (dp - mm * invs[e])).astype(BF16))
                 dq_s[r0 : r0 + rn, cols] = dnn(dsb[0], keys[0]) + dnn(dsb[1], keys[1])
                 for e, (ak, av) in enumerate(((ek, ev), (ok, ov))):
-                    ak[k0 : k0 + kn, :] += dtn(dsb[e], q2)
-                    av[k0 : k0 + kn, :] += dtn(exb[e], dos)
+                    ak[:, k0 : k0 + kn] += dtn(q2, dsb[e])
+                    av[:, k0 : k0 + kn] += dtn(dos, exb[e])
 
         @pl.loop(0, n_chunk)
         def _(n):
@@ -528,9 +560,7 @@
                 v = turn(dq_s[sl, cc] * 0.125, *tq, -1.0)
                 sums[:, cc] += sum8(v)
                 gqs_s[sl, cc] = v.astype(BF16)
-            gk = ek[sl, :] + pltpu.roll(ok[sl, :], 64, 1)
-            gv = pltpu.roll(ev[sl, :], 64, 1) + ov[sl, :]
-            v = jnp.where(low, gk, gv)
+            v = jnp.concatenate([ek[:64, sl] + ok[64:, sl], ev[:64, sl] + ov[64:, sl]], axis=0).T
             v = v + jnp.where(step == 1, cg_r[sl, :].astype(F32), 0.0)
             v = turn(v, *tabs(at, True), -1.0)
             sums[:, wh:] += sum8(v)
@@ -542,7 +572,7 @@
     def seq(lanes):
         return pl.BlockSpec((length, lanes), lambda i: (1 - i, 0))
 
-    seg_w = (tail + 127) // 128 * 128
+    seg_w = length - k_last
     total = na.shape[0]
     return pl.pallas_call(
         kern,
@@ -562,7 +592,8 @@
             pltpu.VMEM((length, wh), F32),
         ]
         + [pltpu.VMEM((length, 128), BF16)] * 4
-        + [pltpu.VMEM((length, 128), F32)] * 7
+        + [pltpu.VMEM((128, length), F32)] * 4
+        + [pltpu.VMEM((length, 128), F32)] * 3
         + [pltpu.VMEM((8, seg_w), F32)],
         cost_estimate=pl.CostEstimate(
             flops=4 * length * width * (wq + wh) + 24 * length * length * wh,
@@ -580,11 +611,11 @@
     blk = total // 4
     o_rows = width // 4
     n_w = len(ubs)
-    sizes = [(o_rows * 5 // 2, wq), (o_rows, wq)] * 2
+    sizes = [(message_rows(k, (o_rows, o_rows * 3 // 2, 0)), wq) for k, _ in MOVES]
 
     def kern(sc_ref, na_r, dy_r, o_r, g_r, w_r, vec_r, s0, ob_r, *refs):
         ub_r, rs_r = refs[:n_w], refs[n_w : 2 * n_w]
-        keep, to1, to2, to3, tbl, acc_q, acc_o = refs[2 * n_w :]
+        outs, (tbl, acc_q, acc_o, o_f) = refs[2 * n_w : -4], refs[-4:]
         s = sc_ref[0]
         c = jnp.bitwise_and(s, 1)
         y = jnp.right_shift(s, 1)
@@ -604,14 +635,16 @@
 
         @pl.when(i == pl.num_programs(0) - 1)
         def _():
-            for k, out in enumerate((keep, to1, to2, to3)):
-                at = pl.multiple_of(jnp.bitwise_xor(s, k) * o_rows, 16)
-                out[:o_rows, :] = acc_q[pl.ds(at, o_rows), :].astype(BF16)
             got = acc_o[...].T
-            lower = got[:o_rows, :].astype(BF16)
-            upper = got[o_rows:, :].astype(BF16)
-            fold(keep, o_rows, o_rows, jnp.where(y == 0, lower, upper), wq)
-            fold(to2, o_rows, o_rows, jnp.where(y == 0, upper, lower), wq)
+            lower, upper = got[:o_rows, :], got[o_rows:, :]
+            for i, v in enumerate((jnp.where(y == 0, lower, upper), jnp.where(y == 0, upper, lower))):
+                fold(o_f.at[i], 0, o_rows, v, wq)
+            for (k, j), out in zip(MOVES, outs):
+                b = jnp.bitwise_xor(sc_ref[1], j)
+                r0 = jnp.bitwise_xor(s, k) * o_rows
+                put_half(out, 0, lambda at, n, r0=r0: acc_q[pl.ds(pl.multiple_of(r0 + at, 8), n), :], o_rows, 32, b)
+                if k in (0, 2):
+                    put_half(out, o_rows // 2, lambda at, n, k=k: o_f[k // 2, pl.ds(at, n), :], o_rows * 3 // 2, 32, b)
             line = lambda v: jnp.sum(v, axis=0, keepdims=True)
             w = w_r[...].astype(F32)
             both = s0[...]
@@ -644,7 +677,11 @@
         + [fixed((16, width))] * n_w,
         out_specs=[fixed(g) for g in sizes] + [fixed((16, width))],
         out_shape=[shape(g, BF16) for g in sizes] + [shape((16, width), F32)],
-        scratch_shapes=[pltpu.VMEM((width, wq), F32), pltpu.VMEM((width, wh), F32)],
+        scratch_shapes=[
+            pltpu.VMEM((width, wq), F32),
+            pltpu.VMEM((width, wh), F32),
+            pltpu.VMEM((2, o_rows * 3 // 2, wq), F32),
+        ],
         cost_estimate=pl.CostEstimate(
             flops=2 * total * width * (wq + wh), bytes_accessed=4 * total * width, transcendentals=0
         ),
@@ -708,40 +745,52 @@
     )(*hids, *gls, *ups, *downs, o_all, gqs_all, wo, wqs, vec, *last)
 
 
-def first_sum(sc, sets, rows, table, planes):
-    lanes = sets[0][0].shape[1]
-    n = sets[0][0].shape[0] - rows - table
-    total = 2 * rows + n + table
-    high = total // planes
+def first_sum(sc, msgs, sizes, high, sets):
+    first, more, table = [v // 2 for v in sizes]
+    lanes = msgs[0].shape[1]
+    total = 2 * first + more + table
     half = high // 2
+    quarter = high // 4
+    planes = total // half
 
     def kern(sc_ref, *refs):
-        mine, away, tmp = refs[-3:]
-        f = lambda ref, at, m: ref[at : at + m, :].astype(F32)
-        for i in range(len(sets)):
-            k_r, r1, r2, r3 = refs[4 * i : 4 * i + 4]
-            tmp[:rows, :] = f(k_r, 0, rows) + f(r2, 0, rows)
-            tmp[rows : 2 * rows, :] = f(r1, 0, rows) + f(r3, 0, rows)
-            tmp[2 * rows : 2 * rows + n, :] = f(k_r, rows, n) + f(r2, rows, n)
+        ins = dict(zip(MOVES, refs[:8]))
+        mine, away, tmp = refs[8:]
+        for i in range(sets):
+
+            def add(at, n, keys):
+                parts = []
+                for m in keys:
+                    base = i * (ins[m].shape[0] // sets) + at(m[0])
+                    parts.append(ins[m][base : base + n, :].astype(F32))
+                while len(parts) > 1:
+                    parts = [a + b for a, b in zip(parts[::2], parts[1::2])]
+                return parts[0]
+
+            even = [m for m in MOVES if m[0] in (0, 2)]
+            odd = [m for m in MOVES if m[0] in (1, 3)]
+            tmp[:first, :] = add(lambda k: 0, first, even)
+            tmp[first : 2 * first, :] = add(lambda k: 0, first, odd)
+            tmp[2 * first : 2 * first + more, :] = add(lambda k: first, more, even)
             if table:
-                near = f(k_r, rows + n, table) + f(r1, rows, table)
-                tmp[2 * rows + n :, :] = near + (f(r2, rows + n, table) + f(r3, rows, table))
+                tmp[2 * first + more :, :] = add(lambda k: first + (more if k in (0, 2) else 0), table, MOVES)
             for out, flip in ((mine, 0), (away, 1)):
-                b = jnp.bitwise_xor(sc_ref[1], flip)
+                b = jnp.bitwise_xor(sc_ref[2], flip)
                 for p in range(planes):
-                    at = pl.multiple_of(p * high + b * half, 8)
-                    out[i * planes + p] = tmp[pl.ds(at, half), :].astype(BF16)
-
-    flat = [v for keep, got in sets for v in (keep, *got)]
-    return pl.pallas_call(
-        kern,
-        in_specs=[SMEM] + [VM] * len(flat),
+                    at = pl.multiple_of(p * half + b * quarter, 8)
+                    out[i * planes + p] = tmp[pl.ds(at, quarter), :].astype(BF16)
+
+    return pl.pallas_call(
+        kern,
+        in_specs=[SMEM] + [VM] * 8,
         out_specs=[VM, VM],
-        out_shape=[shape((planes * len(sets), half, lanes), BF16)] * 2,
+        out_shape=[shape((planes * sets, quarter, lanes), BF16)] * 2,
         scratch_shapes=[pltpu.VMEM((total, lanes), F32)],
-        cost_estimate=pl.CostEstimate(flops=2 * total * lanes, bytes_accessed=8 * total * lanes, transcendentals=0),
+        cost_estimate=pl.CostEstimate(
+            flops=8 * sets * total * lanes, bytes_accessed=10 * sets * total * lanes, transcendentals=0
+        ),
         name="first_sum",
-    )(sc, *flat)
+    )(sc, *msgs)
 
 
 def piece_row(sc_ref, n, h):
@@ -898,20 +947,16 @@
     return lax.optimization_barrier((value,) + others)[0]
 
 
-def send_terms(to1, to2, to3):
-    return [to_shard(v, k) for v, k in ((to1, 1), (to2, 2), (to3, 3))]
-
-
-def reduce_chain(half, away, count, rank):
-    got = to_replica(away, 1, count)
-    h = half.shape[1] // 2
-    b = (rank >> 1) & 1
-
-    def cut(which):
-        f = lambda v: lax.dynamic_slice_in_dim(v, which * h, h, axis=1)
-        return both_add(f(half), f(got))
-
-    quarter, away = cut(b), cut(1 - b)
+def to_group(value, k, j, count):
+    pairs = [(r * 4 + s, (r ^ j) * 4 + (s ^ k)) for r in range(count) for s in range(4)]
+    return lax.ppermute(value, ("replica", "shard"), pairs)
+
+
+def send_terms(msgs, count):
+    return [v if (k, j) == (0, 0) else to_group(v, k, j, count) for (k, j), v in zip(MOVES, msgs)]
+
+
+def reduce_chain(quarter, away, count):
     quarter = both_add(quarter, to_replica(away, 2, count))
     k = 4
     while k < count:
@@ -939,11 +984,11 @@
         shared_bias, up_bias,
     )
     near = [small] + [to_shard(small, k) for k in (1, 2, 3)]
-    own0, k1, k3, m2 = pack_first(sc, after(up_weight, small), down_weight)
+    own0, k1, k3, m2 = pack_first(after(sc, small), up_weight, down_weight)
     k1 = to_shard(k1, 1)
     m2 = to_shard(m2, 2)
     k3 = to_shard(k3, 3)
-    core_out = pack_core(sc, after(up_weight, own0), query_weight, shared_weight)
+    core_out = pack_core(after(sc, own0), up_weight, query_weight, shared_weight)
     core_got = to_shard(core_out, 1)
     tok_in = to_shard(tokens, 1)
     dy_in = to_shard(result_grad, 1)
@@ -964,34 +1009,33 @@
 
     rows = part
 
-    def wave(w, pieces, down_at, table=None):
-        return mlp_wave(w, sc, nm, dy, pieces, down_at, down_weight, vec, table)
+    def wave(w, pieces, down_at, high, slot=None, prev=(), table=None):
+        return mlp_wave(w, sc, nm, dy, pieces, down_at, down_weight, vec, high, slot, prev, table)
 
     m1 = to_shard(y1, 2)
-    hid0, gl0, wu0, wd0, ub0, rs0, keep0, *send0 = wave(0, [(own0, 0), (k1, 0), (m2, 0), (k3, 0)], (m2, rows))
+    hid0, gl0, wu0, wd0, ub0, rs0, *msg0 = wave(0, [(own0, 0), (k1, 0), (m2, 0), (k3, 0)], (m2, rows), part, 0)
     ma = to_shard(after(ya, m1), 2)
-    hid1, gl1, wu1, wd1, ub1, rs1, keep1, *send1 = wave(
-        1, [(own1, 0), (core_got, 0), (m1, 0), (m1, rows)], (m1, 2 * rows)
+    hid1, gl1, wu1, wd1, ub1, rs1, *msg01 = wave(
+        1, [(own1, 0), (core_got, 0), (m1, 0), (m1, rows)], (m1, 2 * rows), part, 1, msg0
     )
     m2b = to_shard(after(y2, ma), 2)
-    got0 = send_terms(*[after(v, ma) for v in send0])
-    got1 = send_terms(*[after(v, ma) for v in send1])
+    got01 = send_terms([after(v, ma) for v in msg01], replicas)
     o_all, gqs_all, cache, sums, wqs, wo = attention(
         sc, na, dy, (ownq, core_got, ma, output_weight), vec, angles, segs, shared_grad
     )
-    keepa, ta1, ta2, ta3, table = attn_terms(
+    *msga, table = attn_terms(
         sc, na, dy, o_all, gqs_all, wqs, vec, sums, ob, (ub0, ub1), (rs0, rs1)
     )
-    hid2, gl2, wu2, wd2, _, _, keep2, *send2 = wave(
-        2, [(own2, 0), (core_got, 2 * rows), (m2b, 0), (m2b, rows)], (m2b, 2 * rows), table
+    hid2, gl2, wu2, wd2, _, _, *msg2 = wave(
+        2, [(own2, 0), (core_got, 2 * rows), (m2b, 0), (m2b, rows)], (m2b, 2 * rows), 32, table=table
     )
 
-    def chain(sets, table_rows, planes):
-        return reduce_chain(*first_sum(sc, sets, part, table_rows, planes), replicas, r)
-
-    p01 = chain([(keep0, got0), (keep1, got1)], 0, 4)
-    pa = chain([(keepa, send_terms(ta1, ta2, ta3))], 0, 21)
-    p2 = chain([(keep2, send_terms(*send2))], 32, 25)
+    def chain(got, sizes, high, sets):
+        return reduce_chain(*first_sum(sc, got, sizes, high, sets), replicas)
+
+    p01 = chain(got01, (part, width // 2, 0), part, 2)
+    pa = chain(send_terms(msga, replicas), (part, part * 3 // 2, 0), 32, 1)
+    p2 = chain(send_terms(msg2, replicas), (part, width // 2, 32), 32, 1)
 
     hids, gls, wus, wds = (hid0, hid1, hid2), (gl0, gl1, gl2), (wu0, wu1, wu2), (wd0, wd1, wd2)
 

time: 302 us -> 308 us (1.020)
  waiting for transfers between devices: 71.5 us -> 90.9 us
  starting transfers between devices: 51.4 us -> 44.9 us
  Pallas kernels: 164 us -> 159 us
  other arithmetic: 9.24 us -> 4.68 us
    ppermute x0 -> x21, starting transfers between devices: none -> 22.8 us  [to_group(): return lax.ppermute(value, ('replica', 'shard'), pairs)]
    ppermute x0 -> x21, waiting for transfers between devices: none -> 19.3 us  [to_group(): return lax.ppermute(value, ('replica', 'shard'), pairs)]
    ppermute x18 -> x15, starting transfers between devices: 29.9 us -> 13.4 us  [to_replica(): return lax.ppermute(value, 'replica', [(r, r ^ k) for r in range(count)])]
    ppermute x18 -> x15, waiting for transfers between devices: 28.7 us -> 44.9 us  [to_replica(): return lax.ppermute(value, 'replica', [(r, r ^ k) for r in range(count)])]
    ppermute x27 -> x15, waiting for transfers between devices: 42.8 us -> 26.7 us  [to_shard(): return lax.ppermute(value, 'shard', [(s, s ^ k) for s in range(4)])]
    ppermute x27 -> x15, starting transfers between devices: 21.5 us -> 8.66 us  [to_shard(): return lax.ppermute(value, 'shard', [(s, s ^ k) for s in range(4)])]
    pallas_call x1, Pallas kernels: 49.8 us -> 44.7 us  [attention(): pl.pallas_call(kern, grid=(2,), in_specs=[SMEM, seq(width), seq(width), f...]
    convert_element_type x9 -> x6, other arithmetic: 6.97 us -> 2.27 us  [both_add(): return (a.astype(F32) + b.astype(F32)).astype(BF16)]
  transfers between devices with their start and end apart: 45 -> 51, of which waited for: 12 -> 17; matrix products, arithmetic and copies ran while one was open for 3% -> 2% of each run, Pallas kernels for 53% -> 47%
where the time goes in v2:
time: 308 us; the launch traced here: 307 us
  Pallas kernels  159 us (52%)
  waiting for transfers between devices  90.9 us (30%)
  starting transfers between devices  44.9 us (15%)
  local copies, waits for them, and re-layouts  6.01 us (2%)
  other arithmetic  4.68 us (2%)
    ppermute x15, waiting for transfers between devices, to_replica(): return lax.ppermute(value, 'replica', [(r, r ^ k) for r in range(count)])  44.9 us
    pallas_call x1, Pallas kernels, attention(): pl.pallas_call(kern, grid=(2,), in_specs=[SMEM, seq(width), seq(width), f...  44.7 us
    pallas_call x3, Pallas kernels, mlp_wave(): pl.pallas_call(kern, grid=(4,), in_specs=[SMEM, row, row] + [fixed((wid,...  39.2 us
    ppermute x15, waiting for transfers between devices, to_shard(): return lax.ppermute(value, 'shard', [(s, s ^ k) for s in range(4)])  26.7 us
    pallas_call x2, Pallas kernels, outputs(): pl.pallas_call(kern, grid=(4,), in_specs=[rows(wid2)] * (2 * n_w) + [fixe...  25.9 us
    ppermute x21, starting transfers between devices, to_group(): return lax.ppermute(value, ('replica', 'shard'), pairs)  22.8 us
    ppermute x21, waiting for transfers between devices, to_group(): return lax.ppermute(value, ('replica', 'shard'), pairs)  19.3 us
    ppermute x15, starting transfers between devices, to_replica(): return lax.ppermute(value, 'replica', [(r, r ^ k) for r in range(count)])  13.4 us
  transfers between devices with their start and end apart: 51, of which 17 were waited for; matrix products, arithmetic and copies ran while one was open for 2% of the time, Pallas kernels for 47%

profile of v2, /device:TPU:0, one launch (start us, length us, event | category | flops | bytes accessed | tf_op | source)
XLA Modules:
  0.0 307.1 jit_solution(3929232704886671970)
XLA Ops:
  1.8 1.6 pack_small.1.refs_0_
  3.4 2.6 pack_first.1
  6.0 2.6 pack_core.1
  9.1 2.6 collective-permute-start.4
  11.8 1.5 collective-permute-done.4.refs_3_
  13.4 2.2 collective-permute-done.3.refs_2_
  16.2 4.6 %norm_pair.2 = (bf16[2048,768]{1,0:T(8,128)(2,1)}, bf16[2048,768]{1,0:T(8,128)(2,1)}, bf16[2048,768]{1,0:T(8,128)(2,1)}, f32[8,768]{1,0:T(8,128)}, f32[16,768]{1,0:T(8,128)}) custom-call(bf16[1024,768]{1,0:T(8,128)(2,1)} %refs_17_.1, bf16[1024,768]{1,0:T(8,128)(2,1)} %refs_18_.1, bf16[16,768]{1,0:T(8,128)(2,1)} %pack_small.1.refs_0_, ...), custom_call_target="tpu_custom_call" | custom-call | flops 15728640 | bytes 12582912 | tf_op jit(solution)/shard_map/norm_pair/pallas_call | solution.py:234
  20.9 0.9 collective-permute-start.6
  21.7 3.9 %pack_rest.1 = (bf16[192,512]{1,0:T(8,128)(2,1)}, bf16[192,512]{1,0:T(8,128)(2,1)}, bf16[192,512]{1,0:T(8,128)(2,1)}, bf16[768,512]{1,0:T(8,128)(2,1)}, bf16[768...) custom-call(s32[3]{0:T(128)} %pad_add_fusion.2.sc_ref, bf16[192,3072]{1,0:T(8,128)(2,1)} %w_ref.5, bf16[768,768]{1,0:T(8,128)(2,1)} %d0.5, ...), custom_call_target="tpu_custom_call" | custom-call | tf_op jit(solution)/shard_map/pack_rest/pallas_call | solution.py:196
  25.7 1.2 collective-permute-start.9
  27.5 0.8 pad_add_fusion.1.sr_r
  29.0 4.7 %norm_pair.3 = (bf16[2048,768]{1,0:T(8,128)(2,1)}, bf16[2048,768]{1,0:T(8,128)(2,1)}, bf16[2048,768]{1,0:T(8,128)(2,1)}, f32[8,768]{1,0:T(8,128)}, f32[16,768]{1,0:T(8,128)}) custom-call(bf16[1024,768]{1,0:T(8,128)(2,1)} %copy-done.1, bf16[1024,768]{1,0:T(8,128)(2,1)} %collective-permute-done.1.dy_ref, ...), custom_call_target="tpu_custom_call", output_to_operand_aliasing={{0}: (6, {}), {1}: (7, {}), {2}: (8, {})} | custom-call | flops 15728640 | bytes 12582912 | tf_op jit(solution)/shard_map/norm_pair/pallas_call | solution.py:234
  33.8 20.5 %collective-permute-done.9.refs_2_ = bf16[768,512]{1,0:T(8,128)(2,1)} collective-permute-done((bf16[768,512]{1,0:T(8,128)(2,1)}, bf16[768,512]{1,0:T(8,128)(2,1)}, u32[]{:S(2)}, u32[]{:S(2)}) %collective-permute-start.9) | collective-permute-done | bytes 786464 | tf_op jit(solution)/shard_map/ppermute | solution.py:935
  55.1 2.5 collective-permute-done.7.refs_3_
  57.6 12.7 %mlp_wave.3 = (bf16[2048,512]{1,0:T(8,128)(2,1)}, bf16[2048,512]{1,0:T(8,128)(2,1)}, bf16[768,512]{1,0:T(8,128)(2,1)}, bf16[512,768]{1,0:T(8,128)(2,1)}, f32[8,5...) custom-call(s32[3]{0:T(128)} %pad_add_fusion.2.sc_ref, ...), custom_call_target="tpu_custom_call" | custom-call | flops 6442450944 | bytes 15728640 | tf_op jit(solution)/shard_map/mlp_wave/pallas_call | solution.py:385
  70.3 13.1 %mlp_wave.4 = (bf16[2048,512]{1,0:T(8,128)(2,1)}, bf16[2048,512]{1,0:T(8,128)(2,1)}, bf16[768,512]{1,0:T(8,128)(2,1)}, bf16[512,768]{1,0:T(8,128)(2,1)}, f32[8,5...) custom-call(s32[3]{0:T(128)} %pad_add_fusion.2.sc_ref, ...), custom_call_target="tpu_custom_call", output_to_operand_aliasing={{6}: (8, {}), {7}: (9, {}), {8}: (10, {}), {9}: (11, {}), {... | custom-call | flops 6442450944 | bytes 15728640 | tf_op jit(solution)/shard_map/mlp_wave/pallas_call | solution.py:385
  84.3 44.7 %attention.1 = (bf16[2048,384]{1,0:T(8,128)(2,1)}, bf16[2048,512]{1,0:T(8,128)(2,1)}, bf16[1024,128]{1,0:T(8,128)(2,1)}, f32[8,512]{1,0:T(8,128)}, bf16[768,512]{1,0:T(8,128)(2,1)}, /*index=5*/bf16[384,768]{1,0:T(8,128)(2,1)}) custom-call(s32[3]{0:T(128)} %pad_add_fusion.2.sc_ref, bf16[2048,768]{1,0:T(8,128)(2,1)} %get-tuple-element.159.na_r, ...), custom_call_target="tpu_custom_call" | custom-call | flops 12482248704 | bytes 9437184 | tf_op jit(solution)/shard_map/attention/pallas_call | solution.py:577
  129.0 9.7 %attn_terms.1 = (bf16[240,512]{1,0:T(8,128)(2,1)}, bf16[240,512]{1,0:T(8,128)(2,1)}, bf16[96,512]{1,0:T(8,128)(2,1)}, bf16[96,512]{1,0:T(8,128)(2,1)}, bf16[240,...) custom-call(s32[3]{0:T(128)} %pad_add_fusion.2.sc_ref, ...), custom_call_target="tpu_custom_call" | custom-call | flops 2818572288 | bytes 6291456 | tf_op jit(solution)/shard_map/attn_terms/pallas_call | solution.py:671
  139.6 1.5 collective-permute-start.39
  141.1 1.0 collective-permute-start.42
  142.1 1.3 collective-permute-start.44
  143.4 5.6 %collective-permute-done.41.refs_3_ = bf16[96,512]{1,0:T(8,128)(2,1)S(1)} collective-permute-done((bf16[96,512]{1,0:T(8,128)(2,1)}, bf16[96,512]{1,0:T(8,128)(2,1)S(1)}, u32[]{:S(2)}, u32[]{:S(2)}) %collective-permute-start.41) | collective-permute-done | bytes 98336 | tf_op jit(solution)/shard_map/ppermute | solution.py:952
  149.0 2.2 collective-permute-start.45
  151.2 1.3 collective-permute-start.43
  152.5 2.2 collective-permute-done.45.refs_7_
  154.7 2.7 collective-permute-start.33
  157.5 1.2 collective-permute-start.29
  158.7 2.6 collective-permute-done.43.refs_5_
  161.9 2.4 first_sum.5
  164.4 2.1 collective-permute-start.31
  166.5 2.5 collective-permute-done.32.refs_6_
  169.0 0.9 collective-permute-start.30
  170.0 1.4 collective-permute-start.27
  171.3 1.6 collective-permute-start.46
  172.9 13.3 %mlp_wave.5 = (bf16[2048,512]{1,0:T(8,128)(2,1)}, bf16[2048,512]{1,0:T(8,128)(2,1)}, bf16[768,512]{1,0:T(8,128)(2,1)}, bf16[512,768]{1,0:T(8,128)(2,1)}, f32[8,5...) custom-call(s32[3]{0:T(128)} %pad_add_fusion.2.sc_ref, ...), custom_call_target="tpu_custom_call" | custom-call | flops 6442450944 | bytes 15728640 | tf_op jit(solution)/shard_map/mlp_wave/pallas_call | solution.py:385
  188.0 6.4 %collective-permute-done.30.refs_4_ = bf16[576,512]{1,0:T(8,128)(2,1)S(1)} collective-permute-done((bf16[576,512]{1,0:T(8,128)(2,1)}, bf16[576,512]{1,0:T(8,128)(2,1)S(1)}, u32[]{:S(2)}, u32[]{:S(2)}) %collective-permute-start.30) | collective-permute-done | bytes 589856 | tf_op jit(solution)/shard_map/ppermute | solution.py:952
  195.2 0.8 copy-done.8
  196.0 3.4 %first_sum.4 = (bf16[8,48,512]{2,1,0:T(8,128)(2,1)}, bf16[8,48,512]{2,1,0:T(8,128)(2,1)}) custom-call(s32[3]{0:T(128)} %pad_add_fusion.2.sc_ref, bf16[576,512]{1,0:T(8,128)(2,1)} %get-tuple-element.198.refs_0_, bf16[576,512]{1,0:T(8,128)(2,1)} %copy-done.8, bf16[192,512]{1,0:T(8,128)(2,1)} %copy-done.23, bf16[192,512]{1,0:T(8,128)(2,1)} %copy-done.22, ...), custom_call_target="tpu_custom_call" | custom-call | flops 3145728 | bytes 3932160 | tf_op jit(solution)/shard_map/first_sum/pallas_call | solution.py:783
  199.4 1.6 collective-permute-start.34
  201.0 1.3 collective-permute-start.21
  202.7 1.0 collective-permute-start.18
  203.8 2.0 collective-permute-start.19
  205.8 12.0 %outputs.2 = (bf16[1024,768]{1,0:T(8,128)(2,1)}, bf16[1024,768]{1,0:T(8,128)(2,1)}) custom-call(bf16[2048,512]{1,0:T(8,128)(2,1)} %get-tuple-element.140.refs_0_, bf16[2048,512]{1,0:T(8,128)(2,1)} %get-tuple-element.153.refs_1_, bf16[2048,512]{1,0:T(8,128)(2,1)} %get-tuple-element.171.refs_2_, bf16[2048,512]{1,0:T(8,128)(2,1)} %get-tuple-element.172.refs_3_, ...), custom_call_target="tpu_custom_call" | custom-call | flops 6247415808 | bytes 18874368 | tf_op jit(solution)/shard_map/outputs/pallas_call | solution.py:731
  217.8 2.6 collective-permute-start.47
  221.8 2.5 first_sum.3
  224.8 12.4 %collective-permute-done.47 = bf16[21,8,512]{2,1,0:T(8,128)(2,1)} collective-permute-done((bf16[21,8,512]{2,1,0:T(8,128)(2,1)S(1)}, bf16[21,8,512]{2,1,0:T(8,128)(2,1)}, u32[]{:S(2)}, u32[]{:S(2)}) %collective-permute-start.47) | collective-permute-done | bytes 172064 | tf_op jit(solution)/shard_map/ppermute | solution.py:939
  237.2 1.0 add_convert_fusion.4.refs_0_
  238.7 1.5 collective-permute-start.49
  240.2 1.0 add_convert_fusion.3
  241.2 8.0 %collective-permute-done.50.refs_3_ = bf16[21,8,512]{2,1,0:T(8,128)(2,1)S(1)} collective-permute-done((bf16[21,8,512]{2,1,0:T(8,128)(2,1)S(1)}, bf16[21,8,512]{2,1,0:T(8,128)(2,1)S(1)}, u32[]{:S(2)}, u32[]{:S(2)}) %collective-permute-start.50) | collective-permute-done | bytes 172064 | tf_op jit(solution)/shard_map/ppermute | solution.py:939
  249.2 1.5 collective-permute-start.48
  250.8 2.0 collective-permute-done.49.refs_2_
  252.8 1.3 collective-permute-start.38
  254.2 1.2 collective-permute-done.48.refs_1_
  256.0 6.6 %collective-permute-done.23 = bf16[25,8,512]{2,1,0:T(8,128)(2,1)S(1)} collective-permute-done((bf16[25,8,512]{2,1,0:T(8,128)(2,1)S(1)}, bf16[25,8,512]{2,1,0:T(8,128)(2,1)S(1)}, u32[]{:S(2)}, u32[]{:S(2)}) %collective-permute-start.23) | collective-permute-done | bytes 204832 | tf_op jit(solution)/shard_map/ppermute | solution.py:939
  262.7 0.9 collective-permute-start.36
  263.7 6.4 %collective-permute-done.38.refs_3_ = bf16[8,48,512]{2,1,0:T(8,128)(2,1)S(1)} collective-permute-done((bf16[8,48,512]{2,1,0:T(8,128)(2,1)S(1)}, bf16[8,48,512]{2,1,0:T(8,128)(2,1)S(1)}, u32[]{:S(2)}, u32[]{:S(2)}) %collective-permute-start.38) | collective-permute-done | bytes 393248 | tf_op jit(solution)/shard_map/ppermute | solution.py:939
  270.1 7.5 %collective-permute-done.37.refs_2_ = bf16[8,48,512]{2,1,0:T(8,128)(2,1)S(1)} collective-permute-done((bf16[8,48,512]{2,1,0:T(8,128)(2,1)S(1)}, bf16[8,48,512]{2,1,0:T(8,128)(2,1)S(1)}, u32[]{:S(2)}, u32[]{:S(2)}) %collective-permute-start.37) | collective-permute-done | bytes 393248 | tf_op jit(solution)/shard_map/ppermute | solution.py:939
  277.5 0.9 collective-permute-done.36.refs_1_
  279.9 3.1 attn_grads.1
  283.0 4.1 %early_grads.1 = (f32[192,3072]{1,0:T(8,128)}, f32[768,768]{1,0:T(8,128)}) custom-call(s32[3]{0:T(128)} %pad_add_fusion.2.sc_ref, bf16[8,48,512]{2,1,0:T(8,128)(2,1)} %copy-done.2, bf16[8,48,512]{2,1,0:T(8,128)(2,1)} %copy-done.12, bf16[8,48,512]{2,1,0:T(8,128)(2,1)} %copy-done.11, bf16[8,48,512]{2,1,0:T(8,128)(2,1)} %copy-done.10), custom_call_target="tpu_custom_call" | custom-call | bytes 7077888 | tf_op jit(solution)/shard_map/early_grads/pallas_call | solution.py:826
  287.7 4.1 %late_grads.1 = (f32[192,3072]{1,0:T(8,128)}, f32[768,768]{1,0:T(8,128)}, f32[192]{0:T(256)}, f32[192]{0:T(256)}, f32[192]{0:T(256)}, /*index=5*/f32[192]{0:T(25...) custom-call(s32[3]{0:T(128)} %pad_add_fusion.2.sc_ref, ...), custom_call_target="tpu_custom_call", output_to_operand_aliasing={{0}: (5, {}), {1}: (6, {})} | custom-call | bytes 2359296 | tf_op jit(solution)/shard_map/late_grads/pallas_call | solution.py:894
  291.9 1.1 copy-done.3
  293.0 13.9 %outputs.3 = (bf16[1024,768]{1,0:T(8,128)(2,1)}, bf16[1024,768]{1,0:T(8,128)(2,1)}) custom-call(bf16[2048,512]{1,0:T(8,128)(2,1)} %get-tuple-element.140.refs_0_, bf16[2048,512]{1,0:T(8,128)(2,1)} %get-tuple-element.153.refs_1_, bf16[2048,512]{1,0:T(8,128)(2,1)} %get-tuple-element.171.refs_2_, bf16[2048,512]{1,0:T(8,128)(2,1)} %get-tuple-element.172.refs_3_, ...), custom_call_target="tpu_custom_call" | custom-call | flops 6247415808 | bytes 18874368 | tf_op jit(solution)/shard_map/outputs/pallas_call | solution.py:731
  (167 shorter events, 15.2 us)
Async XLA Ops:
  0.7 26.6 %collective-permute-start = (bf16[1024,768]{1,0:T(8,128)(2,1)}, bf16[1024,768]{1,0:T(8,128)(2,1)S(1)}, u32[]{:S(2)}, u32[]{:S(2)}) collective-permute-start(bf16[1024,768]{1,0:T(8,128)(2,1)} %refs_17_.1), channel_id=1, source_target_pairs={{0,1},{1,0},{2,3},{3,2},{4,5},{5,4},{6,7},{7,6},{8,9},{9,8},{10,11... | collective-permute-start | bytes 4718600 | tf_op jit(solution)/shard_map/ppermute | solution.py:935
  8.6 12.2 %collective-permute-start.8 = (bf16[960,512]{1,0:T(8,128)(2,1)}, bf16[960,512]{1,0:T(8,128)(2,1)}, u32[]{:S(2)}, u32[]{:S(2)}) collective-permute-start(bf16[960,512]{1,0:T(8,128)(2,1)} %pack_core.1), channel_id=1, source_target_pairs={{0,1},{1,0},{2,3},{3,2},{4,5},{5,4},{6,7},{7,6},{8,9},{9,8},{10,11... | collective-permute-start | bytes 2949128 | tf_op jit(solution)/shard_map/ppermute | solution.py:935
  8.7 20.4 %collective-permute-start.1 = (bf16[1024,768]{1,0:T(8,128)(2,1)S(1)}, bf16[1024,768]{1,0:T(8,128)(2,1)}, u32[]{:S(2)}, u32[]{:S(2)}) collective-permute-start(bf16[1024,768]{1,0:T(8,128)(2,1)S(1)} %copy-done), channel_id=1, source_target_pairs={{0,1},{1,0},{2,3},{3,2},{4,5},{5,4},{6,7},{7,6},{8,9},{9,8},{10,11... | collective-permute-start | bytes 4718600 | tf_op jit(solution)/shard_map/ppermute | solution.py:935
  9.1 4.1 %collective-permute-start.4 = (bf16[16,768]{1,0:T(8,128)(2,1)S(1)}, bf16[16,768]{1,0:T(8,128)(2,1)S(1)}, u32[]{:S(2)}, u32[]{:S(2)}) collective-permute-start(bf16[16,768]{1,0:T(8,128)(2,1)S(1)} %copy-done.18), channel_id=1, source_target_pairs={{0,3},{1,2},{2,1},{3,0},{4,7},{5,6},{6,5},{7,4},{8,11},{9,10},{10,... | collective-permute-start | bytes 73736 | tf_op jit(solution)/shard_map/ppermute | solution.py:935
  11.8 3.8 %collective-permute-start.3 = (bf16[16,768]{1,0:T(8,128)(2,1)S(1)}, bf16[16,768]{1,0:T(8,128)(2,1)S(1)}, u32[]{:S(2)}, u32[]{:S(2)}) collective-permute-start(bf16[16,768]{1,0:T(8,128)(2,1)S(1)} %copy-done.18), channel_id=1, source_target_pairs={{0,2},{1,3},{2,0},{3,1},{4,6},{5,7},{6,4},{7,5},{8,10},{9,11},{10,... | collective-permute-start | bytes 73736 | tf_op jit(solution)/shard_map/ppermute | solution.py:935
  13.3 2.3 collective-permute-start.2
  15.6 10.1 %collective-permute-start.12 = (s32[2,1024]{1,0:T(2,128)S(1)}, s32[2,1024]{1,0:T(2,128)S(1)}, u32[]{:S(2)}, u32[]{:S(2)}) collective-permute-start(s32[2,1024]{1,0:T(2,128)S(1)} %pad_add_fusion), channel_id=1, source_target_pairs={{0,1},{1,0},{2,3},{3,2},{4,5},{5,4},{6,7},{7,6},{8,9},{9,8},{10,11... | collective-permute-start | bytes 24584 | tf_op jit(solution)/shard_map/ppermute | solution.py:935
  15.6 39.5 %collective-permute-start.5 = (bf16[192,512]{1,0:T(8,128)(2,1)}, bf16[192,512]{1,0:T(8,128)(2,1)}, u32[]{:S(2)}, u32[]{:S(2)}) collective-permute-start(bf16[192,512]{1,0:T(8,128)(2,1)} %get-tuple-element.137), channel_id=1, source_target_pairs={{0,1},{1,0},{2,3},{3,2},{4,5},{5,4},{6,7},{7,6},{8,9},{9,8},{10,11... | collective-permute-start | bytes 589832 | tf_op jit(solution)/shard_map/ppermute | solution.py:935
  20.9 36.7 %collective-permute-start.6 = (bf16[576,512]{1,0:T(8,128)(2,1)}, bf16[576,512]{1,0:T(8,128)(2,1)}, u32[]{:S(2)}, u32[]{:S(2)}) collective-permute-start(bf16[576,512]{1,0:T(8,128)(2,1)} %get-tuple-element.138), channel_id=1, source_target_pairs={{0,2},{1,3},{2,0},{3,1},{4,6},{5,7},{6,4},{7,5},{8,10},{9,11},{10,... | collective-permute-start | bytes 1769480 | tf_op jit(solution)/shard_map/ppermute | solution.py:935
  25.7 28.6 %collective-permute-start.9 = (bf16[768,512]{1,0:T(8,128)(2,1)}, bf16[768,512]{1,0:T(8,128)(2,1)}, u32[]{:S(2)}, u32[]{:S(2)}) collective-permute-start(bf16[768,512]{1,0:T(8,128)(2,1)} %get-tuple-element.144), channel_id=1, source_target_pairs={{0,2},{1,3},{2,0},{3,1},{4,6},{5,7},{6,4},{7,5},{8,10},{9,11},{10,... | collective-permute-start | bytes 2359304 | tf_op jit(solution)/shard_map/ppermute | solution.py:935
  27.3 30.3 %collective-permute-start.7 = (bf16[192,512]{1,0:T(8,128)(2,1)S(1)}, bf16[192,512]{1,0:T(8,128)(2,1)}, u32[]{:S(2)}, u32[]{:S(2)}) collective-permute-start(bf16[192,512]{1,0:T(8,128)(2,1)S(1)} %copy-done.44), channel_id=1, source_target_pairs={{0,3},{1,2},{2,1},{3,0},{4,7},{5,6},{6,5},{7,4},{8,11},{9,10},{10,... | collective-permute-start | bytes 589832 | tf_op jit(solution)/shard_map/ppermute | solution.py:935
  29.0 25.3 %copy-start.42 = (bf16[672,512]{1,0:T(8,128)(2,1)S(1)}, bf16[672,512]{1,0:T(8,128)(2,1)}, u32[]{:S(2)}) copy-start(bf16[672,512]{1,0:T(8,128)(2,1)} %get-tuple-element.157) | copy-start | bytes 2064388
  54.3 29.1 %collective-permute-start.10 = (bf16[672,512]{1,0:T(8,128)(2,1)S(1)}, bf16[672,512]{1,0:T(8,128)(2,1)S(1)}, u32[]{:S(2)}, u32[]{:S(2)}) collective-permute-start(bf16[672,512]{1,0:T(8,128)(2,1)S(1)} %copy-done.42), channel_id=1, source_target_pairs={{0,2},{1,3},{2,0},{3,1},{4,6},{5,7},{6,4},{7,5},{8,10},{9,11},{10,... | collective-permute-start | bytes 2064392 | tf_op jit(solution)/shard_map/ppermute | solution.py:935
  83.5 87.9 %collective-permute-start.11 = (bf16[768,512]{1,0:T(8,128)(2,1)S(1)}, bf16[768,512]{1,0:T(8,128)(2,1)}, u32[]{:S(2)}, u32[]{:S(2)}) collective-permute-start(bf16[768,512]{1,0:T(8,128)(2,1)S(1)} %copy-done.41), channel_id=1, source_target_pairs={{0,2},{1,3},{2,0},{3,1},{4,6},{5,7},{6,4},{7,5},{8,10},{9,11},{10,... | collective-permute-start | bytes 2359304 | tf_op jit(solution)/shard_map/ppermute | solution.py:935
  129.0 25.7 %copy-start.47 = (bf16[192,512]{1,0:T(8,128)(2,1)S(1)}, bf16[192,512]{1,0:T(8,128)(2,1)}, u32[]{:S(2)}) copy-start(bf16[192,512]{1,0:T(8,128)(2,1)} %get-tuple-element.212) | copy-start | bytes 589828
  129.0 28.4 %copy-start.46 = (bf16[192,512]{1,0:T(8,128)(2,1)S(1)}, bf16[192,512]{1,0:T(8,128)(2,1)}, u32[]{:S(2)}) copy-start(bf16[192,512]{1,0:T(8,128)(2,1)} %get-tuple-element.210) | copy-start | bytes 589828
  129.0 28.4 %copy-start.45 = (bf16[192,512]{1,0:T(8,128)(2,1)S(1)}, bf16[192,512]{1,0:T(8,128)(2,1)}, u32[]{:S(2)}) copy-start(bf16[192,512]{1,0:T(8,128)(2,1)} %get-tuple-element.204) | copy-start | bytes 589828
  138.8 3.3 %collective-permute-start.40 = (bf16[96,512]{1,0:T(8,128)(2,1)}, bf16[96,512]{1,0:T(8,128)(2,1)S(1)}, u32[]{:S(2)}, u32[]{:S(2)}) collective-permute-start(bf16[96,512]{1,0:T(8,128)(2,1)} %get-tuple-element.221), channel_id=1, source_target_pairs={{0,1},{1,0},{2,3},{3,2},{4,5},{5,4},{6,7},{7,6},{8,9},{9,8},{10,11... | collective-permute-start | bytes 294920 | tf_op jit(solution)/shard_map/ppermute | solution.py:952
  139.6 17.8 %collective-permute-start.39 = (bf16[240,512]{1,0:T(8,128)(2,1)}, bf16[240,512]{1,0:T(8,128)(2,1)S(1)}, u32[]{:S(2)}, u32[]{:S(2)}) collective-permute-start(bf16[240,512]{1,0:T(8,128)(2,1)} %get-tuple-element.220), channel_id=1, source_target_pairs={{0,4},{1,5},{2,6},{3,7},{4,0},{5,1},{6,2},{7,3},{8,12},{9,13},{10,... | collective-permute-start | bytes 737288 | tf_op jit(solution)/shard_map/ppermute | solution.py:952
  141.1 16.4 %collective-permute-start.42 = (bf16[240,512]{1,0:T(8,128)(2,1)}, bf16[240,512]{1,0:T(8,128)(2,1)S(1)}, u32[]{:S(2)}, u32[]{:S(2)}) collective-permute-start(bf16[240,512]{1,0:T(8,128)(2,1)} %get-tuple-element.223), channel_id=1, source_target_pairs={{0,2},{1,3},{2,0},{3,1},{4,6},{5,7},{6,4},{7,5},{8,10},{9,11},{10,... | collective-permute-start | bytes 737288 | tf_op jit(solution)/shard_map/ppermute | solution.py:952
  142.1 6.9 %collective-permute-start.41 = (bf16[96,512]{1,0:T(8,128)(2,1)}, bf16[96,512]{1,0:T(8,128)(2,1)S(1)}, u32[]{:S(2)}, u32[]{:S(2)}) collective-permute-start(bf16[96,512]{1,0:T(8,128)(2,1)} %get-tuple-element.222), channel_id=1, source_target_pairs={{0,5},{1,4},{2,7},{3,6},{4,1},{5,0},{6,3},{7,2},{8,13},{9,12},{10,... | collective-permute-start | bytes 294920 | tf_op jit(solution)/shard_map/ppermute | solution.py:952
  142.1 19.2 %copy-start.35 = (bf16[96,512]{1,0:T(8,128)(2,1)}, bf16[96,512]{1,0:T(8,128)(2,1)S(1)}, u32[]{:S(2)}) copy-start(bf16[96,512]{1,0:T(8,128)(2,1)S(1)} %collective-permute-done.40.refs_2_) | copy-start | bytes 294916
  142.1 9.1 %collective-permute-start.44 = (bf16[96,512]{1,0:T(8,128)(2,1)}, bf16[96,512]{1,0:T(8,128)(2,1)S(1)}, u32[]{:S(2)}, u32[]{:S(2)}) collective-permute-start(bf16[96,512]{1,0:T(8,128)(2,1)} %get-tuple-element.225), channel_id=1, source_target_pairs={{0,3},{1,2},{2,1},{3,0},{4,7},{5,6},{6,5},{7,4},{8,11},{9,10},{10,... | collective-permute-start | bytes 294920 | tf_op jit(solution)/shard_map/ppermute | solution.py:952
  149.0 5.7 %collective-permute-start.45 = (bf16[96,512]{1,0:T(8,128)(2,1)}, bf16[96,512]{1,0:T(8,128)(2,1)S(1)}, u32[]{:S(2)}, u32[]{:S(2)}) collective-permute-start(bf16[96,512]{1,0:T(8,128)(2,1)} %get-tuple-element.226), channel_id=1, source_target_pairs={{0,7},{1,6},{2,5},{3,4},{4,3},{5,2},{6,1},{7,0},{8,15},{9,14},{10,... | collective-permute-start | bytes 294920 | tf_op jit(solution)/shard_map/ppermute | solution.py:952
  151.2 10.1 %collective-permute-start.43 = (bf16[240,512]{1,0:T(8,128)(2,1)}, bf16[240,512]{1,0:T(8,128)(2,1)S(1)}, u32[]{:S(2)}, u32[]{:S(2)}) collective-permute-start(bf16[240,512]{1,0:T(8,128)(2,1)} %get-tuple-element.224), channel_id=1, source_target_pairs={{0,6},{1,7},{2,4},{3,5},{4,2},{5,3},{6,0},{7,1},{8,14},{9,15},{10,... | collective-permute-start | bytes 737288 | tf_op jit(solution)/shard_map/ppermute | solution.py:952
  154.7 9.7 %collective-permute-start.33 = (bf16[192,512]{1,0:T(8,128)(2,1)S(1)}, bf16[192,512]{1,0:T(8,128)(2,1)S(1)}, u32[]{:S(2)}, u32[]{:S(2)}) collective-permute-start(bf16[192,512]{1,0:T(8,128)(2,1)S(1)} %copy-done.47), channel_id=1, source_target_pairs={{0,7},{1,6},{2,5},{3,4},{4,3},{5,2},{6,1},{7,0},{8,15},{9,14},{10,... | collective-permute-start | bytes 589832 | tf_op jit(solution)/shard_map/ppermute | solution.py:952
  157.4 11.6 %collective-permute-start.32 = (bf16[192,512]{1,0:T(8,128)(2,1)S(1)}, bf16[192,512]{1,0:T(8,128)(2,1)S(1)}, u32[]{:S(2)}, u32[]{:S(2)}) collective-permute-start(bf16[192,512]{1,0:T(8,128)(2,1)S(1)} %copy-done.46), channel_id=1, source_target_pairs={{0,3},{1,2},{2,1},{3,0},{4,7},{5,6},{6,5},{7,4},{8,11},{9,10},{10,... | collective-permute-start | bytes 589832 | tf_op jit(solution)/shard_map/ppermute | solution.py:952
  157.5 12.5 %collective-permute-start.29 = (bf16[192,512]{1,0:T(8,128)(2,1)S(1)}, bf16[192,512]{1,0:T(8,128)(2,1)S(1)}, u32[]{:S(2)}, u32[]{:S(2)}) collective-permute-start(bf16[192,512]{1,0:T(8,128)(2,1)S(1)} %copy-done.45), channel_id=1, source_target_pairs={{0,5},{1,4},{2,7},{3,6},{4,1},{5,0},{6,3},{7,2},{8,13},{9,12},{10,... | collective-permute-start | bytes 589832 | tf_op jit(solution)/shard_map/ppermute | solution.py:952
  161.2 25.0 %collective-permute-start.28 = (bf16[192,512]{1,0:T(8,128)(2,1)}, bf16[192,512]{1,0:T(8,128)(2,1)S(1)}, u32[]{:S(2)}, u32[]{:S(2)}) collective-permute-start(bf16[192,512]{1,0:T(8,128)(2,1)} %get-tuple-element.202), channel_id=1, source_target_pairs={{0,1},{1,0},{2,3},{3,2},{4,5},{5,4},{6,7},{7,6},{8,9},{9,8},{10,11... | collective-permute-start | bytes 589832 | tf_op jit(solution)/shard_map/ppermute | solution.py:952
  164.4 21.9 %copy-start.20 = (bf16[192,512]{1,0:T(8,128)(2,1)}, bf16[192,512]{1,0:T(8,128)(2,1)S(1)}, u32[]{:S(2)}) copy-start(bf16[192,512]{1,0:T(8,128)(2,1)S(1)} %collective-permute-done.33.refs_7_) | copy-start | bytes 589828
  164.4 22.7 %collective-permute-start.31 = (bf16[576,512]{1,0:T(8,128)(2,1)}, bf16[576,512]{1,0:T(8,128)(2,1)S(1)}, u32[]{:S(2)}, u32[]{:S(2)}) collective-permute-start(bf16[576,512]{1,0:T(8,128)(2,1)} %get-tuple-element.208), channel_id=1, source_target_pairs={{0,6},{1,7},{2,4},{3,5},{4,2},{5,3},{6,0},{7,1},{8,14},{9,15},{10,... | collective-permute-start | bytes 1769480 | tf_op jit(solution)/shard_map/ppermute | solution.py:952
  169.0 17.2 %copy-start.21 = (bf16[192,512]{1,0:T(8,128)(2,1)}, bf16[192,512]{1,0:T(8,128)(2,1)S(1)}, u32[]{:S(2)}) copy-start(bf16[192,512]{1,0:T(8,128)(2,1)S(1)} %collective-permute-done.32.refs_6_) | copy-start | bytes 589828
  169.0 25.4 %collective-permute-start.30 = (bf16[576,512]{1,0:T(8,128)(2,1)}, bf16[576,512]{1,0:T(8,128)(2,1)S(1)}, u32[]{:S(2)}, u32[]{:S(2)}) collective-permute-start(bf16[576,512]{1,0:T(8,128)(2,1)} %get-tuple-element.206), channel_id=1, source_target_pairs={{0,2},{1,3},{2,0},{3,1},{4,6},{5,7},{6,4},{7,5},{8,10},{9,11},{10,... | collective-permute-start | bytes 1769480 | tf_op jit(solution)/shard_map/ppermute | solution.py:952
  170.0 16.3 %copy-start.22 = (bf16[192,512]{1,0:T(8,128)(2,1)}, bf16[192,512]{1,0:T(8,128)(2,1)S(1)}, u32[]{:S(2)}) copy-start(bf16[192,512]{1,0:T(8,128)(2,1)S(1)} %collective-permute-done.29.refs_3_) | copy-start | bytes 589828
  170.0 24.4 %collective-permute-start.27 = (bf16[576,512]{1,0:T(8,128)(2,1)}, bf16[576,512]{1,0:T(8,128)(2,1)S(1)}, u32[]{:S(2)}, u32[]{:S(2)}) collective-permute-start(bf16[576,512]{1,0:T(8,128)(2,1)} %get-tuple-element.200), channel_id=1, source_target_pairs={{0,4},{1,5},{2,6},{3,7},{4,0},{5,1},{6,2},{7,3},{8,12},{9,13},{10,... | collective-permute-start | bytes 1769480 | tf_op jit(solution)/shard_map/ppermute | solution.py:952
  171.3 15.1 %collective-permute-start.46 = (bf16[21,8,512]{2,1,0:T(8,128)(2,1)}, bf16[21,8,512]{2,1,0:T(8,128)(2,1)S(1)}, u32[]{:S(2)}, u32[]{:S(2)}) collective-permute-start(bf16[21,8,512]{2,1,0:T(8,128)(2,1)} %get-tuple-element.228), channel_id=1, source_target_pairs={{0,8},{4,12},{8,0},{12,4},{16,24},{20,28},{24,16},{28,20},{1,9},{5... | collective-permute-start | bytes 516104 | tf_op jit(solution)/shard_map/ppermute | solution.py:939
  186.3 16.0 %collective-permute-start.16 = (bf16[112,512]{1,0:T(8,128)(2,1)}, bf16[112,512]{1,0:T(8,128)(2,1)S(1)}, u32[]{:S(2)}, u32[]{:S(2)}) collective-permute-start(bf16[112,512]{1,0:T(8,128)(2,1)} %get-tuple-element.189), channel_id=1, source_target_pairs={{0,1},{1,0},{2,3},{3,2},{4,5},{5,4},{6,7},{7,6},{8,9},{9,8},{10,11... | collective-permute-start | bytes 344072 | tf_op jit(solution)/shard_map/ppermute | solution.py:952
  186.4 16.3 %collective-permute-start.17 = (bf16[112,512]{1,0:T(8,128)(2,1)}, bf16[112,512]{1,0:T(8,128)(2,1)S(1)}, u32[]{:S(2)}, u32[]{:S(2)}) collective-permute-start(bf16[112,512]{1,0:T(8,128)(2,1)} %get-tuple-element.190), channel_id=1, source_target_pairs={{0,5},{1,4},{2,7},{3,6},{4,1},{5,0},{6,3},{7,2},{8,13},{9,12},{10,... | collective-permute-start | bytes 344072 | tf_op jit(solution)/shard_map/ppermute | solution.py:952
  187.1 16.6 %collective-permute-start.20 = (bf16[112,512]{1,0:T(8,128)(2,1)}, bf16[112,512]{1,0:T(8,128)(2,1)S(1)}, u32[]{:S(2)}, u32[]{:S(2)}) collective-permute-start(bf16[112,512]{1,0:T(8,128)(2,1)} %get-tuple-element.193), channel_id=1, source_target_pairs={{0,3},{1,2},{2,1},{3,0},{4,7},{5,6},{6,5},{7,4},{8,11},{9,10},{10,... | collective-permute-start | bytes 344072 | tf_op jit(solution)/shard_map/ppermute | solution.py:952
  199.4 21.0 %collective-permute-start.34 = (bf16[8,48,512]{2,1,0:T(8,128)(2,1)}, bf16[8,48,512]{2,1,0:T(8,128)(2,1)S(1)}, u32[]{:S(2)}, u32[]{:S(2)}) collective-permute-start(bf16[8,48,512]{2,1,0:T(8,128)(2,1)} %get-tuple-element.214), channel_id=1, source_target_pairs={{0,8},{4,12},{8,0},{12,4},{16,24},{20,28},{24,16},{28,20},{1,9},{5... | collective-permute-start | bytes 1179656 | tf_op jit(solution)/shard_map/ppermute | solution.py:939
  201.0 16.8 %collective-permute-start.21 = (bf16[112,512]{1,0:T(8,128)(2,1)}, bf16[112,512]{1,0:T(8,128)(2,1)S(1)}, u32[]{:S(2)}, u32[]{:S(2)}) collective-permute-start(bf16[112,512]{1,0:T(8,128)(2,1)} %get-tuple-element.194), channel_id=1, source_target_pairs={{0,7},{1,6},{2,5},{3,4},{4,3},{5,2},{6,1},{7,0},{8,15},{9,14},{10,... | collective-permute-start | bytes 344072 | tf_op jit(solution)/shard_map/ppermute | solution.py:952
  202.3 15.5 %copy-start.28 = (bf16[112,512]{1,0:T(8,128)(2,1)}, bf16[112,512]{1,0:T(8,128)(2,1)S(1)}, u32[]{:S(2)}) copy-start(bf16[112,512]{1,0:T(8,128)(2,1)S(1)} %collective-permute-done.16.refs_2_) | copy-start | bytes 344068
  202.3 18.2 %collective-permute-start.15 = (bf16[304,512]{1,0:T(8,128)(2,1)}, bf16[304,512]{1,0:T(8,128)(2,1)S(1)}, u32[]{:S(2)}, u32[]{:S(2)}) collective-permute-start(bf16[304,512]{1,0:T(8,128)(2,1)} %get-tuple-element.188), channel_id=1, source_target_pairs={{0,4},{1,5},{2,6},{3,7},{4,0},{5,1},{6,2},{7,3},{8,12},{9,13},{10,... | collective-permute-start | bytes 933896 | tf_op jit(solution)/shard_map/ppermute | solution.py:952
  202.7 18.4 %collective-permute-start.18 = (bf16[304,512]{1,0:T(8,128)(2,1)}, bf16[304,512]{1,0:T(8,128)(2,1)S(1)}, u32[]{:S(2)}, u32[]{:S(2)}) collective-permute-start(bf16[304,512]{1,0:T(8,128)(2,1)} %get-tuple-element.191), channel_id=1, source_target_pairs={{0,2},{1,3},{2,0},{3,1},{4,6},{5,7},{6,4},{7,5},{8,10},{9,11},{10,... | collective-permute-start | bytes 933896 | tf_op jit(solution)/shard_map/ppermute | solution.py:952
  203.8 17.9 %collective-permute-start.19 = (bf16[304,512]{1,0:T(8,128)(2,1)}, bf16[304,512]{1,0:T(8,128)(2,1)}, u32[]{:S(2)}, u32[]{:S(2)}) collective-permute-start(bf16[304,512]{1,0:T(8,128)(2,1)} %get-tuple-element.192), channel_id=1, source_target_pairs={{0,6},{1,7},{2,4},{3,5},{4,2},{5,3},{6,0},{7,1},{8,14},{9,15},{10,... | collective-permute-start | bytes 933896 | tf_op jit(solution)/shard_map/ppermute | solution.py:952
  205.8 15.2 %copy-start.9 = (bf16[8,48,512]{2,1,0:T(8,128)(2,1)S(1)}, bf16[8,48,512]{2,1,0:T(8,128)(2,1)}, u32[]{:S(2)}) copy-start(bf16[8,48,512]{2,1,0:T(8,128)(2,1)} %get-tuple-element.213) | copy-start | bytes 1179652
  217.8 19.4 %collective-permute-start.47 = (bf16[21,8,512]{2,1,0:T(8,128)(2,1)S(1)}, bf16[21,8,512]{2,1,0:T(8,128)(2,1)}, u32[]{:S(2)}, u32[]{:S(2)}) collective-permute-start(bf16[21,8,512]{2,1,0:T(8,128)(2,1)S(1)} %add_convert_fusion.5), channel_id=1, source_target_pairs={{0,16},{4,20},{8,24},{12,28},{16,0},{20,4},{24,8},{28,12},{1,17},{... | collective-permute-start | bytes 516104 | tf_op jit(solution)/shard_map/ppermute | solution.py:939
  220.4 71.4 %collective-permute-start.13 = (bf16[1024,768]{1,0:T(8,128)(2,1)}, bf16[1024,768]{1,0:T(8,128)(2,1)S(1)}, u32[]{:S(2)}, u32[]{:S(2)}) collective-permute-start(bf16[1024,768]{1,0:T(8,128)(2,1)} %get-tuple-element.182), channel_id=1, source_target_pairs={{0,1},{1,0},{2,3},{3,2},{4,5},{5,4},{6,7},{7,6},{8,9},{9,8},{10,11... | collective-permute-start | bytes 4718600 | tf_op jit(solution)/shard_map/ppermute | solution.py:935
  220.5 71.4 %collective-permute-start.14 = (bf16[1024,768]{1,0:T(8,128)(2,1)}, bf16[1024,768]{1,0:T(8,128)(2,1)}, u32[]{:S(2)}, u32[]{:S(2)}) collective-permute-start(bf16[1024,768]{1,0:T(8,128)(2,1)} %get-tuple-element.183), channel_id=1, source_target_pairs={{0,1},{1,0},{2,3},{3,2},{4,5},{5,4},{6,7},{7,6},{8,9},{9,8},{10,11... | collective-permute-start | bytes 4718600 | tf_op jit(solution)/shard_map/ppermute | solution.py:935
  221.1 29.6 %collective-permute-start.35 = (bf16[8,48,512]{2,1,0:T(8,128)(2,1)S(1)}, bf16[8,48,512]{2,1,0:T(8,128)(2,1)S(1)}, u32[]{:S(2)}, u32[]{:S(2)}) collective-permute-start(bf16[8,48,512]{2,1,0:T(8,128)(2,1)S(1)} %add_convert_fusion.1), channel_id=1, source_target_pairs={{0,16},{4,20},{8,24},{12,28},{16,0},{20,4},{24,8},{28,12},{1,17},{... | collective-permute-start | bytes 1179656 | tf_op jit(solution)/shard_map/ppermute | solution.py:939
  224.3 14.4 %collective-permute-start.22 = (bf16[25,8,512]{2,1,0:T(8,128)(2,1)}, bf16[25,8,512]{2,1,0:T(8,128)(2,1)S(1)}, u32[]{:S(2)}, u32[]{:S(2)}) collective-permute-start(bf16[25,8,512]{2,1,0:T(8,128)(2,1)} %get-tuple-element.196), channel_id=1, source_target_pairs={{0,8},{4,12},{8,0},{12,4},{16,24},{20,28},{24,16},{28,20},{1,9},{5... | collective-permute-start | bytes 614408 | tf_op jit(solution)/shard_map/ppermute | solution.py:939
  238.2 41.7 %copy-start.5 = (bf16[21,8,512]{2,1,0:T(8,128)(2,1)}, bf16[21,8,512]{2,1,0:T(8,128)(2,1)S(1)}, u32[]{:S(2)}) copy-start(bf16[21,8,512]{2,1,0:T(8,128)(2,1)S(1)} %add_convert_fusion.4.refs_0_) | copy-start | bytes 516100
  238.2 11.0 %collective-permute-start.50 = (bf16[21,8,512]{2,1,0:T(8,128)(2,1)S(1)}, bf16[21,8,512]{2,1,0:T(8,128)(2,1)S(1)}, u32[]{:S(2)}, u32[]{:S(2)}) collective-permute-start(bf16[21,8,512]{2,1,0:T(8,128)(2,1)S(1)} %add_convert_fusion.4.refs_0_), channel_id=1, source_target_pairs={{0,12},{4,8},{8,4},{12,0},{16,28},{20,24},{24,20},{28,16},{1,13},{... | collective-permute-start | bytes 516104 | tf_op jit(solution)/shard_map/ppermute | solution.py:939
  238.7 14.1 %collective-permute-start.49 = (bf16[21,8,512]{2,1,0:T(8,128)(2,1)S(1)}, bf16[21,8,512]{2,1,0:T(8,128)(2,1)S(1)}, u32[]{:S(2)}, u32[]{:S(2)}) collective-permute-start(bf16[21,8,512]{2,1,0:T(8,128)(2,1)S(1)} %add_convert_fusion.4.refs_0_), channel_id=1, source_target_pairs={{0,8},{4,12},{8,0},{12,4},{16,24},{20,28},{24,16},{28,20},{1,9},{5... | collective-permute-start | bytes 516104 | tf_op jit(solution)/shard_map/ppermute | solution.py:939
  249.2 6.2 %collective-permute-start.48 = (bf16[21,8,512]{2,1,0:T(8,128)(2,1)S(1)}, bf16[21,8,512]{2,1,0:T(8,128)(2,1)S(1)}, u32[]{:S(2)}, u32[]{:S(2)}) collective-permute-start(bf16[21,8,512]{2,1,0:T(8,128)(2,1)S(1)} %add_convert_fusion.4.refs_0_), channel_id=1, source_target_pairs={{0,4},{4,0},{8,12},{12,8},{16,20},{20,16},{24,28},{28,24},{1,5},{5... | collective-permute-start | bytes 516104 | tf_op jit(solution)/shard_map/ppermute | solution.py:939
  250.7 12.0 %collective-permute-start.23 = (bf16[25,8,512]{2,1,0:T(8,128)(2,1)S(1)}, bf16[25,8,512]{2,1,0:T(8,128)(2,1)S(1)}, u32[]{:S(2)}, u32[]{:S(2)}) collective-permute-start(bf16[25,8,512]{2,1,0:T(8,128)(2,1)S(1)} %add_convert_fusion.3), channel_id=1, source_target_pairs={{0,16},{4,20},{8,24},{12,28},{16,0},{20,4},{24,8},{28,12},{1,17},{... | collective-permute-start | bytes 614408 | tf_op jit(solution)/shard_map/ppermute | solution.py:939
  250.8 32.1 %copy-start.2 = (bf16[8,48,512]{2,1,0:T(8,128)(2,1)}, bf16[8,48,512]{2,1,0:T(8,128)(2,1)S(1)}, u32[]{:S(2)}) copy-start(bf16[8,48,512]{2,1,0:T(8,128)(2,1)S(1)} %add_convert_fusion.refs_0_) | copy-start | bytes 1179652
  252.8 17.2 %collective-permute-start.38 = (bf16[8,48,512]{2,1,0:T(8,128)(2,1)S(1)}, bf16[8,48,512]{2,1,0:T(8,128)(2,1)S(1)}, u32[]{:S(2)}, u32[]{:S(2)}) collective-permute-start(bf16[8,48,512]{2,1,0:T(8,128)(2,1)S(1)} %add_convert_fusion.refs_0_), channel_id=1, source_target_pairs={{0,12},{4,8},{8,4},{12,0},{16,28},{20,24},{24,20},{28,16},{1,13},{... | collective-permute-start | bytes 1179656 | tf_op jit(solution)/shard_map/ppermute | solution.py:939
  255.4 22.2 %collective-permute-start.37 = (bf16[8,48,512]{2,1,0:T(8,128)(2,1)S(1)}, bf16[8,48,512]{2,1,0:T(8,128)(2,1)S(1)}, u32[]{:S(2)}, u32[]{:S(2)}) collective-permute-start(bf16[8,48,512]{2,1,0:T(8,128)(2,1)S(1)} %add_convert_fusion.refs_0_), channel_id=1, source_target_pairs={{0,8},{4,12},{8,0},{12,4},{16,24},{20,28},{24,16},{28,20},{1,9},{5... | collective-permute-start | bytes 1179656 | tf_op jit(solution)/shard_map/ppermute | solution.py:939
  262.7 15.7 %collective-permute-start.36 = (bf16[8,48,512]{2,1,0:T(8,128)(2,1)S(1)}, bf16[8,48,512]{2,1,0:T(8,128)(2,1)S(1)}, u32[]{:S(2)}, u32[]{:S(2)}) collective-permute-start(bf16[8,48,512]{2,1,0:T(8,128)(2,1)S(1)} %add_convert_fusion.refs_0_), channel_id=1, source_target_pairs={{0,4},{4,0},{8,12},{12,8},{16,20},{20,16},{24,28},{28,24},{1,5},{5... | collective-permute-start | bytes 1179656 | tf_op jit(solution)/shard_map/ppermute | solution.py:939
  263.7 23.4 %copy-start.4 = (bf16[25,8,512]{2,1,0:T(8,128)(2,1)}, bf16[25,8,512]{2,1,0:T(8,128)(2,1)S(1)}, u32[]{:S(2)}) copy-start(bf16[25,8,512]{2,1,0:T(8,128)(2,1)S(1)} %add_convert_fusion.2.refs_0_) | copy-start | bytes 614404
  270.1 17.0 %collective-permute-start.26 = (bf16[25,8,512]{2,1,0:T(8,128)(2,1)S(1)}, bf16[25,8,512]{2,1,0:T(8,128)(2,1)S(1)}, u32[]{:S(2)}, u32[]{:S(2)}) collective-permute-start(bf16[25,8,512]{2,1,0:T(8,128)(2,1)S(1)} %add_convert_fusion.2.refs_0_), channel_id=1, source_target_pairs={{0,12},{4,8},{8,4},{12,0},{16,28},{20,24},{24,20},{28,16},{1,13},{... | collective-permute-start | bytes 614408 | tf_op jit(solution)/shard_map/ppermute | solution.py:939
  277.5 9.5 %collective-permute-start.25 = (bf16[25,8,512]{2,1,0:T(8,128)(2,1)S(1)}, bf16[25,8,512]{2,1,0:T(8,128)(2,1)}, u32[]{:S(2)}, u32[]{:S(2)}) collective-permute-start(bf16[25,8,512]{2,1,0:T(8,128)(2,1)S(1)} %add_convert_fusion.2.refs_0_), channel_id=1, source_target_pairs={{0,8},{4,12},{8,0},{12,4},{16,24},{20,28},{24,16},{28,20},{1,9},{5... | collective-permute-start | bytes 614408 | tf_op jit(solution)/shard_map/ppermute | solution.py:939
  279.2 7.9 %collective-permute-start.24 = (bf16[25,8,512]{2,1,0:T(8,128)(2,1)S(1)}, bf16[25,8,512]{2,1,0:T(8,128)(2,1)}, u32[]{:S(2)}, u32[]{:S(2)}) collective-permute-start(bf16[25,8,512]{2,1,0:T(8,128)(2,1)S(1)} %add_convert_fusion.2.refs_0_), channel_id=1, source_target_pairs={{0,4},{4,0},{8,12},{12,8},{16,20},{20,16},{24,28},{28,24},{1,5},{5... | collective-permute-start | bytes 614408 | tf_op jit(solution)/shard_map/ppermute | solution.py:939
  (35 other events, 158.8 us)

commit v3 on v2

--- a/solution.py
+++ b/solution.py
@@ -164,6 +164,7 @@
         out_specs=VM,
         out_shape=shape(((n + 1) * rows, 2 * wid), BF16),
         name="pack_core",
+        compiler_params=pltpu.CompilerParams(vmem_limit_bytes=12 << 20),
     )(sc, up_weight, query_weight, shared_weight)
 
 
@@ -201,6 +202,7 @@
         + [shape((msg, lanes), BF16)] * 2
         + [shape((msg_a, lanes), BF16)],
         name="pack_rest",
+        compiler_params=pltpu.CompilerParams(vmem_limit_bytes=20 << 20),
     )(sc, up_weight, down_weight, query_weight, shared_weight, output_weight, got)
 
 
@@ -243,6 +245,7 @@
             flops=20 * n_tok * width, bytes_accessed=16 * n_tok * width, transcendentals=0
         ),
         name="norm_pair",
+        compiler_params=pltpu.CompilerParams(vmem_limit_bytes=16 << 20),
     )(tok, dy, *near, *prev)
     return res[:3], res[3], res[4]
 
@@ -408,6 +411,7 @@
             transcendentals=2 * n_tok * wid2,
         ),
         name="mlp_wave",
+        compiler_params=pltpu.CompilerParams(vmem_limit_bytes=36 << 20),
     )(sc, nm, dy, down_own, vec, *srcs, *extra, *prev)
 
 
@@ -601,6 +605,7 @@
             transcendentals=length * length * wh // 64,
         ),
         name="attention",
+        compiler_params=pltpu.CompilerParams(vmem_limit_bytes=40 << 20),
     )(sc, na, dy, vec, waves_of, seg_rows, cgrad, *weights)
 
 
@@ -686,6 +691,7 @@
             flops=2 * total * width * (wq + wh), bytes_accessed=4 * total * width, transcendentals=0
         ),
         name="attn_terms",
+        compiler_params=pltpu.CompilerParams(vmem_limit_bytes=28 << 20),
     )(sc, na, dy, o_all, gqs_all, wqs, vec, sums, ob, *ubs, *rss)
 
 
@@ -790,6 +796,7 @@
             flops=8 * sets * total * lanes, bytes_accessed=10 * sets * total * lanes, transcendentals=0
         ),
         name="first_sum",
+        compiler_params=pltpu.CompilerParams(vmem_limit_bytes=14 << 20),
     )(sc, *msgs)
 
 
@@ -831,6 +838,7 @@
         scratch_shapes=[pltpu.VMEM((width, wid), F32)],
         cost_estimate=pl.CostEstimate(flops=0, bytes_accessed=12 * part * ff, transcendentals=0),
         name="early_grads",
+        compiler_params=pltpu.CompilerParams(vmem_limit_bytes=18 << 20),
     )(sc, *pieces)
 
 
@@ -898,6 +906,7 @@
         input_output_aliases={1 + n_p + i: i for i in range(len(prev))},
         cost_estimate=pl.CostEstimate(flops=0, bytes_accessed=4 * part * ff, transcendentals=0),
         name="late_grads",
+        compiler_params=pltpu.CompilerParams(vmem_limit_bytes=10 << 20),
     )(sc, *pieces, *prev)
 
 
@@ -928,6 +937,7 @@
         scratch_shapes=[pltpu.VMEM((planes * high, wq), F32)],
         cost_estimate=pl.CostEstimate(flops=0, bytes_accessed=12 * part * width, transcendentals=0),
         name="attn_grads",
+        compiler_params=pltpu.CompilerParams(vmem_limit_bytes=10 << 20),
     )(sc, *pieces)
 
 

time: 308 us -> 297 us (0.964)
  Pallas kernels: 159 us -> 128 us
  local copies, waits for them, and re-layouts: 6.01 us -> 23.5 us
  waiting for transfers between devices: 90.9 us -> 97.4 us
    unnamed x96 -> x94, local copies, waits for them, and re-layouts: 6 us -> 23.4 us
    pallas_call x3, Pallas kernels: 39.2 us -> 30.7 us  [mlp_wave(): pl.pallas_call(kern, grid=(4,), in_specs=[SMEM, row, row] + [fixed((wid,...]
    pallas_call x3, Pallas kernels: 8.38 us -> 3.03 us  [first_sum(): pl.pallas_call(kern, in_specs=[SMEM] + [VM] * 8, out_specs=[VM, VM], out_...]
    ppermute x15, waiting for transfers between devices: 44.9 us -> 50.2 us  [to_replica(): return lax.ppermute(value, 'replica', [(r, r ^ k) for r in range(count)])]
    pallas_call x2, Pallas kernels: 9.34 us -> 5.58 us  [norm_pair(): pl.pallas_call(kern, grid=(2,), in_specs=[src, src] + [small] * n_near +...]
    pallas_call x1, Pallas kernels: 44.7 us -> 41.1 us  [attention(): pl.pallas_call(kern, grid=(2,), in_specs=[SMEM, seq(width), seq(width), f...]
    pallas_call x1, Pallas kernels: 9.73 us -> 6.48 us  [attn_terms(): pl.pallas_call(kern, grid=(4,), in_specs=[SMEM, row, row, pl.BlockSpec((b...]
  transfers between devices with their start and end apart: 51 -> 51, of which waited for: 17 -> 20; matrix products, arithmetic and copies ran while one was open for 2% -> 1% of each run, Pallas kernels for 47% -> 38%
where the time goes in v3:
time: 297 us
  Pallas kernels  128 us (43%)
  waiting for transfers between devices  97.4 us (33%)
  starting transfers between devices  43.9 us (15%)
  local copies, waits for them, and re-layouts  23.5 us (8%)
  other arithmetic  3.02 us (1%)
    ppermute x15, waiting for transfers between devices, to_replica(): return lax.ppermute(value, 'replica', [(r, r ^ k) for r in range(count)])  50.2 us
    pallas_call x1, Pallas kernels, attention(): pl.pallas_call(kern, grid=(2,), in_specs=[SMEM, seq(width), seq(width), f...  41.1 us
    pallas_call x3, Pallas kernels, mlp_wave(): pl.pallas_call(kern, grid=(4,), in_specs=[SMEM, row, row] + [fixed((wid,...  30.7 us
    ppermute x15, waiting for transfers between devices, to_shard(): return lax.ppermute(value, 'shard', [(s, s ^ k) for s in range(4)])  28.4 us
    pallas_call x2, Pallas kernels, outputs(): pl.pallas_call(kern, grid=(4,), in_specs=[rows(wid2)] * (2 * n_w) + [fixe...  25.7 us
    unnamed x94, local copies, waits for them, and re-layouts  23.4 us
    ppermute x21, starting transfers between devices, to_group(): return lax.ppermute(value, ('replica', 'shard'), pairs)  21.4 us
    ppermute x21, waiting for transfers between devices, to_group(): return lax.ppermute(value, ('replica', 'shard'), pairs)  18.9 us
  transfers between devices with their start and end apart: 51, of which 20 were waited for; matrix products, arithmetic and copies ran while one was open for 1% of the time, Pallas kernels for 38%

profile of v3, /device:TPU:0, one launch (start us, length us, event | category | flops | bytes accessed | tf_op | source)
XLA Modules:
  0.0 297.0 jit_solution(6425622957413541470)
XLA Ops:
  1.8 1.6 pack_small.1.refs_0_
  3.5 2.6 pack_first.1
  7.6 2.6 collective-permute-start.4
  10.5 1.3 collective-permute-done.4.refs_3_
  12.1 1.9 collective-permute-done.3.refs_2_
  14.6 1.9 norm_pair.2
  17.3 1.8 pack_rest.1
  19.1 1.4 collective-permute-start.9
  21.0 3.7 %norm_pair.3 = (bf16[2048,768]{1,0:T(8,128)(2,1)S(1)}, bf16[2048,768]{1,0:T(8,128)(2,1)S(1)}, bf16[2048,768]{1,0:T(8,128)(2,1)S(1)}, f32[8,768]{1,0:T(8,128)}, f32[16,768]{1,0:T(8,128)}) custom-call(bf16[1024,768]{1,0:T(8,128)(2,1)} %collective-permute-done.tok_ref, ...), custom_call_target="tpu_custom_call", output_to_operand_aliasing={{0}: (6, {}), {1}: (7, {}), {2}: (8, {})} | custom-call | flops 15728640 | bytes 12582912 | tf_op jit(solution)/shard_map/norm_pair/pallas_call | solution.py:236
  24.7 1.6 copy-done.6
  26.3 23.4 %collective-permute-done.9.refs_2_ = bf16[768,512]{1,0:T(8,128)(2,1)S(1)} collective-permute-done((bf16[768,512]{1,0:T(8,128)(2,1)S(1)}, bf16[768,512]{1,0:T(8,128)(2,1)S(1)}, u32[]{:S(2)}, u32[]{:S(2)}) %collective-permute-start.9) | collective-permute-done | bytes 786464 | tf_op jit(solution)/shard_map/ppermute | solution.py:945
  50.3 1.7 collective-permute-done.7.refs_3_
  52.1 1.9 copy-done.7
  54.0 10.2 %mlp_wave.3 = (bf16[2048,512]{1,0:T(8,128)(2,1)S(1)}, bf16[2048,512]{1,0:T(8,128)(2,1)S(1)}, bf16[768,512]{1,0:T(8,128)(2,1)S(1)}, bf16[512,768]{1,0:T(8,128)(2,...) custom-call(s32[3]{0:T(128)S(1)} %copy-done.28, ...), custom_call_target="tpu_custom_call" | custom-call | flops 6442450944 | bytes 15728640 | tf_op jit(solution)/shard_map/mlp_wave/pallas_call | solution.py:388
  64.2 1.3 copy-done.10
  65.5 1.3 copy-done.11
  68.7 10.2 %mlp_wave.4 = (bf16[2048,512]{1,0:T(8,128)(2,1)S(1)}, bf16[2048,512]{1,0:T(8,128)(2,1)S(1)}, bf16[768,512]{1,0:T(8,128)(2,1)S(1)}, bf16[512,768]{1,0:T(8,128)(2,...) custom-call(s32[3]{0:T(128)S(1)} %copy-done.28, ...), custom_call_target="tpu_custom_call", output_to_operand_aliasing={{6}: (8, {}), {7}: (9, {}), {8}: (10, {}), {9}: (11, {}), {... | custom-call | flops 6442450944 | bytes 15728640 | tf_op jit(solution)/shard_map/mlp_wave/pallas_call | solution.py:388
  78.9 1.3 copy-done.12
  80.2 1.4 copy-done.13
  82.5 0.9 copy-done.20
  86.5 1.4 collective-permute-start.11
  87.9 1.1 copy-done.30
  89.0 41.1 %attention.1 = (bf16[2048,384]{1,0:T(8,128)(2,1)S(1)}, bf16[2048,512]{1,0:T(8,128)(2,1)S(1)}, bf16[1024,128]{1,0:T(8,128)(2,1)}, f32[8,512]{1,0:T(8,128)S(1)}, b...) custom-call(s32[3]{0:T(128)S(1)} %copy-done.28, bf16[2048,768]{1,0:T(8,128)(2,1)S(1)} %get-tuple-element.159.na_r, ...), custom_call_target="tpu_custom_call" | custom-call | flops 12482248704 | bytes 9437184 | tf_op jit(solution)/shard_map/attention/pallas_call | solution.py:581
  130.1 6.5 %attn_terms.1 = (bf16[240,512]{1,0:T(8,128)(2,1)S(1)}, bf16[240,512]{1,0:T(8,128)(2,1)S(1)}, bf16[96,512]{1,0:T(8,128)(2,1)S(1)}, bf16[96,512]{1,0:T(8,128)(2,1)...) custom-call(s32[3]{0:T(128)S(1)} %copy-done.28, ...), custom_call_target="tpu_custom_call" | custom-call | flops 2818572288 | bytes 6291456 | tf_op jit(solution)/shard_map/attn_terms/pallas_call | solution.py:676
  137.3 1.5 collective-permute-start.39
  138.8 1.4 collective-permute-start.42
  141.1 5.4 %collective-permute-done.41.refs_3_ = bf16[96,512]{1,0:T(8,128)(2,1)S(1)} collective-permute-done((bf16[96,512]{1,0:T(8,128)(2,1)S(1)}, bf16[96,512]{1,0:T(8,128)(2,1)S(1)}, u32[]{:S(2)}, u32[]{:S(2)}) %collective-permute-start.41) | collective-permute-done | bytes 98336 | tf_op jit(solution)/shard_map/ppermute | solution.py:962
  146.5 2.6 collective-permute-start.45
  150.0 2.3 collective-permute-done.45.refs_7_
  152.3 2.8 collective-permute-start.33
  155.5 3.5 %collective-permute-done.43.refs_5_ = bf16[240,512]{1,0:T(8,128)(2,1)S(1)} collective-permute-done((bf16[240,512]{1,0:T(8,128)(2,1)S(1)}, bf16[240,512]{1,0:T(8,128)(2,1)S(1)}, u32[]{:S(2)}, u32[]{:S(2)}) %collective-permute-start.43) | collective-permute-done | bytes 245792 | tf_op jit(solution)/shard_map/ppermute | solution.py:962
  159.8 2.0 collective-permute-done.33.refs_7_
  161.8 1.7 collective-permute-start.31
  163.5 2.8 collective-permute-done.32.refs_6_
  166.3 1.4 collective-permute-start.30
  167.7 1.3 collective-permute-start.27
  169.0 1.6 collective-permute-start.46
  170.6 1.9 copy-done.8
  172.5 10.2 %mlp_wave.5 = (bf16[2048,512]{1,0:T(8,128)(2,1)S(1)}, bf16[2048,512]{1,0:T(8,128)(2,1)S(1)}, bf16[768,512]{1,0:T(8,128)(2,1)S(1)}, bf16[512,768]{1,0:T(8,128)(2,...) custom-call(s32[3]{0:T(128)S(1)} %copy-done.28, ...), custom_call_target="tpu_custom_call" | custom-call | flops 6442450944 | bytes 15728640 | tf_op jit(solution)/shard_map/mlp_wave/pallas_call | solution.py:388
  182.7 1.3 copy-done.14
  184.0 1.3 copy-done.15
  189.0 2.8 collective-permute-done.30.refs_4_
  191.9 1.3 first_sum.4
  193.1 1.6 collective-permute-start.34
  194.8 1.3 collective-permute-start.21
  197.6 2.0 collective-permute-start.19
  199.6 11.9 %outputs.2 = (bf16[1024,768]{1,0:T(8,128)(2,1)}, bf16[1024,768]{1,0:T(8,128)(2,1)}) custom-call(bf16[2048,512]{1,0:T(8,128)(2,1)} %copy-done.10, bf16[2048,512]{1,0:T(8,128)(2,1)} %copy-done.12, bf16[2048,512]{1,0:T(8,128)(2,1)} %copy-done.14, bf16[2048,512]{1,0:T(8,128)(2,1)} %copy-done.11, bf16[2048,512]{1,0:T(8,128)(2,1)} %copy-done.13, ...), custom_call_target="tpu_custom_call" | custom-call | flops 6247415808 | bytes 18874368 | tf_op jit(solution)/shard_map/outputs/pallas_call | solution.py:737
  211.6 2.7 collective-permute-start.47
  214.7 1.1 add_convert_fusion.1
  217.7 13.4 %collective-permute-done.47 = bf16[21,8,512]{2,1,0:T(8,128)(2,1)S(1)} collective-permute-done((bf16[21,8,512]{2,1,0:T(8,128)(2,1)}, bf16[21,8,512]{2,1,0:T(8,128)(2,1)S(1)}, u32[]{:S(2)}, u32[]{:S(2)}) %collective-permute-start.47) | collective-permute-done | bytes 172064 | tf_op jit(solution)/shard_map/ppermute | solution.py:949
  231.2 0.9 collective-permute-start.50
  232.1 1.5 collective-permute-start.49
  233.6 9.7 %collective-permute-done.50.refs_3_ = bf16[21,8,512]{2,1,0:T(8,128)(2,1)S(1)} collective-permute-done((bf16[21,8,512]{2,1,0:T(8,128)(2,1)S(1)}, bf16[21,8,512]{2,1,0:T(8,128)(2,1)S(1)}, u32[]{:S(2)}, u32[]{:S(2)}) %collective-permute-start.50) | collective-permute-done | bytes 172064 | tf_op jit(solution)/shard_map/ppermute | solution.py:949
  243.3 1.4 collective-permute-start.48
  244.8 2.0 collective-permute-done.49.refs_2_
  246.8 1.3 collective-permute-start.38
  248.1 1.4 collective-permute-done.48.refs_1_
  249.5 7.1 %collective-permute-done.23 = bf16[25,8,512]{2,1,0:T(8,128)(2,1)S(1)} collective-permute-done((bf16[25,8,512]{2,1,0:T(8,128)(2,1)S(1)}, bf16[25,8,512]{2,1,0:T(8,128)(2,1)S(1)}, u32[]{:S(2)}, u32[]{:S(2)}) %collective-permute-start.23) | collective-permute-done | bytes 204832 | tf_op jit(solution)/shard_map/ppermute | solution.py:949
  257.4 6.7 %collective-permute-done.38.refs_3_ = bf16[8,48,512]{2,1,0:T(8,128)(2,1)S(1)} collective-permute-done((bf16[8,48,512]{2,1,0:T(8,128)(2,1)S(1)}, bf16[8,48,512]{2,1,0:T(8,128)(2,1)S(1)}, u32[]{:S(2)}, u32[]{:S(2)}) %collective-permute-start.38) | collective-permute-done | bytes 393248 | tf_op jit(solution)/shard_map/ppermute | solution.py:949
  264.0 7.6 %collective-permute-done.37.refs_2_ = bf16[8,48,512]{2,1,0:T(8,128)(2,1)S(1)} collective-permute-done((bf16[8,48,512]{2,1,0:T(8,128)(2,1)S(1)}, bf16[8,48,512]{2,1,0:T(8,128)(2,1)S(1)}, u32[]{:S(2)}, u32[]{:S(2)}) %collective-permute-start.37) | collective-permute-done | bytes 393248 | tf_op jit(solution)/shard_map/ppermute | solution.py:949
  273.0 2.4 attn_grads.1
  275.5 3.3 %early_grads.1 = (f32[192,3072]{1,0:T(8,128)}, f32[768,768]{1,0:T(8,128)}) custom-call(s32[3]{0:T(128)S(1)} %copy-done.28, bf16[8,48,512]{2,1,0:T(8,128)(2,1)S(1)} %add_convert_fusion.refs_0_, bf16[8,48,512]{2,1,0:T(8,128)(2,1)S(1)} %collective-permute-done.36.refs_1_, bf16[8,48,512]{2,1,0:T(8,128)(2,1)S(1)} %collective-permute-done.37.refs_2_, ...), custom_call_target="tpu_custom_call" | custom-call | bytes 7077888 | tf_op jit(solution)/shard_map/early_grads/pallas_call | solution.py:833
  280.3 2.8 late_grads.1
  283.1 13.7 %outputs.3 = (bf16[1024,768]{1,0:T(8,128)(2,1)}, bf16[1024,768]{1,0:T(8,128)(2,1)}) custom-call(bf16[2048,512]{1,0:T(8,128)(2,1)} %copy-done.10, bf16[2048,512]{1,0:T(8,128)(2,1)} %copy-done.12, bf16[2048,512]{1,0:T(8,128)(2,1)} %copy-done.14, bf16[2048,512]{1,0:T(8,128)(2,1)} %copy-done.11, bf16[2048,512]{1,0:T(8,128)(2,1)} %copy-done.13, ...), custom_call_target="tpu_custom_call" | custom-call | flops 6247415808 | bytes 18874368 | tf_op jit(solution)/shard_map/outputs/pallas_call | solution.py:737
  (165 shorter events, 26.4 us)
Async XLA Ops:
  0.7 20.2 %collective-permute-start = (bf16[1024,768]{1,0:T(8,128)(2,1)}, bf16[1024,768]{1,0:T(8,128)(2,1)}, u32[]{:S(2)}, u32[]{:S(2)}) collective-permute-start(bf16[1024,768]{1,0:T(8,128)(2,1)} %refs_17_.1), channel_id=1, source_target_pairs={{0,1},{1,0},{2,3},{3,2},{4,5},{5,4},{6,7},{7,6},{8,9},{9,8},{10,11... | collective-permute-start | bytes 4718600 | tf_op jit(solution)/shard_map/ppermute | solution.py:945
  3.5 11.2 %copy-start.3 = (bf16[1024,768]{1,0:T(8,128)(2,1)S(1)}, bf16[1024,768]{1,0:T(8,128)(2,1)}, u32[]{:S(2)}) copy-start(bf16[1024,768]{1,0:T(8,128)(2,1)} %refs_17_.1) | copy-start | bytes 4718596
  6.0 8.0 %copy-start.46 = (bf16[192,512]{1,0:T(8,128)(2,1)S(1)}, bf16[192,512]{1,0:T(8,128)(2,1)}, u32[]{:S(2)}) copy-start(bf16[192,512]{1,0:T(8,128)(2,1)} %get-tuple-element.137) | copy-start | bytes 589828
  7.0 9.6 %copy-start.44 = (bf16[576,512]{1,0:T(8,128)(2,1)S(1)}, bf16[576,512]{1,0:T(8,128)(2,1)}, u32[]{:S(2)}) copy-start(bf16[576,512]{1,0:T(8,128)(2,1)} %get-tuple-element.138) | copy-start | bytes 1769476
  7.0 10.3 %copy-start.5 = (bf16[768,768]{1,0:T(8,128)(2,1)S(1)}, bf16[768,768]{1,0:T(8,128)(2,1)}, u32[]{:S(2)}) copy-start(bf16[768,768]{1,0:T(8,128)(2,1)} %d0.5) | copy-start | bytes 3538948
  7.0 10.3 %copy-start.24 = (bf16[192,768]{1,0:T(8,128)(2,1)S(1)}, bf16[192,768]{1,0:T(8,128)(2,1)}, u32[]{:S(2)}) copy-start(bf16[192,768]{1,0:T(8,128)(2,1)} %refs_3_.3) | copy-start | bytes 884740
  7.0 9.6 %collective-permute-start.8 = (bf16[960,512]{1,0:T(8,128)(2,1)S(1)}, bf16[960,512]{1,0:T(8,128)(2,1)S(1)}, u32[]{:S(2)}, u32[]{:S(2)}) collective-permute-start(bf16[960,512]{1,0:T(8,128)(2,1)S(1)} %pack_core.1), channel_id=1, source_target_pairs={{0,1},{1,0},{2,3},{3,2},{4,5},{5,4},{6,7},{7,6},{8,9},{9,8},{10,11... | collective-permute-start | bytes 2949128 | tf_op jit(solution)/shard_map/ppermute | solution.py:945
  7.4 13.6 %collective-permute-start.1 = (bf16[1024,768]{1,0:T(8,128)(2,1)S(1)}, bf16[1024,768]{1,0:T(8,128)(2,1)S(1)}, u32[]{:S(2)}, u32[]{:S(2)}) collective-permute-start(bf16[1024,768]{1,0:T(8,128)(2,1)S(1)} %copy-done.4), channel_id=1, source_target_pairs={{0,1},{1,0},{2,3},{3,2},{4,5},{5,4},{6,7},{7,6},{8,9},{9,8},{10,11... | collective-permute-start | bytes 4718600 | tf_op jit(solution)/shard_map/ppermute | solution.py:945
  7.6 4.2 %collective-permute-start.4 = (bf16[16,768]{1,0:T(8,128)(2,1)S(1)}, bf16[16,768]{1,0:T(8,128)(2,1)S(1)}, u32[]{:S(2)}, u32[]{:S(2)}) collective-permute-start(bf16[16,768]{1,0:T(8,128)(2,1)S(1)} %copy-done.25), channel_id=1, source_target_pairs={{0,3},{1,2},{2,1},{3,0},{4,7},{5,6},{6,5},{7,4},{8,11},{9,10},{10,... | collective-permute-start | bytes 73736 | tf_op jit(solution)/shard_map/ppermute | solution.py:945
  10.2 3.8 %collective-permute-start.3 = (bf16[16,768]{1,0:T(8,128)(2,1)S(1)}, bf16[16,768]{1,0:T(8,128)(2,1)S(1)}, u32[]{:S(2)}, u32[]{:S(2)}) collective-permute-start(bf16[16,768]{1,0:T(8,128)(2,1)S(1)} %copy-done.25), channel_id=1, source_target_pairs={{0,2},{1,3},{2,0},{3,1},{4,6},{5,7},{6,4},{7,5},{8,10},{9,11},{10,... | collective-permute-start | bytes 73736 | tf_op jit(solution)/shard_map/ppermute | solution.py:945
  11.8 2.3 collective-permute-start.2
  14.0 5.1 %collective-permute-start.12 = (s32[2,1024]{1,0:T(2,128)S(1)}, s32[2,1024]{1,0:T(2,128)S(1)}, u32[]{:S(2)}, u32[]{:S(2)}) collective-permute-start(s32[2,1024]{1,0:T(2,128)S(1)} %pad_add_fusion), channel_id=1, source_target_pairs={{0,1},{1,0},{2,3},{3,2},{4,5},{5,4},{6,7},{7,6},{8,9},{9,8},{10,11... | collective-permute-start | bytes 24584 | tf_op jit(solution)/shard_map/ppermute | solution.py:945
  14.1 36.3 %collective-permute-start.5 = (bf16[192,512]{1,0:T(8,128)(2,1)S(1)}, bf16[192,512]{1,0:T(8,128)(2,1)S(1)}, u32[]{:S(2)}, u32[]{:S(2)}) collective-permute-start(bf16[192,512]{1,0:T(8,128)(2,1)S(1)} %copy-done.46), channel_id=1, source_target_pairs={{0,1},{1,0},{2,3},{3,2},{4,5},{5,4},{6,7},{7,6},{8,9},{9,8},{10,11... | collective-permute-start | bytes 589832 | tf_op jit(solution)/shard_map/ppermute | solution.py:945
  16.6 154.0 %copy-start.27 = (f32[16,768]{1,0:T(8,128)}, f32[16,768]{1,0:T(8,128)S(1)}, u32[]{:S(2)}) copy-start(f32[16,768]{1,0:T(8,128)S(1)} %get-tuple-element.134.vec_r.refs_16_) | copy-start | bytes 147460
  16.6 35.5 %collective-permute-start.6 = (bf16[576,512]{1,0:T(8,128)(2,1)S(1)}, bf16[576,512]{1,0:T(8,128)(2,1)S(1)}, u32[]{:S(2)}, u32[]{:S(2)}) collective-permute-start(bf16[576,512]{1,0:T(8,128)(2,1)S(1)} %copy-done.44), channel_id=1, source_target_pairs={{0,2},{1,3},{2,0},{3,1},{4,6},{5,7},{6,4},{7,5},{8,10},{9,11},{10,... | collective-permute-start | bytes 1769480 | tf_op jit(solution)/shard_map/ppermute | solution.py:945
  19.1 30.6 %collective-permute-start.9 = (bf16[768,512]{1,0:T(8,128)(2,1)S(1)}, bf16[768,512]{1,0:T(8,128)(2,1)S(1)}, u32[]{:S(2)}, u32[]{:S(2)}) collective-permute-start(bf16[768,512]{1,0:T(8,128)(2,1)S(1)} %get-tuple-element.144), channel_id=1, source_target_pairs={{0,2},{1,3},{2,0},{3,1},{4,6},{5,7},{6,4},{7,5},{8,10},{9,11},{10,... | collective-permute-start | bytes 2359304 | tf_op jit(solution)/shard_map/ppermute | solution.py:945
  20.9 31.2 %collective-permute-start.7 = (bf16[192,512]{1,0:T(8,128)(2,1)S(1)}, bf16[192,512]{1,0:T(8,128)(2,1)S(1)}, u32[]{:S(2)}, u32[]{:S(2)}) collective-permute-start(bf16[192,512]{1,0:T(8,128)(2,1)S(1)} %copy-done.45), channel_id=1, source_target_pairs={{0,3},{1,2},{2,1},{3,0},{4,7},{5,6},{6,5},{7,4},{8,11},{9,10},{10,... | collective-permute-start | bytes 589832 | tf_op jit(solution)/shard_map/ppermute | solution.py:945
  21.0 31.1 %copy-start.36 = (bf16[192,512]{1,0:T(8,128)(2,1)S(1)}, bf16[192,512]{1,0:T(8,128)(2,1)}, u32[]{:S(2)}) copy-start(bf16[192,512]{1,0:T(8,128)(2,1)} %get-tuple-element.136.refs_0_) | copy-start | bytes 589828
  49.7 35.9 %collective-permute-start.10 = (bf16[672,512]{1,0:T(8,128)(2,1)S(1)}, bf16[672,512]{1,0:T(8,128)(2,1)S(1)}, u32[]{:S(2)}, u32[]{:S(2)}) collective-permute-start(bf16[672,512]{1,0:T(8,128)(2,1)S(1)} %get-tuple-element.157), channel_id=1, source_target_pairs={{0,2},{1,3},{2,0},{3,1},{4,6},{5,7},{6,4},{7,5},{8,10},{9,11},{10,... | collective-permute-start | bytes 2064392 | tf_op jit(solution)/shard_map/ppermute | solution.py:945
  68.7 19.2 %copy-start.33 = (bf16[1024,128]{1,0:T(8,128)(2,1)S(1)}, bf16[1024,128]{1,0:T(8,128)(2,1)}, u32[]{:S(2)}) copy-start(bf16[1024,128]{1,0:T(8,128)(2,1)} %cg_r.1) | copy-start | bytes 786436
  86.5 82.6 %collective-permute-start.11 = (bf16[768,512]{1,0:T(8,128)(2,1)}, bf16[768,512]{1,0:T(8,128)(2,1)S(1)}, u32[]{:S(2)}, u32[]{:S(2)}) collective-permute-start(bf16[768,512]{1,0:T(8,128)(2,1)} %get-tuple-element.158), channel_id=1, source_target_pairs={{0,2},{1,3},{2,0},{3,1},{4,6},{5,7},{6,4},{7,5},{8,10},{9,11},{10,... | collective-permute-start | bytes 2359304 | tf_op jit(solution)/shard_map/ppermute | solution.py:945
  130.1 22.2 %copy-start.40 = (bf16[192,512]{1,0:T(8,128)(2,1)S(1)}, bf16[192,512]{1,0:T(8,128)(2,1)}, u32[]{:S(2)}) copy-start(bf16[192,512]{1,0:T(8,128)(2,1)} %copy-done.39) | copy-start | bytes 589828
  130.1 25.0 %copy-start.38 = (bf16[192,512]{1,0:T(8,128)(2,1)S(1)}, bf16[192,512]{1,0:T(8,128)(2,1)}, u32[]{:S(2)}) copy-start(bf16[192,512]{1,0:T(8,128)(2,1)} %copy-done.37) | copy-start | bytes 589828
  130.1 36.2 %copy-start.32 = (bf16[576,512]{1,0:T(8,128)(2,1)S(1)}, bf16[576,512]{1,0:T(8,128)(2,1)}, u32[]{:S(2)}) copy-start(bf16[576,512]{1,0:T(8,128)(2,1)} %copy-done.31) | copy-start | bytes 1769476
  130.1 40.5 %copy-start.35 = (bf16[192,512]{1,0:T(8,128)(2,1)S(1)}, bf16[192,512]{1,0:T(8,128)(2,1)}, u32[]{:S(2)}) copy-start(bf16[192,512]{1,0:T(8,128)(2,1)} %copy-done.34) | copy-start | bytes 589828
  136.7 3.6 %collective-permute-start.40 = (bf16[96,512]{1,0:T(8,128)(2,1)S(1)}, bf16[96,512]{1,0:T(8,128)(2,1)S(1)}, u32[]{:S(2)}, u32[]{:S(2)}) collective-permute-start(bf16[96,512]{1,0:T(8,128)(2,1)S(1)} %get-tuple-element.221), channel_id=1, source_target_pairs={{0,1},{1,0},{2,3},{3,2},{4,5},{5,4},{6,7},{7,6},{8,9},{9,8},{10,11... | collective-permute-start | bytes 294920 | tf_op jit(solution)/shard_map/ppermute | solution.py:962
  137.3 17.8 %collective-permute-start.39 = (bf16[240,512]{1,0:T(8,128)(2,1)S(1)}, bf16[240,512]{1,0:T(8,128)(2,1)S(1)}, u32[]{:S(2)}, u32[]{:S(2)}) collective-permute-start(bf16[240,512]{1,0:T(8,128)(2,1)S(1)} %get-tuple-element.220), channel_id=1, source_target_pairs={{0,4},{1,5},{2,6},{3,7},{4,0},{5,1},{6,2},{7,3},{8,12},{9,13},{10,... | collective-permute-start | bytes 737288 | tf_op jit(solution)/shard_map/ppermute | solution.py:962
  138.8 16.3 %collective-permute-start.42 = (bf16[240,512]{1,0:T(8,128)(2,1)S(1)}, bf16[240,512]{1,0:T(8,128)(2,1)S(1)}, u32[]{:S(2)}, u32[]{:S(2)}) collective-permute-start(bf16[240,512]{1,0:T(8,128)(2,1)S(1)} %get-tuple-element.223), channel_id=1, source_target_pairs={{0,2},{1,3},{2,0},{3,1},{4,6},{5,7},{6,4},{7,5},{8,10},{9,11},{10,... | collective-permute-start | bytes 737288 | tf_op jit(solution)/shard_map/ppermute | solution.py:962
  140.2 6.3 %collective-permute-start.41 = (bf16[96,512]{1,0:T(8,128)(2,1)S(1)}, bf16[96,512]{1,0:T(8,128)(2,1)S(1)}, u32[]{:S(2)}, u32[]{:S(2)}) collective-permute-start(bf16[96,512]{1,0:T(8,128)(2,1)S(1)} %get-tuple-element.222), channel_id=1, source_target_pairs={{0,5},{1,4},{2,7},{3,6},{4,1},{5,0},{6,3},{7,2},{8,13},{9,12},{10,... | collective-permute-start | bytes 294920 | tf_op jit(solution)/shard_map/ppermute | solution.py:962
  140.2 8.9 %collective-permute-start.44 = (bf16[96,512]{1,0:T(8,128)(2,1)S(1)}, bf16[96,512]{1,0:T(8,128)(2,1)S(1)}, u32[]{:S(2)}, u32[]{:S(2)}) collective-permute-start(bf16[96,512]{1,0:T(8,128)(2,1)S(1)} %get-tuple-element.225), channel_id=1, source_target_pairs={{0,3},{1,2},{2,1},{3,0},{4,7},{5,6},{6,5},{7,4},{8,11},{9,10},{10,... | collective-permute-start | bytes 294920 | tf_op jit(solution)/shard_map/ppermute | solution.py:962
  146.5 5.8 %collective-permute-start.45 = (bf16[96,512]{1,0:T(8,128)(2,1)S(1)}, bf16[96,512]{1,0:T(8,128)(2,1)S(1)}, u32[]{:S(2)}, u32[]{:S(2)}) collective-permute-start(bf16[96,512]{1,0:T(8,128)(2,1)S(1)} %get-tuple-element.226), channel_id=1, source_target_pairs={{0,7},{1,6},{2,5},{3,4},{4,3},{5,2},{6,1},{7,0},{8,15},{9,14},{10,... | collective-permute-start | bytes 294920 | tf_op jit(solution)/shard_map/ppermute | solution.py:962
  149.1 9.8 %collective-permute-start.43 = (bf16[240,512]{1,0:T(8,128)(2,1)S(1)}, bf16[240,512]{1,0:T(8,128)(2,1)S(1)}, u32[]{:S(2)}, u32[]{:S(2)}) collective-permute-start(bf16[240,512]{1,0:T(8,128)(2,1)S(1)} %get-tuple-element.224), channel_id=1, source_target_pairs={{0,6},{1,7},{2,4},{3,5},{4,2},{5,3},{6,0},{7,1},{8,14},{9,15},{10,... | collective-permute-start | bytes 737288 | tf_op jit(solution)/shard_map/ppermute | solution.py:962
  152.3 9.5 %collective-permute-start.33 = (bf16[192,512]{1,0:T(8,128)(2,1)S(1)}, bf16[192,512]{1,0:T(8,128)(2,1)S(1)}, u32[]{:S(2)}, u32[]{:S(2)}) collective-permute-start(bf16[192,512]{1,0:T(8,128)(2,1)S(1)} %copy-done.40), channel_id=1, source_target_pairs={{0,7},{1,6},{2,5},{3,4},{4,3},{5,2},{6,1},{7,0},{8,15},{9,14},{10,... | collective-permute-start | bytes 589832 | tf_op jit(solution)/shard_map/ppermute | solution.py:962
  155.1 11.2 %collective-permute-start.32 = (bf16[192,512]{1,0:T(8,128)(2,1)S(1)}, bf16[192,512]{1,0:T(8,128)(2,1)S(1)}, u32[]{:S(2)}, u32[]{:S(2)}) collective-permute-start(bf16[192,512]{1,0:T(8,128)(2,1)S(1)} %copy-done.38), channel_id=1, source_target_pairs={{0,3},{1,2},{2,1},{3,0},{4,7},{5,6},{6,5},{7,4},{8,11},{9,10},{10,... | collective-permute-start | bytes 589832 | tf_op jit(solution)/shard_map/ppermute | solution.py:962
  155.1 12.6 %collective-permute-start.29 = (bf16[192,512]{1,0:T(8,128)(2,1)S(1)}, bf16[192,512]{1,0:T(8,128)(2,1)S(1)}, u32[]{:S(2)}, u32[]{:S(2)}) collective-permute-start(bf16[192,512]{1,0:T(8,128)(2,1)S(1)} %get-tuple-element.204), channel_id=1, source_target_pairs={{0,5},{1,4},{2,7},{3,6},{4,1},{5,0},{6,3},{7,2},{8,13},{9,12},{10,... | collective-permute-start | bytes 589832 | tf_op jit(solution)/shard_map/ppermute | solution.py:962
  159.0 28.2 %collective-permute-start.28 = (bf16[192,512]{1,0:T(8,128)(2,1)}, bf16[192,512]{1,0:T(8,128)(2,1)S(1)}, u32[]{:S(2)}, u32[]{:S(2)}) collective-permute-start(bf16[192,512]{1,0:T(8,128)(2,1)} %get-tuple-element.202), channel_id=1, source_target_pairs={{0,1},{1,0},{2,3},{3,2},{4,5},{5,4},{6,7},{7,6},{8,9},{9,8},{10,11... | collective-permute-start | bytes 589832 | tf_op jit(solution)/shard_map/ppermute | solution.py:962
  161.8 26.2 %collective-permute-start.31 = (bf16[576,512]{1,0:T(8,128)(2,1)}, bf16[576,512]{1,0:T(8,128)(2,1)S(1)}, u32[]{:S(2)}, u32[]{:S(2)}) collective-permute-start(bf16[576,512]{1,0:T(8,128)(2,1)} %get-tuple-element.208), channel_id=1, source_target_pairs={{0,6},{1,7},{2,4},{3,5},{4,2},{5,3},{6,0},{7,1},{8,14},{9,15},{10,... | collective-permute-start | bytes 1769480 | tf_op jit(solution)/shard_map/ppermute | solution.py:962
  166.3 25.6 %collective-permute-start.30 = (bf16[576,512]{1,0:T(8,128)(2,1)S(1)}, bf16[576,512]{1,0:T(8,128)(2,1)S(1)}, u32[]{:S(2)}, u32[]{:S(2)}) collective-permute-start(bf16[576,512]{1,0:T(8,128)(2,1)S(1)} %copy-done.32), channel_id=1, source_target_pairs={{0,2},{1,3},{2,0},{3,1},{4,6},{5,7},{6,4},{7,5},{8,10},{9,11},{10,... | collective-permute-start | bytes 1769480 | tf_op jit(solution)/shard_map/ppermute | solution.py:962
  167.7 24.2 %collective-permute-start.27 = (bf16[576,512]{1,0:T(8,128)(2,1)S(1)}, bf16[576,512]{1,0:T(8,128)(2,1)S(1)}, u32[]{:S(2)}, u32[]{:S(2)}) collective-permute-start(bf16[576,512]{1,0:T(8,128)(2,1)S(1)} %get-tuple-element.200), channel_id=1, source_target_pairs={{0,4},{1,5},{2,6},{3,7},{4,0},{5,1},{6,2},{7,3},{8,12},{9,13},{10,... | collective-permute-start | bytes 1769480 | tf_op jit(solution)/shard_map/ppermute | solution.py:962
  169.0 18.1 %collective-permute-start.46 = (bf16[21,8,512]{2,1,0:T(8,128)(2,1)S(1)}, bf16[21,8,512]{2,1,0:T(8,128)(2,1)S(1)}, u32[]{:S(2)}, u32[]{:S(2)}) collective-permute-start(bf16[21,8,512]{2,1,0:T(8,128)(2,1)S(1)} %get-tuple-element.228), channel_id=1, source_target_pairs={{0,8},{4,12},{8,0},{12,4},{16,24},{20,28},{24,16},{28,20},{1,9},{5... | collective-permute-start | bytes 516104 | tf_op jit(solution)/shard_map/ppermute | solution.py:949
  187.1 9.0 %collective-permute-start.16 = (bf16[112,512]{1,0:T(8,128)(2,1)S(1)}, bf16[112,512]{1,0:T(8,128)(2,1)S(1)}, u32[]{:S(2)}, u32[]{:S(2)}) collective-permute-start(bf16[112,512]{1,0:T(8,128)(2,1)S(1)} %get-tuple-element.189), channel_id=1, source_target_pairs={{0,1},{1,0},{2,3},{3,2},{4,5},{5,4},{6,7},{7,6},{8,9},{9,8},{10,11... | collective-permute-start | bytes 344072 | tf_op jit(solution)/shard_map/ppermute | solution.py:962
  187.2 9.6 %collective-permute-start.17 = (bf16[112,512]{1,0:T(8,128)(2,1)S(1)}, bf16[112,512]{1,0:T(8,128)(2,1)S(1)}, u32[]{:S(2)}, u32[]{:S(2)}) collective-permute-start(bf16[112,512]{1,0:T(8,128)(2,1)S(1)} %get-tuple-element.190), channel_id=1, source_target_pairs={{0,5},{1,4},{2,7},{3,6},{4,1},{5,0},{6,3},{7,2},{8,13},{9,12},{10,... | collective-permute-start | bytes 344072 | tf_op jit(solution)/shard_map/ppermute | solution.py:962
  188.0 9.5 %collective-permute-start.20 = (bf16[112,512]{1,0:T(8,128)(2,1)S(1)}, bf16[112,512]{1,0:T(8,128)(2,1)S(1)}, u32[]{:S(2)}, u32[]{:S(2)}) collective-permute-start(bf16[112,512]{1,0:T(8,128)(2,1)S(1)} %get-tuple-element.193), channel_id=1, source_target_pairs={{0,3},{1,2},{2,1},{3,0},{4,7},{5,6},{6,5},{7,4},{8,11},{9,10},{10,... | collective-permute-start | bytes 344072 | tf_op jit(solution)/shard_map/ppermute | solution.py:962
  193.1 21.1 %collective-permute-start.34 = (bf16[8,48,512]{2,1,0:T(8,128)(2,1)S(1)}, bf16[8,48,512]{2,1,0:T(8,128)(2,1)}, u32[]{:S(2)}, u32[]{:S(2)}) collective-permute-start(bf16[8,48,512]{2,1,0:T(8,128)(2,1)S(1)} %get-tuple-element.214), channel_id=1, source_target_pairs={{0,8},{4,12},{8,0},{12,4},{16,24},{20,28},{24,16},{28,20},{1,9},{5... | collective-permute-start | bytes 1179656 | tf_op jit(solution)/shard_map/ppermute | solution.py:949
  194.8 16.8 %collective-permute-start.21 = (bf16[112,512]{1,0:T(8,128)(2,1)}, bf16[112,512]{1,0:T(8,128)(2,1)S(1)}, u32[]{:S(2)}, u32[]{:S(2)}) collective-permute-start(bf16[112,512]{1,0:T(8,128)(2,1)} %get-tuple-element.194), channel_id=1, source_target_pairs={{0,7},{1,6},{2,5},{3,4},{4,3},{5,2},{6,1},{7,0},{8,15},{9,14},{10,... | collective-permute-start | bytes 344072 | tf_op jit(solution)/shard_map/ppermute | solution.py:962
  196.1 18.1 %collective-permute-start.15 = (bf16[304,512]{1,0:T(8,128)(2,1)S(1)}, bf16[304,512]{1,0:T(8,128)(2,1)S(1)}, u32[]{:S(2)}, u32[]{:S(2)}) collective-permute-start(bf16[304,512]{1,0:T(8,128)(2,1)S(1)} %get-tuple-element.188), channel_id=1, source_target_pairs={{0,4},{1,5},{2,6},{3,7},{4,0},{5,1},{6,2},{7,3},{8,12},{9,13},{10,... | collective-permute-start | bytes 933896 | tf_op jit(solution)/shard_map/ppermute | solution.py:962
  196.8 19.1 %collective-permute-start.18 = (bf16[304,512]{1,0:T(8,128)(2,1)S(1)}, bf16[304,512]{1,0:T(8,128)(2,1)S(1)}, u32[]{:S(2)}, u32[]{:S(2)}) collective-permute-start(bf16[304,512]{1,0:T(8,128)(2,1)S(1)} %get-tuple-element.191), channel_id=1, source_target_pairs={{0,2},{1,3},{2,0},{3,1},{4,6},{5,7},{6,4},{7,5},{8,10},{9,11},{10,... | collective-permute-start | bytes 933896 | tf_op jit(solution)/shard_map/ppermute | solution.py:962
  197.6 18.7 %collective-permute-start.19 = (bf16[304,512]{1,0:T(8,128)(2,1)S(1)}, bf16[304,512]{1,0:T(8,128)(2,1)S(1)}, u32[]{:S(2)}, u32[]{:S(2)}) collective-permute-start(bf16[304,512]{1,0:T(8,128)(2,1)S(1)} %get-tuple-element.192), channel_id=1, source_target_pairs={{0,6},{1,7},{2,4},{3,5},{4,2},{5,3},{6,0},{7,1},{8,14},{9,15},{10,... | collective-permute-start | bytes 933896 | tf_op jit(solution)/shard_map/ppermute | solution.py:962
  211.5 19.6 %copy-start.41 = (bf16[21,8,512]{2,1,0:T(8,128)(2,1)S(1)}, bf16[21,8,512]{2,1,0:T(8,128)(2,1)}, u32[]{:S(2)}) copy-start(bf16[21,8,512]{2,1,0:T(8,128)(2,1)} %add_convert_fusion.5) | copy-start | bytes 516100
  211.6 19.5 %collective-permute-start.47 = (bf16[21,8,512]{2,1,0:T(8,128)(2,1)}, bf16[21,8,512]{2,1,0:T(8,128)(2,1)S(1)}, u32[]{:S(2)}, u32[]{:S(2)}) collective-permute-start(bf16[21,8,512]{2,1,0:T(8,128)(2,1)} %add_convert_fusion.5), channel_id=1, source_target_pairs={{0,16},{4,20},{8,24},{12,28},{16,0},{20,4},{24,8},{28,12},{1,17},{... | collective-permute-start | bytes 516104 | tf_op jit(solution)/shard_map/ppermute | solution.py:949
  214.2 68.8 %collective-permute-start.13 = (bf16[1024,768]{1,0:T(8,128)(2,1)}, bf16[1024,768]{1,0:T(8,128)(2,1)}, u32[]{:S(2)}, u32[]{:S(2)}) collective-permute-start(bf16[1024,768]{1,0:T(8,128)(2,1)} %get-tuple-element.182), channel_id=1, source_target_pairs={{0,1},{1,0},{2,3},{3,2},{4,5},{5,4},{6,7},{7,6},{8,9},{9,8},{10,11... | collective-permute-start | bytes 4718600 | tf_op jit(solution)/shard_map/ppermute | solution.py:945
  214.2 68.8 %collective-permute-start.14 = (bf16[1024,768]{1,0:T(8,128)(2,1)}, bf16[1024,768]{1,0:T(8,128)(2,1)}, u32[]{:S(2)}, u32[]{:S(2)}) collective-permute-start(bf16[1024,768]{1,0:T(8,128)(2,1)} %get-tuple-element.183), channel_id=1, source_target_pairs={{0,1},{1,0},{2,3},{3,2},{4,5},{5,4},{6,7},{7,6},{8,9},{9,8},{10,11... | collective-permute-start | bytes 4718600 | tf_op jit(solution)/shard_map/ppermute | solution.py:945
  215.9 28.8 %collective-permute-start.35 = (bf16[8,48,512]{2,1,0:T(8,128)(2,1)S(1)}, bf16[8,48,512]{2,1,0:T(8,128)(2,1)S(1)}, u32[]{:S(2)}, u32[]{:S(2)}) collective-permute-start(bf16[8,48,512]{2,1,0:T(8,128)(2,1)S(1)} %add_convert_fusion.1), channel_id=1, source_target_pairs={{0,16},{4,20},{8,24},{12,28},{16,0},{20,4},{24,8},{28,12},{1,17},{... | collective-permute-start | bytes 1179656 | tf_op jit(solution)/shard_map/ppermute | solution.py:949
  217.2 14.9 %collective-permute-start.22 = (bf16[25,8,512]{2,1,0:T(8,128)(2,1)S(1)}, bf16[25,8,512]{2,1,0:T(8,128)(2,1)S(1)}, u32[]{:S(2)}, u32[]{:S(2)}) collective-permute-start(bf16[25,8,512]{2,1,0:T(8,128)(2,1)S(1)} %get-tuple-element.196), channel_id=1, source_target_pairs={{0,8},{4,12},{8,0},{12,4},{16,24},{20,28},{24,16},{28,20},{1,9},{5... | collective-permute-start | bytes 614408 | tf_op jit(solution)/shard_map/ppermute | solution.py:949
  231.2 12.2 %collective-permute-start.50 = (bf16[21,8,512]{2,1,0:T(8,128)(2,1)S(1)}, bf16[21,8,512]{2,1,0:T(8,128)(2,1)S(1)}, u32[]{:S(2)}, u32[]{:S(2)}) collective-permute-start(bf16[21,8,512]{2,1,0:T(8,128)(2,1)S(1)} %add_convert_fusion.4.refs_0_), channel_id=1, source_target_pairs={{0,12},{4,8},{8,4},{12,0},{16,28},{20,24},{24,20},{28,16},{1,13},{... | collective-permute-start | bytes 516104 | tf_op jit(solution)/shard_map/ppermute | solution.py:949
  232.1 14.7 %collective-permute-start.49 = (bf16[21,8,512]{2,1,0:T(8,128)(2,1)S(1)}, bf16[21,8,512]{2,1,0:T(8,128)(2,1)S(1)}, u32[]{:S(2)}, u32[]{:S(2)}) collective-permute-start(bf16[21,8,512]{2,1,0:T(8,128)(2,1)S(1)} %add_convert_fusion.4.refs_0_), channel_id=1, source_target_pairs={{0,8},{4,12},{8,0},{12,4},{16,24},{20,28},{24,16},{28,20},{1,9},{5... | collective-permute-start | bytes 516104 | tf_op jit(solution)/shard_map/ppermute | solution.py:949
  243.3 6.2 %collective-permute-start.48 = (bf16[21,8,512]{2,1,0:T(8,128)(2,1)S(1)}, bf16[21,8,512]{2,1,0:T(8,128)(2,1)S(1)}, u32[]{:S(2)}, u32[]{:S(2)}) collective-permute-start(bf16[21,8,512]{2,1,0:T(8,128)(2,1)S(1)} %add_convert_fusion.4.refs_0_), channel_id=1, source_target_pairs={{0,4},{4,0},{8,12},{12,8},{16,20},{20,16},{24,28},{28,24},{1,5},{5... | collective-permute-start | bytes 516104 | tf_op jit(solution)/shard_map/ppermute | solution.py:949
  244.7 12.0 %collective-permute-start.23 = (bf16[25,8,512]{2,1,0:T(8,128)(2,1)S(1)}, bf16[25,8,512]{2,1,0:T(8,128)(2,1)S(1)}, u32[]{:S(2)}, u32[]{:S(2)}) collective-permute-start(bf16[25,8,512]{2,1,0:T(8,128)(2,1)S(1)} %add_convert_fusion.3), channel_id=1, source_target_pairs={{0,16},{4,20},{8,24},{12,28},{16,0},{20,4},{24,8},{28,12},{1,17},{... | collective-permute-start | bytes 614408 | tf_op jit(solution)/shard_map/ppermute | solution.py:949
  246.8 17.2 %collective-permute-start.38 = (bf16[8,48,512]{2,1,0:T(8,128)(2,1)S(1)}, bf16[8,48,512]{2,1,0:T(8,128)(2,1)S(1)}, u32[]{:S(2)}, u32[]{:S(2)}) collective-permute-start(bf16[8,48,512]{2,1,0:T(8,128)(2,1)S(1)} %add_convert_fusion.refs_0_), channel_id=1, source_target_pairs={{0,12},{4,8},{8,4},{12,0},{16,28},{20,24},{24,20},{28,16},{1,13},{... | collective-permute-start | bytes 1179656 | tf_op jit(solution)/shard_map/ppermute | solution.py:949
  249.5 22.1 %collective-permute-start.37 = (bf16[8,48,512]{2,1,0:T(8,128)(2,1)S(1)}, bf16[8,48,512]{2,1,0:T(8,128)(2,1)S(1)}, u32[]{:S(2)}, u32[]{:S(2)}) collective-permute-start(bf16[8,48,512]{2,1,0:T(8,128)(2,1)S(1)} %add_convert_fusion.refs_0_), channel_id=1, source_target_pairs={{0,8},{4,12},{8,0},{12,4},{16,24},{20,28},{24,16},{28,20},{1,9},{5... | collective-permute-start | bytes 1179656 | tf_op jit(solution)/shard_map/ppermute | solution.py:949
  256.7 15.7 %collective-permute-start.36 = (bf16[8,48,512]{2,1,0:T(8,128)(2,1)S(1)}, bf16[8,48,512]{2,1,0:T(8,128)(2,1)S(1)}, u32[]{:S(2)}, u32[]{:S(2)}) collective-permute-start(bf16[8,48,512]{2,1,0:T(8,128)(2,1)S(1)} %add_convert_fusion.refs_0_), channel_id=1, source_target_pairs={{0,4},{4,0},{8,12},{12,8},{16,20},{20,16},{24,28},{28,24},{1,5},{5... | collective-permute-start | bytes 1179656 | tf_op jit(solution)/shard_map/ppermute | solution.py:949
  264.0 14.7 %collective-permute-start.26 = (bf16[25,8,512]{2,1,0:T(8,128)(2,1)S(1)}, bf16[25,8,512]{2,1,0:T(8,128)(2,1)S(1)}, u32[]{:S(2)}, u32[]{:S(2)}) collective-permute-start(bf16[25,8,512]{2,1,0:T(8,128)(2,1)S(1)} %add_convert_fusion.2.refs_0_), channel_id=1, source_target_pairs={{0,12},{4,8},{8,4},{12,0},{16,28},{20,24},{24,20},{28,16},{1,13},{... | collective-permute-start | bytes 614408 | tf_op jit(solution)/shard_map/ppermute | solution.py:949
  271.7 7.8 %collective-permute-start.25 = (bf16[25,8,512]{2,1,0:T(8,128)(2,1)S(1)}, bf16[25,8,512]{2,1,0:T(8,128)(2,1)S(1)}, u32[]{:S(2)}, u32[]{:S(2)}) collective-permute-start(bf16[25,8,512]{2,1,0:T(8,128)(2,1)S(1)} %add_convert_fusion.2.refs_0_), channel_id=1, source_target_pairs={{0,8},{4,12},{8,0},{12,4},{16,24},{20,28},{24,16},{28,20},{1,9},{5... | collective-permute-start | bytes 614408 | tf_op jit(solution)/shard_map/ppermute | solution.py:949
  272.4 7.9 %collective-permute-start.24 = (bf16[25,8,512]{2,1,0:T(8,128)(2,1)S(1)}, bf16[25,8,512]{2,1,0:T(8,128)(2,1)S(1)}, u32[]{:S(2)}, u32[]{:S(2)}) collective-permute-start(bf16[25,8,512]{2,1,0:T(8,128)(2,1)S(1)} %add_convert_fusion.2.refs_0_), channel_id=1, source_target_pairs={{0,4},{4,0},{8,12},{12,8},{16,20},{20,16},{24,28},{28,24},{1,5},{5... | collective-permute-start | bytes 614408 | tf_op jit(solution)/shard_map/ppermute | solution.py:949
  (34 other events, 99.0 us)
